TPU v7x, 32 devices: a whole 2x2x4 slice. The times are simulated.
32 devices in a mesh: lev: 4 (over y, x), wav: 8 (over z, core).
Axes of the slice: x: 2, y: 2, z: 4, core: 2. Of those that a mesh axis runs over, the one named last changes fastest.
Arguments:
- grid_field: bfloat16 [128, 640, 1280], P('lev', 'wav'), may hold values from -6 to 6
- legendre: bfloat16 [640, 640, 640], P('wav'), may hold values from -0.25 to 0.25
- wave_of_slot: int32 [640], replicated, may hold values from 0 to 639, each once
- lat_of_row: int32 [640], P('wav'), may hold values from 0 to 639, each once
- analysis: bfloat16 [128, 128], replicated, may hold values from -0.5 to 0.5
- synthesis: bfloat16 [128, 128], replicated, may hold values from -0.5 to 0.5
- mode_rates: float32 [128], replicated, may hold values from 0.05 to 5
- flux_weights: float32 [128], replicated, may hold values from -0.5 to 0.5
- remap_mats: bfloat16 [4, 64, 128, 128], P('lev', 'wav'), may hold values from -0.5 to 0.5
- pair_dest: int32 [4, 64, 1], P('lev'), may hold values from 0 to 7; in each aligned block of 8 rows (0 to 7, 8 to 15, ..., all dimensions but the last counted through in order) at most 2 rows name the same one
- pair_src: int32 [4, 64], P('lev'), may hold values from 0 to 799
- pair_dst: int32 [4, 64], P('lev'), may hold values from 0 to 47
- ocean_temp: float32 [8, 192, 1024], P(None, 'lev', 'wav'), may hold values from -6 to 6
- diffusivity: float32 [192, 1024], P('lev', 'wav'), may hold values from 0.05 to 0.24
- surface_heat: float32 [192, 1024], P('lev', 'wav'), may hold values from -4 to 4
- land_mask: int32 [192, 1024], P('lev', 'wav'), may hold values 0 or 1
Outputs:
- atm_out: bfloat16 [128, 640, 1280], P('lev', 'wav')
- ocean_out: float32 [8, 192, 1024], P(None, 'lev', 'wav')
- ocean_flux: float32 [192, 1024], P('lev', 'wav')
Inputs may be any that keep to these rules, and one draw needn't show every extreme that they name: `wave_of_slot`: each wavenumber names exactly one slot. `lat_of_row`: each latitude names exactly one row. `pair_dest`: within the pairs of one source owner (aligned blocks of 8 pairs of a level row) no destination column is named more than 2 times.
All inputs are finite; a program needn't handle non-finite values. No bound on the sum of `land_mask` on one device may be relied on, other than what follows from the above.
Results may differ from a plain program's by a relative error of at most 0.015.
Values may be sent and summed in bfloat16 or wider, within the bound.
No kernel may reach another device: no remote copies, remote signals or barrier semaphores. Data moves between devices by JAX's collectives and lax.ppermute only.
A program may use at most 192 MiB of HBM per device.

v0:
```python
import math

import jax
import jax.numpy as jnp
from jax import lax
from jax.sharding import PartitionSpec as P

SWEEPS = 4


def with_halo(value, sides, width):
    for axis, dim in sides:
        count, length = (lax.axis_size(axis), value.shape[dim])
        up = [(i, (i + 1) % count) for i in range(count - 1)]
        down = [(j, i) for i, j in up]
        last = lax.slice_in_dim(value, length - width, length, axis=dim)
        initial = lax.slice_in_dim(value, 0, width, axis=dim)
        before = lax.ppermute(last, axis, up)
        after = lax.ppermute(initial, axis, down)
        value = jnp.concatenate([before, value, after], axis=dim)
    return value


def column_table(wave_ids, halves, lon_count):
    longitude = jnp.arange(lon_count, dtype=jnp.int32)
    phases = longitude[:, None] * wave_ids[None, :] % lon_count
    angles = phases.astype(jnp.float32) * (2.0 * math.pi / lon_count)
    factor = math.sqrt(2.0 / lon_count)
    matrix = jnp.where(halves[None, :] == 0, factor * jnp.cos(angles), -factor * jnp.sin(angles))
    return matrix.astype(jnp.bfloat16)


def per_device(
    grid_field,
    legendre,
    wave_of_slot,
    lat_of_row,
    analysis,
    synthesis,
    mode_rates,
    flux_weights,
    remap_mats,
    pair_dest,
    pair_src,
    pair_dst,
    ocean_temp,
    diffusivity,
    surface_heat,
    land_mask,
):
    groups = lax.axis_size("lev")
    owners = lax.axis_size("wav")
    my_group = lax.axis_index("lev")
    my_owner = lax.axis_index("wav")
    lev_dev, lat_dev, lon_count = grid_field.shape
    wave_count = wave_of_slot.shape[0]
    level_count = lev_dev * groups
    col_count = 2 * wave_count
    per_group = col_count // groups
    per_dev = per_group // owners
    slots_owner = wave_count // owners
    positions = jnp.arange(col_count, dtype=jnp.int32)
    pos_owner = positions % per_group // per_dev
    pos_local = positions // per_group * per_dev + positions % per_dev
    sent_slot = pos_owner * slots_owner + pos_local // 2
    forward_table = column_table(wave_of_slot[sent_slot], pos_local % 2, lon_count)
    natural_table = column_table(jnp.repeat(wave_of_slot, 2), positions % 2, lon_count)
    rows_flat = grid_field.reshape(lev_dev * lat_dev, lon_count)
    fourier = lax.dot_general(
        forward_table, rows_flat, (((0,), (1,)), ((), ())), preferred_element_type=jnp.float32
    ).astype(jnp.bfloat16)
    arrived = lax.all_to_all(
        lax.all_to_all(fourier, "lev", split_axis=0, concat_axis=1, tiled=True),
        "wav",
        split_axis=0,
        concat_axis=1,
        tiled=True,
    )
    local_q = my_group * per_dev + jnp.arange(per_dev, dtype=jnp.int32)
    local_slot = local_q // 2
    my_waves = wave_of_slot[my_owner * slots_owner + local_slot]
    tables = jnp.take(legendre, local_slot, axis=0).reshape(per_dev, owners, lat_dev, wave_count)
    fields = arrived.reshape(per_dev, owners, level_count, lat_dev)
    spectra = jnp.einsum("cwxr,cwrn->cxn", fields, tables, preferred_element_type=jnp.float32)
    degree = jnp.arange(wave_count, dtype=jnp.int32)
    retained = degree[None, :] >= my_waves[:, None]
    spectra = jnp.where(retained[:, None, :], spectra, 0.0).astype(jnp.bfloat16)
    damp_base = (degree * (degree + 1)).astype(jnp.float32) / float(wave_count * wave_count)
    damping = 1.0 / (1.0 + mode_rates[:, None] * damp_base[None, :])
    modal_coef = jnp.einsum("ix,cxn->cin", analysis, spectra, preferred_element_type=jnp.float32)
    modal_coef = (modal_coef * damping[None]).astype(jnp.bfloat16)
    solved = jnp.einsum(
        "xi,cin->cxn", synthesis, modal_coef, preferred_element_type=jnp.float32
    ).astype(jnp.bfloat16)
    flux_coef = jnp.einsum("x,cxn->cn", flux_weights, solved.astype(jnp.float32)).astype(
        jnp.bfloat16
    )
    solved_view = solved.reshape(per_dev, groups, lev_dev, wave_count)
    grid_coef = jnp.einsum(
        "cgxn,cwrn->cgwxr", solved_view, tables, preferred_element_type=jnp.float32
    ).astype(jnp.bfloat16)
    grid_coef = grid_coef.reshape(per_dev, groups * owners * lev_dev * lat_dev)
    flux_lat = jnp.einsum(
        "cn,cwrn->cwr", flux_coef, tables, preferred_element_type=jnp.float32
    ).astype(jnp.bfloat16)
    flux_copies = jnp.broadcast_to(flux_lat[:, None], (per_dev, groups, owners, lat_dev)).reshape(
        per_dev, groups * owners * lat_dev
    )
    returned, flux_back = (
        lax.all_to_all(
            lax.all_to_all(grid_coef, "lev", split_axis=1, concat_axis=0, tiled=True),
            "wav",
            split_axis=1,
            concat_axis=0,
            tiled=True,
        ),
        lax.all_to_all(
            lax.all_to_all(flux_copies, "lev", split_axis=1, concat_axis=0, tiled=True),
            "wav",
            split_axis=1,
            concat_axis=0,
            tiled=True,
        ),
    )
    regridded = lax.dot_general(
        returned, natural_table, (((0,), (1,)), ((), ())), preferred_element_type=jnp.float32
    )
    flux_grid = lax.dot_general(
        flux_back, natural_table, (((0,), (1,)), ((), ())), preferred_element_type=jnp.float32
    ).astype(jnp.bfloat16)
    latitude = jnp.sin(
        math.pi * (lat_of_row.astype(jnp.float32) + 0.5) / (lat_dev * owners) - math.pi / 2
    )
    atm_out = (
        regridded.reshape(lev_dev, lat_dev, lon_count)
        * (1.0 + grid_field.astype(jnp.float32) * latitude[None, :, None])
    ).astype(jnp.bfloat16)
    ocean_levels = ocean_temp.shape[0]
    ocean_rows = diffusivity.shape[0]
    ocean_cols = diffusivity.shape[1]
    ocean_mask = land_mask.astype(jnp.float32)
    level_one = (jnp.arange(ocean_levels, dtype=jnp.int32) == 0).astype(jnp.float32)[:, None, None]
    ocean_now = ocean_temp * ocean_mask[None]
    stacked = jnp.concatenate(
        [ocean_now, ocean_mask[None], diffusivity[None], surface_heat[None]], axis=0
    )
    padded = with_halo(stacked.astype(jnp.bfloat16), (("lev", 1), ("wav", 2)), SWEEPS).astype(
        stacked.dtype
    )
    current = padded[:ocean_levels]
    for sweep_idx in range(SWEEPS):
        margin = sweep_idx + 1
        inside = current[:, 1:-1, 1:-1]
        laplace = (
            current[:, 2:, 1:-1]
            + current[:, :-2, 1:-1]
            + current[:, 1:-1, 2:]
            + current[:, 1:-1, :-2]
            - 4.0 * inside
        )
        mask_in = padded[ocean_levels, margin:-margin, margin:-margin]
        kappa_in = padded[ocean_levels + 1, margin:-margin, margin:-margin]
        heat_in = padded[ocean_levels + 2, margin:-margin, margin:-margin]
        current = mask_in[None] * (inside + kappa_in[None] * laplace + level_one * heat_in[None])
    ocean_now = current
    pieces = lon_count // ocean_cols
    segments = flux_grid.reshape(lat_dev * pieces, ocean_cols)
    pairs_dev = remap_mats.shape[1]
    pair_start = my_owner * pairs_dev
    my_src = lax.dynamic_slice_in_dim(pair_src[0], pair_start, pairs_dev)
    my_dest = lax.dynamic_slice_in_dim(pair_dest[0, :, 0], pair_start, pairs_dev)
    my_dst = lax.dynamic_slice_in_dim(pair_dst[0], pair_start, pairs_dev)
    chosen = jnp.take(segments, my_src, axis=0)
    products = jnp.einsum("pij,pj->pi", remap_mats[0], chosen, preferred_element_type=jnp.float32)
    targets = my_dest * ocean_rows + my_dst
    rows_idx = jnp.arange(lax.axis_size("wav") * ocean_rows, dtype=jnp.int32)
    picker = (rows_idx[:, None] == targets[None, :]).astype(jnp.float32)
    ocean_flux = lax.psum_scatter(
        jnp.dot(
            picker, products, precision=lax.Precision.HIGHEST, preferred_element_type=jnp.float32
        ),
        "wav",
        scatter_dimension=0,
        tiled=True,
    )
    return (atm_out, ocean_now, ocean_flux)


def solution(mesh):
    return jax.shard_map(
        per_device,
        mesh=mesh,
        in_specs=(
            P("lev", "wav", None),
            P("wav", None, None),
            P(),
            P("wav"),
            P(),
            P(),
            P(),
            P(),
            P("lev", "wav", None, None),
            P("lev", None, None),
            P("lev", None),
            P("lev", None),
            P(None, "lev", "wav"),
            P("lev", "wav"),
            P("lev", "wav"),
            P("lev", "wav"),
        ),
        out_specs=(P("lev", "wav", None), P(None, "lev", "wav"), P("lev", "wav")),
        check_vma=False,
    )
```

profile of v0, /device:TPU:0, one launch (start us, length us, event | category | flops | bytes accessed | tf_op | source)
XLA Modules:
  0.0 749.5 jit_solution(11497165225064703030)
XLA Ops:
  7.2 0.1 fusion.80
  7.3 6.6 gather_fusion.2
  13.9 27.5 %select_convert_fusion.11 = bf16[1280,1280]{1,0:T(8,128)(2,1)S(1)} fusion(s32[1280]{0:T(1024)S(1)} %gather_fusion.2, pred[1280]{0:T(1024)(128)(4,1)S(1)} %fusion.70), kind=kLoop, calls=%fused_computation.29.clone.clone.1 | loop fusion | flops 21299200 | bytes 3283200 | tf_op jit(solution)/shard_map/dot_general | solution.py:69
  41.4 11.1 %convolution_convert_fusion = bf16[1280,2560]{1,0:T(8,128)(2,1)S(1)} fusion(bf16[2560,1280]{1,0:T(8,128)(2,1)} %bitcast.167, bf16[1280,1280]{1,0:T(8,128)(2,1)S(1)} %select_convert_fusion.11), kind=kOutput, calls=%fused_computation.12 | convolution fusion | flops 8391884800 | bytes 16384000 | tf_op jit(solution)/shard_map/dot_general | solution.py:69
  52.5 78.6 %all_to_all.99 = bf16[4,320,2560]{2,1,0:T(8,128)(2,1)} all-to-all(bf16[4,320,2560]{2,1,0:T(8,128)(2,1)S(1)} %bitcast.161), channel_id=1, replica_groups=mesh['lev'=4,'wav'=8] {'lev'}, dimensions={0} | all-to-all | bytes 13107200 | tf_op jit(solution)/shard_map/all_to_all | solution.py:73
  131.1 10.7 %copy.25 = bf16[320,4,2560]{2,1,0:T(4,128)(2,1)} copy(bf16[320,4,2560]{2,0,1:T(8,128)(2,1)} %bitcast.158) | data formatting | bytes 13107200 | tf_op jit(solution)/shard_map/all_to_all | solution.py:73
  141.8 10.4 %all_to_all.77 = bf16[8,40,10240]{2,1,0:T(8,128)(2,1)} reshape(bf16[320,4,2560]{2,1,0:T(4,128)(2,1)} %copy.25) | data formatting | bytes 13107200 | tf_op jit(solution)/shard_map/all_to_all | solution.py:72
  152.2 5.8 all-to-all-start.1
  158.1 0.7 gather_fusion.1
  158.8 24.9 %gather_fusion = bf16[40,640,640]{2,1,0:T(8,128)(2,1)} fusion(bf16[80,640,640]{2,1,0:T(8,128)(2,1)} %param.17, s32[1024]{0:T(1024)S(1)} %pad_clamp_fusion.3), kind=kCustom, calls=%fused_computation | custom fusion | bytes 65536160 | tf_op jit(solution)/shard_map/jit(_take)/gather | solution.py:82
  183.8 0.1 iota_compare_fusion.2
  183.9 0.2 add_divide_fusion
  184.0 118.6 %all-to-all-done.1 = bf16[8,40,10240]{2,1,0:T(8,128)(2,1)} async-done(((bf16[8,40,10240]{2,1,0:T(8,128)(2,1)}), bf16[8,40,10240]{2,1,0:T(8,128)(2,1)}, u32[]{:S(2)}, u32[]{:S(2)}) %all-to-all-start.1) | async-done | bytes 6553632 | tf_op jit(solution)/shard_map/all_to_all | solution.py:72
  302.6 16.8 %reshape.491 = bf16[40,8,128,80]{3,2,0,1:T(8,128)(2,1)} reshape(bf16[40,8,10240]{2,0,1:T(8,128)(2,1)} %bitcast.8) | data formatting | bytes 13107200 | tf_op jit(solution)/shard_map/reshape | solution.py:83
  319.4 19.8 %fusion.2 = bf16[40,128,640]{1,2,0:T(8,128)(2,1)} fusion(f32[128,640]{0,1:T(8,128)S(1)} %add_divide_fusion, bf16[40,8,128,80]{3,2,0,1:T(8,128)(2,1)} %reshape.491, pred[40,640]{1,0:T(8,128)(4,1)S(1)} %iota_compare_fusion.2, bf16[128,128]{1,0:T(8,128)(2,1)S(1)} %copy-done.12, bf16[40,8,80,640]{3,2,1,0:T(8,128)(2,1)} %bitcast.154, ...), kind=kOutput, calls=%fused_computation.8 | convolution fusion | flops 5062656000 | bytes 46261288 | tf_op jit(solution)/shard_map/ix,cxn->cin/dot_general | solution.py:90
  339.2 4.7 convolution_convert_fusion.1
  344.0 2.8 copy-done.2
  346.7 1.0 fusion.14
  347.7 25.8 %fusion.57 = f32[40,1,8,80]{3,1,2,0:T(1,128)S(1)} fusion(bf16[40,640,1,1]{1,0,2,3:T(8,128)(2,1)S(1)} %bitcast.165, bf16[40,8,80,640]{3,2,1,0:T(8,128)(2,1)} %bitcast.155, pred[40]{0:T(512)(128)(4,1)S(1)} %compare_and_fusion.1), kind=kOutput, calls=%fused_computation.86 | convolution fusion | flops 49152000 | bytes 32921640 | tf_op jit(solution)/shard_map/cn,cwrn->cwr/dot_general | solution.py:103
  373.5 0.1 broadcast_in_dim.97
  373.7 0.7 broadcast_in_dim.98
  374.4 3.5 all-to-all-start.4
  377.9 25.2 %convert_bitcast_fusion = bf16[40,4,8,32,80]{4,3,1,2,0:T(8,128)(2,1)} fusion(bf16[40,4,32,640,1]{3,2,1,4,0:T(8,128)(2,1)} %bitcast.157, bf16[40,8,80,640]{3,2,1,0:T(8,128)(2,1)} %bitcast.156, pred[40]{0:T(512)(128)(4,1)S(1)} %compare_and_fusion.1), kind=kOutput, calls=%fused_computation.15 | convolution fusion | flops 4213964800 | bytes 45875240 | tf_op jit(solution)/shard_map/cgxn,cwrn->cgwxr/dot_general | solution.py:99
  403.2 11.3 %copy.30 = bf16[40,4,8,32,80]{4,3,2,0,1:T(8,128)(2,1)} copy(bf16[40,4,8,32,80]{4,3,1,2,0:T(8,128)(2,1)} %convert_bitcast_fusion) | data formatting | bytes 13107200 | tf_op jit(solution)/shard_map/convert_element_type | solution.py:101
  414.5 22.5 %all_to_all.80 = bf16[40,4,20480]{2,0,1:T(8,128)(2,1)} reshape(bf16[40,4,8,32,80]{4,3,2,0,1:T(8,128)(2,1)} %copy.30) | data formatting | bytes 13107200 | tf_op jit(solution)/shard_map/all_to_all | solution.py:111
  437.0 5.3 all-to-all-start.2
  442.3 0.3 all_to_all.89
  442.7 0.8 copy.33
  443.5 71.6 %all-to-all-done.2 = bf16[40,4,20480]{2,0,1:T(8,128)(2,1)} async-done(((bf16[40,4,20480]{2,0,1:T(8,128)(2,1)}), bf16[40,4,20480]{2,0,1:T(8,128)(2,1)}, u32[]{:S(2)}, u32[]{:S(2)}) %all-to-all-start.2) | async-done | bytes 6553632 | tf_op jit(solution)/shard_map/all_to_all | solution.py:111
  515.0 3.6 all-to-all-start.5
  518.7 5.4 copy.50
  524.0 4.8 copy.31
  528.9 0.8 all-to-all-done.5
  529.7 4.8 all-to-all-start.3
  534.7 3.3 collective-permute-start
  538.0 1.3 collective-permute-start.1
  539.3 0.1 broadcast_in_dim.92
  539.4 0.2 mul.340
  539.7 0.1 fusion.93
  539.8 28.7 %fusion.127 = bf16[1280,1280,1]{1,0,2:T(8,128)(2,1)} fusion(s32[1280]{0:T(1024)S(1)} %mul.340, pred[1280]{0:T(1024)(128)(4,1)S(1)} %fusion.71), kind=kLoop, calls=%fused_computation.35.clone.1 | loop fusion | flops 21299200 | bytes 3283200 | tf_op jit(solution)/shard_map/dot_general | solution.py:125
  568.6 0.1 compare_and_fusion
  568.7 0.1 fusion.110
  568.8 2.0 collective-permute-start.2
  570.8 1.3 collective-permute-start.3
  572.2 0.1 fusion.95
  572.2 3.3 collective-permute-done.3
  575.5 0.3 maximum_convert_fusion
  575.8 0.1 slice_bitcast_fusion.11
  575.9 0.1 slice_bitcast_fusion.6
  576.0 0.1 slice_bitcast_fusion.7
  576.1 0.1 slice_bitcast_fusion.8
  576.3 0.6 fusion.48
  576.8 0.6 fusion.43
  577.4 0.6 fusion.38
  578.0 1.0 fusion.55
  579.0 28.2 %fusion.33 = bf16[80,1280]{1,0:T(8,128)(2,1)S(1)} fusion(bf16[1280,80]{1,0:T(8,128)(2,1)S(1)} %bitcast.163, s32[1280]{0:T(1024)S(1)} %mul.340, pred[1280]{0:T(1024)(128)(4,1)S(1)} %fusion.71), kind=kOutput, calls=%fused_computation.44 | convolution fusion | flops 283545600 | bytes 416000 | tf_op jit(solution)/shard_map/dot_general | solution.py:128
  607.2 0.3 reshape.446
  607.5 0.6 gather_fusion.3
  608.1 0.2 fusion.49
  608.3 0.9 fusion.56
  609.3 69.7 %all-to-all-done.3 = bf16[160,8,2560]{2,0,1:T(8,128)(2,1)} async-done(((bf16[160,8,2560]{2,0,1:T(8,128)(2,1)}), bf16[160,8,2560]{2,0,1:T(8,128)(2,1)}, u32[]{:S(2)}, u32[]{:S(2)}) %all-to-all-start.3) | async-done | bytes 6553632 | tf_op jit(solution)/shard_map/all_to_all | solution.py:110
  679.0 9.5 %copy.32 = bf16[2560,1280]{1,0:T(8,128)(2,1)} copy(bf16[2560,1280]{0,1:T(8,128)(2,1)} %bitcast.22) | data formatting | bytes 13107200 | tf_op jit(solution)/shard_map/dot_general | solution.py:125
  688.6 14.7 %multiply_convert_fusion = bf16[32,80,1280]{2,1,0:T(8,128)(2,1)} fusion(bf16[32,80,1280]{2,1,0:T(8,128)(2,1)} %param.16, bf16[32,80,1280]{2,1,0:T(8,128)(2,1)} %bitcast.160, f32[80]{0:T(128)S(1)} %add_sine_fusion, bf16[1280,1280,1]{1,0,2:T(8,128)(2,1)} %fusion.127), kind=kOutput, calls=%fused_computation.11 | convolution fusion | flops 8404992000 | bytes 22937920 | tf_op jit(solution)/shard_map/dot_general | solution.py:125
  703.2 39.0 %reduce-scatter.2.cloned.1.call-done = f32[48,128]{1,0:T(8,128)} async-done(((f32[384,128]{1,0:T(8,128)}), f32[48,128]{1,0:T(8,128)}) %reduce-scatter.2.cloned.1.call-update) | async-done | bytes 24592 | tf_op jit(solution)/shard_map/reduce_scatter | solution.py:178
  (54 shorter events, 0.5 us)
Async XLA Ops:
  7.2 601.0 %copy-start = (bf16[1,8,128,128]{3,2,1,0:T(8,128)(2,1)S(1)}, bf16[1,8,128,128]{3,2,1,0:T(8,128)(2,1)}, u32[]{:S(2)}) copy-start(bf16[1,8,128,128]{3,2,1,0:T(8,128)(2,1)} %param.24) | copy-start | bytes 786436
  152.2 5.8 copy-start.1
  152.2 150.4 %all-to-all-start.1 = ((bf16[8,40,10240]{2,1,0:T(8,128)(2,1)}), bf16[8,40,10240]{2,1,0:T(8,128)(2,1)}, u32[]{:S(2)}, u32[]{:S(2)}) async-start(bf16[8,40,10240]{2,1,0:T(8,128)(2,1)} %all_to_all.77), calls=%async_computation.1 | async-start | bytes 13107200 | tf_op jit(solution)/shard_map/all_to_all | solution.py:72
  158.8 25.0 %copy-start.8 = (f32[128]{0:T(128)S(1)}, f32[128]{0:T(128)}, u32[]{:S(2)}) copy-start(f32[128]{0:T(128)} %param.22) | copy-start | bytes 1540
  302.6 16.8 %copy-start.12 = (bf16[128,128]{1,0:T(8,128)(2,1)S(1)}, bf16[128,128]{1,0:T(8,128)(2,1)}, u32[]{:S(2)}) copy-start(bf16[128,128]{1,0:T(8,128)(2,1)} %param.20) | copy-start | bytes 98308
  319.4 19.8 %copy-start.4 = (bf16[128,128]{1,0:T(8,128)(2,1)S(1)}, bf16[128,128]{1,0:T(8,128)(2,1)}, u32[]{:S(2)}) copy-start(bf16[128,128]{1,0:T(8,128)(2,1)} %param.21) | copy-start | bytes 98308
  339.2 7.5 %copy-start.9 = (f32[128]{0:T(128)S(1)}, f32[128]{0:T(128)}, u32[]{:S(2)}) copy-start(f32[128]{0:T(128)} %param.23) | copy-start | bytes 1540
  343.9 2.8 copy-start.2
  374.4 62.6 %all-to-all-start.4 = ((bf16[40,4,640]{2,0,1:T(8,128)(2,1)}), bf16[40,4,640]{2,0,1:T(8,128)(2,1)S(1)}, u32[]{:S(2)}, u32[]{:S(2)}) async-start(bf16[40,4,640]{2,0,1:T(8,128)(2,1)} %broadcast_in_dim.98), calls=%async_computation.4 | async-start | bytes 409600 | tf_op jit(solution)/shard_map/all_to_all | solution.py:118
  437.0 78.0 %all-to-all-start.2 = ((bf16[40,4,20480]{2,0,1:T(8,128)(2,1)}), bf16[40,4,20480]{2,0,1:T(8,128)(2,1)}, u32[]{:S(2)}, u32[]{:S(2)}) async-start(bf16[40,4,20480]{2,0,1:T(8,128)(2,1)} %all_to_all.80), calls=%async_computation.2 | async-start | bytes 13107200 | tf_op jit(solution)/shard_map/all_to_all | solution.py:111
  515.0 14.7 %all-to-all-start.5 = ((bf16[160,8,80]{2,0,1:T(8,128)(2,1)}), bf16[160,8,80]{2,0,1:T(8,128)(2,1)S(1)}, u32[]{:S(2)}, u32[]{:S(2)}) async-start(bf16[160,8,80]{2,0,1:T(8,128)(2,1)} %copy.33), calls=%async_computation.5 | async-start | bytes 655360 | tf_op jit(solution)/shard_map/all_to_all | solution.py:117
  528.8 5.7 copy-start.5
  528.8 5.7 copy-start.6
  528.8 5.7 copy-start.7
  528.8 5.8 copy-start.3
  528.8 10.8 %copy-start.14 = (s32[1,64]{1,0:T(1,128)S(1)}, s32[1,64]{1,0:T(1,128)}, u32[]{:S(2)}) copy-start(s32[1,64]{1,0:T(1,128)} %param.26) | copy-start | bytes 772
  528.9 10.9 %copy-start.13 = (s32[80]{0:T(128)S(1)}, s32[80]{0:T(128)}, u32[]{:S(2)}) copy-start(s32[80]{0:T(128)} %param.19) | copy-start | bytes 964
  529.7 149.3 %all-to-all-start.3 = ((bf16[160,8,2560]{2,0,1:T(8,128)(2,1)}), bf16[160,8,2560]{2,0,1:T(8,128)(2,1)}, u32[]{:S(2)}, u32[]{:S(2)}) async-start(bf16[160,8,2560]{2,0,1:T(8,128)(2,1)} %copy.31), calls=%async_computation.3 | async-start | bytes 13107200 | tf_op jit(solution)/shard_map/all_to_all | solution.py:110
  534.5 37.7 %copy-start.10 = (s32[1,64]{1,0:T(1,128)S(1)}, s32[1,64]{1,0:T(1,128)}, u32[]{:S(2)}) copy-start(s32[1,64]{1,0:T(1,128)} %param.27) | copy-start | bytes 772
  534.5 37.7 %copy-start.11 = (s32[1,64,1]{1,2,0:T(1,128)S(1)}, s32[1,64,1]{1,2,0:T(1,128)}, u32[]{:S(2)}) copy-start(s32[1,64,1]{1,2,0:T(1,128)} %param.25) | copy-start | bytes 772
  534.5 207.8 %reduce-scatter.2.cloned.1.call-start = ((), (), s32[]{:S(2)}) async-start(), calls=%async_computation.7 | async-start | bytes 221184 | tf_op jit(solution)/shard_map/reduce_scatter | solution.py:178
  534.7 34.0 %collective-permute-start = (bf16[11,4,128]{2,1,0:T(4,128)(2,1)S(1)}, bf16[11,4,128]{2,1,0:T(4,128)(2,1)S(1)}, u32[]{:S(2)}, u32[]{:S(2)}) collective-permute-start(bf16[11,4,128]{2,1,0:T(4,128)(2,1)S(1)} %get-tuple-element.17), channel_id=1, source_target_pairs={{0,8},{8,16},{16,24},{1,9},{9,17},{17,25},{2,10},{10,18},{18,26},{... | collective-permute-start | bytes 33800 | tf_op jit(solution)/shard_map/ppermute | solution.py:18
  538.0 30.7 %collective-permute-start.1 = (bf16[11,4,128]{2,1,0:T(4,128)(2,1)S(1)}, bf16[11,4,128]{2,1,0:T(4,128)(2,1)S(1)}, u32[]{:S(2)}, u32[]{:S(2)}) collective-permute-start(bf16[11,4,128]{2,1,0:T(4,128)(2,1)S(1)} %get-tuple-element.18), channel_id=1, source_target_pairs={{8,0},{16,8},{24,16},{9,1},{17,9},{25,17},{10,2},{18,10},{26,18},{... | collective-permute-start | bytes 33800 | tf_op jit(solution)/shard_map/ppermute | solution.py:19
  568.8 3.4 collective-permute-start.2
  570.8 4.7 collective-permute-start.3
Sparse Core Ops, SparseCore 0:
  609.4 132.7 reduce-scatter.1
where the time goes:
time: 757 us; the launch traced here: 750 us
  waiting for transfers between devices  303 us (40%)
  matrix products  132 us (17%)
  local copies, waits for them, and re-layouts  130 us (17%)
  blocking collectives  78.6 us (10%)
  other arithmetic  60.1 us (8%)
  starting transfers between devices  31 us (4%)
  between operations  15 us (2%)
    all_to_all x1, waiting for transfers between devices, per_device(): lax.all_to_all(lax.all_to_all(fourier, 'lev', split_axis=0, concat_axis=1...  119 us
    all_to_all x1, blocking collectives, per_device(): lax.all_to_all(fourier, 'lev', split_axis=0, concat_axis=1, tiled=True)  78.6 us
    all_to_all x1, waiting for transfers between devices, per_device(): lax.all_to_all(grid_coef, 'lev', split_axis=1, concat_axis=0, tiled=True)  71.6 us
    all_to_all x1, waiting for transfers between devices, per_device(): lax.all_to_all(lax.all_to_all(grid_coef, 'lev', split_axis=1, concat_axis...  69.7 us
    reduce_scatter x1, waiting for transfers between devices, per_device(): lax.psum_scatter(jnp.dot(picker, products, precision=lax.Precision.HIGHES...  39 us
    dot_general x1, other arithmetic, per_device(): lax.dot_general(returned, natural_table, (((0,), (1,)), ((), ())), prefer...  28.7 us
    dot_general x1, matrix products, per_device(): lax.dot_general(flux_back, natural_table, (((0,), (1,)), ((), ())), prefe...  28.2 us
    dot_general x1, other arithmetic, per_device(): lax.dot_general(forward_table, rows_flat, (((0,), (1,)), ((), ())), prefe...  27.5 us
  transfers between devices with their start and end apart: 10, of which 6 were waited for; matrix products, arithmetic and copies ran while one was open for 21% of the time, Pallas kernels for 0%

commit v1 on v0

v1 whole, which is shorter than its diff:
```python
import math

import jax
import jax.numpy as jnp
from jax import lax
from jax.sharding import PartitionSpec as P


SWEEPS = 4
CAP = 2
AXES = ("lev", "wav")
CHUNKS = (1, 2, 2)


def with_halo(value, sides, width):
    for axis, dim in sides:
        count, length = (lax.axis_size(axis), value.shape[dim])
        up = [(i, (i + 1) % count) for i in range(count - 1)]
        down = [(j, i) for i, j in up]
        last = lax.slice_in_dim(value, length - width, length, axis=dim)
        initial = lax.slice_in_dim(value, 0, width, axis=dim)
        before = lax.ppermute(last, axis, up)
        after = lax.ppermute(initial, axis, down)
        value = jnp.concatenate([before, value, after], axis=dim)
    return value


def exchange(value):
    return lax.all_to_all(value, AXES, split_axis=0, concat_axis=0, tiled=True)


def wave_table(waves, valid, lon_count):
    shape = waves.shape[:-1] + (2, waves.shape[-1])
    quarter = jnp.arange(2, dtype=jnp.int32) * (lon_count // 4)
    quarter = jnp.broadcast_to(quarter[:, None], shape).reshape(-1)
    waves = jnp.broadcast_to(waves[..., None, :], shape).reshape(-1)
    scale = jnp.where(valid, math.sqrt(2.0 / lon_count), 0.0)
    scale = jnp.broadcast_to(scale[..., None, :], shape).reshape(-1)
    longitude = jnp.arange(lon_count, dtype=jnp.int32)
    steps = (waves[:, None] * longitude[None, :] + quarter[:, None]).astype(jnp.float32)
    steps = steps - lon_count * jnp.round(steps * (1.0 / lon_count))
    return (scale[:, None] * jnp.cos(steps * (2.0 * math.pi / lon_count))).astype(jnp.bfloat16)


def return_order(steps):
    return list(range(1, steps)) + [0]


def split_slots(count):
    total = sum(CHUNKS)
    if count % total:
        return [(0, count)]
    unit, start, out = count // total, 0, []
    for part in CHUNKS:
        out.append((start, part * unit))
        start += part * unit
    return out


def ocean(ocean_temp, diffusivity, surface_heat, land_mask):
    ocean_levels = ocean_temp.shape[0]
    ocean_mask = land_mask.astype(jnp.float32)
    level_one = (jnp.arange(ocean_levels, dtype=jnp.int32) == 0).astype(jnp.float32)[:, None, None]
    ocean_now = ocean_temp * ocean_mask[None]
    stacked = jnp.concatenate(
        [ocean_now, ocean_mask[None], diffusivity[None], surface_heat[None]], axis=0
    )
    padded = with_halo(stacked.astype(jnp.bfloat16), (("lev", 1), ("wav", 2)), SWEEPS).astype(
        stacked.dtype
    )
    current = padded[:ocean_levels]
    for sweep_idx in range(SWEEPS):
        margin = sweep_idx + 1
        inside = current[:, 1:-1, 1:-1]
        laplace = (
            current[:, 2:, 1:-1]
            + current[:, :-2, 1:-1]
            + current[:, 1:-1, 2:]
            + current[:, 1:-1, :-2]
            - 4.0 * inside
        )
        mask_in = padded[ocean_levels, margin:-margin, margin:-margin]
        kappa_in = padded[ocean_levels + 1, margin:-margin, margin:-margin]
        heat_in = padded[ocean_levels + 2, margin:-margin, margin:-margin]
        current = mask_in[None] * (inside + kappa_in[None] * laplace + level_one * heat_in[None])
    return current


def per_device(
    grid_field,
    legendre,
    wave_of_slot,
    lat_of_row,
    analysis,
    synthesis,
    mode_rates,
    flux_weights,
    remap_mats,
    pair_dest,
    pair_src,
    pair_dst,
    ocean_temp,
    diffusivity,
    surface_heat,
    land_mask,
):
    groups = lax.axis_size("lev")
    owners = lax.axis_size("wav")
    devices = groups * owners
    my_group = lax.axis_index("lev")
    my_owner = lax.axis_index("wav")
    lev_dev, lat_dev, lon_count = grid_field.shape
    wave_count = wave_of_slot.shape[0]
    slots_owner = wave_count // owners
    slots_dev = -(-slots_owner // groups)
    cells = lev_dev * lat_dev
    rows_flat = grid_field.reshape(cells, lon_count)
    degree = jnp.arange(wave_count, dtype=jnp.int32)
    damp_base = (degree * (degree + 1)).astype(jnp.float32) / float(wave_count * wave_count)
    damping = 1.0 / (1.0 + mode_rates[:, None] * damp_base[None, :])

    def slots_of(group, owner, start, count):
        local = group * slots_dev + start + jnp.arange(count, dtype=jnp.int32)
        slot = owner * slots_owner + jnp.minimum(local, slots_owner - 1)
        return local, wave_of_slot[slot], local < slots_owner

    chunks = split_slots(slots_dev)
    spare = groups * slots_dev - slots_owner
    all_waves = jnp.pad(wave_of_slot.reshape(owners, slots_owner), ((0, 0), (0, spare)))
    all_waves = all_waves.reshape(owners, groups, slots_dev).transpose(1, 0, 2)
    all_valid = jnp.arange(groups * slots_dev, dtype=jnp.int32) < slots_owner
    all_valid = all_valid.reshape(groups, 1, slots_dev)

    def forward(start, count):
        waves = all_waves[:, :, start : start + count]
        valid = jnp.broadcast_to(all_valid[:, :, start : start + count], waves.shape)
        table = lax.optimization_barrier(wave_table(waves, valid, lon_count))
        fourier = lax.dot_general(
            table, rows_flat, (((1,), (1,)), ((), ())), preferred_element_type=jnp.float32
        ).astype(jnp.bfloat16)
        return table, fourier.reshape(devices, 2 * count, cells)

    def spectral(arrived, start, count):
        arrived, my_analysis, my_synthesis, my_damping, my_weights = lax.optimization_barrier(
            (arrived, analysis, synthesis, damping, flux_weights)
        )
        local, my_waves, _ = slots_of(my_group, my_owner, start, count)
        if slots_owner == slots_dev * groups:
            leg = lax.dynamic_slice_in_dim(legendre, my_group * slots_dev + start, count, axis=0)
        else:
            leg = jnp.take(legendre, jnp.minimum(local, slots_owner - 1), axis=0)
        fields = arrived.reshape(groups, owners, 2, count, lev_dev, lat_dev)
        fields = fields.transpose(3, 1, 2, 0, 4, 5).reshape(
            count, owners, 2 * groups * lev_dev, lat_dev
        )
        leg_rows = leg.reshape(count, owners, lat_dev, wave_count)
        spectra = jnp.einsum(
            "swmr,swrn->smn", fields, leg_rows, preferred_element_type=jnp.float32
        ).reshape(count, 2, groups * lev_dev, wave_count)
        retained = degree[None, :] >= my_waves[:, None]
        spectra = jnp.where(retained[:, None, None, :], spectra, 0.0).astype(jnp.bfloat16)
        modal_coef = jnp.einsum(
            "ix,skxn->skin", my_analysis, spectra, preferred_element_type=jnp.float32
        )
        modal_coef = (modal_coef * my_damping[None, None]).astype(jnp.bfloat16)
        solved = jnp.einsum(
            "xi,skin->skxn", my_synthesis, modal_coef, preferred_element_type=jnp.float32
        ).astype(jnp.bfloat16)
        flux_coef = jnp.sum(
            my_weights[None, None, :, None] * solved.astype(jnp.float32), axis=2
        ).astype(jnp.bfloat16)
        grid_coef = jnp.einsum(
            "smn,swrn->swmr",
            solved.reshape(count, 2 * groups * lev_dev, wave_count),
            leg_rows,
            preferred_element_type=jnp.float32,
        ).astype(jnp.bfloat16)
        grid_coef = grid_coef.reshape(count, owners, 2, groups, lev_dev, lat_dev)
        grid_coef = grid_coef.transpose(3, 1, 2, 0, 4, 5).reshape(devices, 2 * count, cells)
        flux_lat = lax.dot_general(
            flux_coef, leg, (((2,), (2,)), ((0,), (0,))), preferred_element_type=jnp.float32
        ).astype(jnp.bfloat16)
        flux_lat = flux_lat.reshape(count, 2, owners, lat_dev).transpose(1, 0, 2, 3)
        return grid_coef, flux_lat.reshape(2 * count, owners, lat_dev)

    tables, arrivals, returned, sent, flux_parts = [], [], [], [], []
    for chunk in chunks:
        table, fourier = forward(*chunk)
        tables.append(table)
        arrivals.append(exchange(fourier))
    for index, chunk in enumerate(chunks):
        grid_coef, flux_lat = spectral(arrivals[index], *chunk)
        sent.append(grid_coef)
        flux_parts.append(flux_lat)
    for value in sent:
        returned.append(exchange(value))
    flux_lat = jnp.concatenate(flux_parts, axis=0).transpose(1, 0, 2)
    flux_copies = jnp.broadcast_to(flux_lat[None], (groups,) + flux_lat.shape)
    flux_back = exchange(flux_copies.reshape(devices, 2 * slots_dev, lat_dev))

    flux_grid = 0.0
    for (start, count), table in zip(chunks, tables):
        part = flux_back[:, 2 * start : 2 * (start + count)].reshape(-1, lat_dev)
        flux_grid += lax.dot_general(
            part, table, (((0,), (0,)), ((), ())), preferred_element_type=jnp.float32
        )
    flux_grid = flux_grid.astype(jnp.bfloat16)

    latitude = jnp.sin(
        math.pi * (lat_of_row.astype(jnp.float32) + 0.5) / (lat_dev * owners) - math.pi / 2
    )
    latitude = jnp.broadcast_to(latitude[None], (lev_dev, lat_dev)).reshape(cells, 1)
    regridded = 0.0
    for index in return_order(len(chunks)):
        regridded += lax.dot_general(
            returned[index].reshape(-1, cells),
            tables[index],
            (((0,), (0,)), ((), ())),
            preferred_element_type=jnp.float32,
        )
    atm_out = regridded * (1.0 + rows_flat.astype(jnp.float32) * latitude)
    atm_out = atm_out.astype(jnp.bfloat16).reshape(lev_dev, lat_dev, lon_count)

    ocean_now = ocean(ocean_temp, diffusivity, surface_heat, land_mask)

    ocean_rows, ocean_cols = diffusivity.shape
    pieces = lon_count // ocean_cols
    segments = flux_grid.reshape(lat_dev * pieces, ocean_cols)
    pairs_dev = remap_mats.shape[1]
    all_dest = pair_dest[0, :, 0].reshape(owners, pairs_dev)
    all_dst = pair_dst[0].reshape(owners, pairs_dev)
    earlier = jnp.arange(pairs_dev)[None, :] < jnp.arange(pairs_dev)[:, None]
    rank = jnp.sum(
        (all_dest[:, :, None] == all_dest[:, None, :]) & earlier[None], axis=2, dtype=jnp.int32
    )
    my_src = lax.dynamic_slice_in_dim(pair_src[0], my_owner * pairs_dev, pairs_dev)
    chosen = jnp.take(segments, my_src, axis=0)
    products = jnp.einsum("pij,pj->pi", remap_mats[0], chosen, preferred_element_type=jnp.float32)
    place = lax.dynamic_index_in_dim(all_dest * CAP + rank, my_owner, 0, keepdims=False)
    outgoing = jnp.dot(
        (jnp.arange(owners * CAP, dtype=jnp.int32)[:, None] == place[None, :]).astype(jnp.float32),
        products,
        precision=lax.Precision.HIGHEST,
        preferred_element_type=jnp.float32,
    )
    outgoing = outgoing.reshape(owners, CAP, ocean_cols)
    incoming = lax.all_to_all(outgoing, "wav", split_axis=0, concat_axis=0, tiled=True)
    mine = (all_dest == my_owner)[:, None, :] & (
        rank[:, None, :] == jnp.arange(CAP, dtype=jnp.int32)[None, :, None]
    )
    row_hit = all_dst[None, :, None, :] == jnp.arange(ocean_rows, dtype=jnp.int32)[:, None, None, None]
    picker = jnp.any(mine[None] & row_hit, axis=3).astype(jnp.float32)
    ocean_flux = jnp.dot(
        picker.reshape(ocean_rows, owners * CAP),
        incoming.reshape(owners * CAP, ocean_cols),
        precision=lax.Precision.HIGHEST,
        preferred_element_type=jnp.float32,
    )
    return (atm_out, ocean_now, ocean_flux)


def solution(mesh):
    return jax.shard_map(
        per_device,
        mesh=mesh,
        in_specs=(
            P("lev", "wav", None),
            P("wav", None, None),
            P(),
            P("wav"),
            P(),
            P(),
            P(),
            P(),
            P("lev", "wav", None, None),
            P("lev", None, None),
            P("lev", None),
            P("lev", None),
            P(None, "lev", "wav"),
            P("lev", "wav"),
            P("lev", "wav"),
            P("lev", "wav"),
        ),
        out_specs=(P("lev", "wav", None), P(None, "lev", "wav"), P("lev", "wav")),
        check_vma=False,
    )
```

time: 757 us -> 492 us (0.65)
  waiting for transfers between devices: 303 us -> 162 us
  blocking collectives: 78.6 us -> 0 us
  matrix products: 132 us -> 106 us
  starting transfers between devices: 31 us -> 56.8 us
  other arithmetic: 60.1 us -> 34.5 us
  between operations: 15 us -> 1.64 us
  local copies, waits for them, and re-layouts: 130 us -> 122 us
    all_to_all x5 -> x8, waiting for transfers between devices: 261 us -> 149 us  [the longest x7 149 us: exchange(): return lax.all_to_all(value, AXES, split_axis=0, concat_axis=0, tiled=True)]
    all_to_all x1 -> x0, blocking collectives: 78.6 us -> none  [per_device(): lax.all_to_all(fourier, 'lev', split_axis=0, concat_axis=1, tiled=True)]
    dot_general x2 -> x0, other arithmetic: 56.2 us -> none  [the longest x1 28.7 us: per_device(): lax.dot_general(returned, natural_table, (((0,), (1,)), ((), ())), prefer...]
    all_to_all x6 -> x0, local copies, waits for them, and re-layouts: 49.5 us -> none  [the longest x1 22.5 us: per_device(): lax.all_to_all(grid_coef, 'lev', split_axis=1, concat_axis=0, tiled=True)]
    reduce_scatter x1 -> x0, waiting for transfers between devices: 39 us -> none  [per_device(): lax.psum_scatter(jnp.dot(picker, products, precision=lax.Precision.HIGHES...]
    reshape x1 -> x16, local copies, waits for them, and re-layouts: 16.8 us -> 55 us  [the longest x3 22.3 us: spectral(): grid_coef.transpose(3, 1, 2, 0, 4, 5).reshape(devices, 2 * count, cells)]
    gather x3, local copies, waits for them, and re-layouts: 32.2 us -> 2.4 us  [slots_of(): return (local, wave_of_slot[slot], local < slots_owner)]
    transpose x0 -> x7, local copies, waits for them, and re-layouts: none -> 27.8 us  [the longest x3 14.5 us: spectral(): grid_coef.transpose(3, 1, 2, 0, 4, 5).reshape(devices, 2 * count, cells)]
  transfers between devices with their start and end apart: 10 -> 12, of which waited for: 6 -> 10; matrix products, arithmetic and copies ran while one was open for 21% -> 37% of each run, Pallas kernels for 0% -> 0%
where the time goes in v1:
time: 492 us; the launch traced here: 483 us
  waiting for transfers between devices  162 us (33%)
  local copies, waits for them, and re-layouts  122 us (25%)
  matrix products  106 us (22%)
  starting transfers between devices  56.8 us (12%)
  other arithmetic  34.5 us (7%)
    all_to_all x7, waiting for transfers between devices, exchange(): return lax.all_to_all(value, AXES, split_axis=0, concat_axis=0, tiled=True)  149 us
    all_to_all x7, starting transfers between devices, exchange(): return lax.all_to_all(value, AXES, split_axis=0, concat_axis=0, tiled=True)  45.7 us
    dot_general x3, matrix products, per_device(): lax.dot_general(returned[index].reshape(-1, cells), tables[index], (((0,)...  25.4 us
    convert_element_type x2, other arithmetic, wave_table(): (scale[:, None] * jnp.cos(steps * (2.0 * math.pi / lon_count))).astype(jn...  25 us
    reshape x3, local copies, waits for them, and re-layouts, spectral(): grid_coef.transpose(3, 1, 2, 0, 4, 5).reshape(devices, 2 * count, cells)  22.3 us
    dot_general x3, matrix products, forward(): lax.dot_general(table, rows_flat, (((1,), (1,)), ((), ())), preferred_ele...  21.3 us
    reshape x3, local copies, waits for them, and re-layouts, spectral(): fields = arrived.reshape(groups, owners, 2, count, lev_dev, lat_dev)  21.2 us
    dot_general x3, matrix products, spectral(): jnp.einsum('smn,swrn->swmr', solved.reshape(count, 2 * groups * lev_dev,...  17 us
  transfers between devices with their start and end apart: 12, of which 10 were waited for; matrix products, arithmetic and copies ran while one was open for 37% of the time, Pallas kernels for 0%

profile of v1, /device:TPU:0, one launch (start us, length us, event | category | flops | bytes accessed | tf_op | source)
XLA Modules:
  0.0 483.2 jit_solution(164190003681796666)
XLA Ops:
  2.0 5.2 %multiply_convert_fusion.2 = bf16[256,1280]{1,0:T(8,128)(2,1)S(1)} fusion(s32[256]{0:T(256)S(1)} %add.315, s32[256]{0:T(256)S(1)} %mul.430, f32[256]{0:T(256)S(1)} %mul.428), kind=kLoop, calls=%fused_computation.49 | loop fusion | flops 3276800 | bytes 658432 | tf_op jit(solution)/shard_map/convert_element_type | solution.py:42
  8.1 5.8 %fusion.4 = bf16[32,8,2560]{2,1,0:T(8,128)(2,1)} fusion(bf16[256,1280]{1,0:T(8,128)(2,1)S(1)} %multiply_convert_fusion.2, bf16[2560,1280]{1,0:T(8,128)(2,1)} %bitcast.277), kind=kOutput, calls=%fused_computation.19 | convolution fusion | flops 1678376960 | bytes 8519680 | tf_op jit(solution)/shard_map/dot_general | solution.py:138
  13.9 7.3 %all-to-all-start.4 = ((bf16[32,8,2560]{2,1,0:T(8,128)(2,1)}), bf16[32,8,2560]{2,1,0:T(8,128)(2,1)S(1)}, u32[]{:S(2)}, u32[]{:S(2)}) async-start(bf16[32,8,2560]{2,1,0:T(8,128)(2,1)} %fusion.4), calls=%async_computation.4 | async-start | bytes 2621440 | tf_op jit(solution)/shard_map/all_to_all | solution.py:29
  22.1 19.8 %multiply_convert_fusion = (bf16[512,1280]{1,0:T(8,128)(2,1)S(1)}, bf16[512,1280]{1,0:T(8,128)(2,1)S(1)}) fusion(s32[512]{0:T(512)S(1)} %mul.418, f32[512]{0:T(512)S(1)} %mul.416, s32[512]{0:T(512)S(1)} %add.295, s32[512]{0:T(512)S(1)} %mul.401, f32[512]{0:T(512)S(1)} %mul.399), kind=kLoop, calls=%fused_computation.30 | loop fusion | flops 13107200 | bytes 2631680 | tf_op jit(solution)/shard_map/convert_element_type | solution.py:42
  43.0 7.7 %convolution_convert_fusion.1 = bf16[512,2560]{1,0:T(8,128)(2,1)} fusion(bf16[512,1280]{1,0:T(8,128)(2,1)S(1)} %get-tuple-element.58, bf16[2560,1280]{1,0:T(8,128)(2,1)} %bitcast.278), kind=kOutput, calls=%fused_computation.17 | convolution fusion | flops 3356753920 | bytes 10485760 | tf_op jit(solution)/shard_map/dot_general | solution.py:138
  50.7 3.6 all-to-all-done.4
  55.4 3.5 all-to-all-start
  58.9 7.7 %convolution_convert_fusion = bf16[512,2560]{1,0:T(8,128)(2,1)} fusion(bf16[512,1280]{1,0:T(8,128)(2,1)S(1)} %get-tuple-element.57, bf16[2560,1280]{1,0:T(8,128)(2,1)} %bitcast.279), kind=kOutput, calls=%fused_computation.16 | convolution fusion | flops 3356753920 | bytes 10485760 | tf_op jit(solution)/shard_map/dot_general | solution.py:138
  66.7 53.5 %all-to-all-done = bf16[32,16,2560]{2,1,0:T(8,128)(2,1)} async-done(((bf16[32,16,2560]{2,1,0:T(8,128)(2,1)}), bf16[32,16,2560]{2,1,0:T(8,128)(2,1)}, u32[]{:S(2)}, u32[]{:S(2)}) %all-to-all-start) | async-done | bytes 2621472 | tf_op jit(solution)/shard_map/all_to_all | solution.py:29
  120.2 3.8 all-to-all-start.2
  126.7 1.1 gather_fusion.1
  130.0 2.2 constant_dynamic-slice_fusion.2
  134.8 10.5 %constant_dynamic-slice_fusion.3 = (bf16[8,640,640]{2,1,0:T(8,128)(2,1)}, bf16[8,640,640]{2,1,0:T(8,128)(2,1)}) fusion(bf16[80,640,640]{2,1,0:T(8,128)(2,1)} %param.17, s32[]{:T(128)S(6)} %select_n.105, s32[]{:T(128)S(6)} %select_n.100), kind=kLoop, calls=%fused_computation.162 | loop fusion | bytes 26214408 | tf_op jit(solution)/shard_map/dynamic_slice | solution.py:149
  145.3 4.8 reshape.404
  150.1 2.2 copy.108
  152.3 2.5 fusion.98
  154.8 2.4 copy.110
  157.2 4.1 multiply_reduce_fusion.2
  161.3 1.7 convolution_convert_fusion.7
  163.1 8.1 %reshape.386 = bf16[4,8,2,8,32,80]{5,4,3,2,1,0:T(8,128)(2,1)} reshape(bf16[32,16,2560]{2,1,0:T(8,128)(2,1)} %all-to-all-done) | data formatting | bytes 5242880 | tf_op jit(solution)/shard_map/reshape | solution.py:152
  171.3 5.5 %copy.94 = bf16[8,8,2,4,32,80]{5,4,3,2,1,0:T(8,128)(2,1)} copy(bf16[8,8,2,4,32,80]{5,4,0,2,1,3:T(8,128)(2,1)} %bitcast.269) | data formatting | bytes 5242880 | tf_op jit(solution)/shard_map/transpose | solution.py:153
  176.7 8.6 %all-to-all-done.2 = bf16[32,16,2560]{2,1,0:T(8,128)(2,1)} async-done(((bf16[32,16,2560]{2,1,0:T(8,128)(2,1)}), bf16[32,16,2560]{2,1,0:T(8,128)(2,1)}, u32[]{:S(2)}, u32[]{:S(2)}) %all-to-all-start.2) | async-done | bytes 2621472 | tf_op jit(solution)/shard_map/all_to_all | solution.py:29
  185.3 8.3 %reshape.395 = bf16[4,8,2,8,32,80]{5,4,3,2,1,0:T(8,128)(2,1)} reshape(bf16[32,16,2560]{2,1,0:T(8,128)(2,1)} %all-to-all-done.2) | data formatting | bytes 5242880 | tf_op jit(solution)/shard_map/reshape | solution.py:152
  193.6 5.6 %copy.101 = bf16[8,8,2,4,32,80]{5,4,3,2,1,0:T(8,128)(2,1)} copy(bf16[8,8,2,4,32,80]{5,4,0,2,1,3:T(8,128)(2,1)} %bitcast.270) | data formatting | bytes 5242880 | tf_op jit(solution)/shard_map/transpose | solution.py:153
  199.3 4.1 fusion.95
  203.4 3.4 copy.96
  206.8 8.2 %fusion.97 = bf16[8,256,640,1]{2,1,3,0:T(8,128)(2,1)} fusion(bf16[8,8,256,80]{3,2,1,0:T(8,128)(2,1)} %bitcast.283, bf16[8,8,80,640]{3,2,1,0:T(8,128)(2,1)} %bitcast.263), kind=kOutput, calls=%fused_computation.180 | convolution fusion | flops 1677721600 | bytes 11796480 | tf_op jit(solution)/shard_map/swmr,swrn->smn/dot_general | solution.py:157
  215.0 4.5 copy.103
  219.5 4.6 multiply_reduce_fusion
  224.1 4.7 convolution_convert_fusion.5
  229.0 3.3 multiply_reduce_fusion.1
  232.3 4.8 convolution_convert_fusion.6
  238.1 2.6 all-to-all-start.6
  240.7 12.0 %all-to-all-done.6 = bf16[32,40,80]{2,1,0:T(8,128)(2,1)S(1)} async-done(((bf16[32,40,80]{2,1,0:T(8,128)(2,1)}), bf16[32,40,80]{2,1,0:T(8,128)(2,1)S(1)}, u32[]{:S(2)}, u32[]{:S(2)}) %all-to-all-start.6) | async-done | bytes 204832 | tf_op jit(solution)/shard_map/all_to_all | solution.py:29
  253.0 1.7 convolution_add_fusion.3
  256.9 3.7 all-to-all-start.7
  260.7 7.3 %convert_bitcast_fusion.1 = bf16[8,8,256,80]{2,3,1,0:T(8,128)(2,1)} fusion(bf16[8,8,80,640]{3,2,1,0:T(8,128)(2,1)} %bitcast.265, bf16[8,256,640,1]{2,1,3,0:T(8,128)(2,1)} %bitcast.299), kind=kOutput, calls=%fused_computation.31 | convolution fusion | flops 1679032320 | bytes 11796480 | tf_op jit(solution)/shard_map/smn,swrn->swmr/dot_general | solution.py:172
  268.0 6.0 %copy.98 = bf16[8,8,256,80]{3,2,1,0:T(8,128)(2,1)} copy(bf16[8,8,256,80]{2,3,1,0:T(8,128)(2,1)} %convert_bitcast_fusion.1) | data formatting | bytes 5242880 | tf_op jit(solution)/shard_map/convert_element_type | solution.py:177
  274.1 5.5 %copy.99 = bf16[4,8,2,8,32,80]{5,4,3,2,1,0:T(8,128)(2,1)} copy(bf16[4,8,2,8,32,80]{5,4,0,2,1,3:T(8,128)(2,1)} %bitcast.271) | data formatting | bytes 5242880 | tf_op jit(solution)/shard_map/transpose | solution.py:179
  279.5 8.6 %reshape.391 = bf16[32,16,2560]{2,1,0:T(8,128)(2,1)} reshape(bf16[4,8,2,8,32,80]{5,4,3,2,1,0:T(8,128)(2,1)} %copy.99) | data formatting | bytes 5242880 | tf_op jit(solution)/shard_map/reshape | solution.py:179
  288.1 4.3 all-to-all-start.1
  292.4 7.3 %convert_bitcast_fusion = bf16[8,8,256,80]{2,3,1,0:T(8,128)(2,1)} fusion(bf16[8,8,80,640]{3,2,1,0:T(8,128)(2,1)} %bitcast.264, bf16[8,256,640,1]{2,1,3,0:T(8,128)(2,1)} %bitcast.298), kind=kOutput, calls=%fused_computation.28 | convolution fusion | flops 1679032320 | bytes 11796480 | tf_op jit(solution)/shard_map/smn,swrn->swmr/dot_general | solution.py:172
  299.7 6.0 %copy.105 = bf16[8,8,256,80]{3,2,1,0:T(8,128)(2,1)} copy(bf16[8,8,256,80]{2,3,1,0:T(8,128)(2,1)} %convert_bitcast_fusion) | data formatting | bytes 5242880 | tf_op jit(solution)/shard_map/convert_element_type | solution.py:177
  305.7 5.4 %copy.106 = bf16[4,8,2,8,32,80]{5,4,3,2,1,0:T(8,128)(2,1)} copy(bf16[4,8,2,8,32,80]{5,4,0,2,1,3:T(8,128)(2,1)} %bitcast.272) | data formatting | bytes 5242880 | tf_op jit(solution)/shard_map/transpose | solution.py:179
  311.1 8.6 %reshape.400 = bf16[32,16,2560]{2,1,0:T(8,128)(2,1)} reshape(bf16[4,8,2,8,32,80]{5,4,3,2,1,0:T(8,128)(2,1)} %copy.106) | data formatting | bytes 5242880 | tf_op jit(solution)/shard_map/reshape | solution.py:179
  319.8 33.9 %all-to-all-done.1 = bf16[32,16,2560]{2,1,0:T(8,128)(2,1)} async-done(((bf16[32,16,2560]{2,1,0:T(8,128)(2,1)}), bf16[32,16,2560]{2,1,0:T(8,128)(2,1)}, u32[]{:S(2)}, u32[]{:S(2)}) %all-to-all-start.1) | async-done | bytes 2621472 | tf_op jit(solution)/shard_map/all_to_all | solution.py:29
  353.7 3.5 all-to-all-start.3
  357.3 3.5 collective-permute-start
  360.8 1.3 collective-permute-start.1
  363.2 3.8 collective-permute-done
  367.0 6.6 %collective-permute-done.1 = bf16[11,4,128]{2,1,0:T(4,128)(2,1)S(1)} collective-permute-done((bf16[11,4,128]{2,1,0:T(4,128)(2,1)S(1)}, bf16[11,4,128]{2,1,0:T(4,128)(2,1)S(1)}, u32[]{:S(2)}, u32[]{:S(2)}) %collective-permute-start.1) | collective-permute-done | bytes 11296 | tf_op jit(solution)/shard_map/ppermute | solution.py:23
  373.7 1.3 collective-permute-start.2
  375.0 1.3 collective-permute-start.3
  376.4 2.5 collective-permute-done.3
  381.9 2.3 fusion.25
  384.2 3.8 copy.112
  388.0 3.6 copy.113
  391.5 5.1 %reshape.409 = bf16[32,8,2560]{2,1,0:T(8,128)(2,1)} reshape(bf16[4,8,2,4,32,80]{5,4,3,2,1,0:T(8,128)(2,1)} %copy.113) | data formatting | bytes 2621440 | tf_op jit(solution)/shard_map/reshape | solution.py:179
  396.6 21.9 %all-to-all-done.3 = bf16[32,16,2560]{2,1,0:T(8,128)(2,1)} async-done(((bf16[32,16,2560]{2,1,0:T(8,128)(2,1)}), bf16[32,16,2560]{2,1,0:T(8,128)(2,1)}, u32[]{:S(2)}, u32[]{:S(2)}) %all-to-all-start.3) | async-done | bytes 2621472 | tf_op jit(solution)/shard_map/all_to_all | solution.py:29
  418.5 20.6 %all-to-all-start.5 = ((bf16[32,8,2560]{2,1,0:T(8,128)(2,1)}), bf16[32,8,2560]{2,1,0:T(8,128)(2,1)}, u32[]{:S(2)}, u32[]{:S(2)}) async-start(bf16[32,8,2560]{2,1,0:T(8,128)(2,1)} %reshape.409), calls=%async_computation.5 | async-start | bytes 2621440 | tf_op jit(solution)/shard_map/all_to_all | solution.py:29
  441.6 5.3 %fusion.96 = f32[2560,1280]{1,0:T(8,128)S(1)} fusion(bf16[512,2560]{1,0:T(8,128)(2,1)} %bitcast.23, bf16[512,1280]{1,0:T(8,128)(2,1)S(1)} %copy-done.10), kind=kOutput, calls=%fused_computation.179 | convolution fusion | flops 3355443200 | bytes 17039360 | tf_op jit(solution)/shard_map/dot_general | solution.py:215
  446.9 9.3 %convolution_add_fusion.1 = f32[2560,1280]{1,0:T(8,128)} fusion(f32[2560,1280]{1,0:T(8,128)S(1)} %fusion.96, bf16[512,2560]{1,0:T(8,128)(2,1)} %bitcast.45, bf16[512,1280]{1,0:T(8,128)(2,1)S(1)} %copy-done.6), kind=kOutput, calls=%fused_computation.6 | convolution fusion | flops 3358720000 | bytes 30146560 | tf_op jit(solution)/shard_map/dot_general | solution.py:215
  456.2 16.0 %all-to-all-done.5 = bf16[32,8,2560]{2,1,0:T(8,128)(2,1)} async-done(((bf16[32,8,2560]{2,1,0:T(8,128)(2,1)}), bf16[32,8,2560]{2,1,0:T(8,128)(2,1)}, u32[]{:S(2)}, u32[]{:S(2)}) %all-to-all-start.5) | async-done | bytes 1310752 | tf_op jit(solution)/shard_map/all_to_all | solution.py:29
  472.2 10.8 %fusion.1 = bf16[2560,1280]{1,0:T(8,128)(2,1)} fusion(bf16[2560,1280]{1,0:T(8,128)(2,1)} %bitcast.280, f32[2560,1280]{1,0:T(8,128)} %convolution_add_fusion.1, bf16[256,1280]{1,0:T(8,128)(2,1)S(1)} %copy-done.8, f32[2560]{0:T(1024)S(1)} %mul.443, bf16[32,8,2560]{2,1,0:T(8,128)(2,1)} %all-to-all-done.5), kind=kOutput, calls=%fused_computation.7 | convolution fusion | flops 1697382400 | bytes 28190720 | tf_op jit(solution)/shard_map/dot_general | solution.py:215
  (165 shorter events, 22.9 us)
Async XLA Ops:
  0.6 255.3 %copy-start = (bf16[1,8,128,128]{3,2,1,0:T(8,128)(2,1)S(1)}, bf16[1,8,128,128]{3,2,1,0:T(8,128)(2,1)}, u32[]{:S(2)}) copy-start(bf16[1,8,128,128]{3,2,1,0:T(8,128)(2,1)} %param.24) | copy-start | bytes 786436
  7.2 0.9 copy-start.7
  13.9 40.4 %all-to-all-start.4 = ((bf16[32,8,2560]{2,1,0:T(8,128)(2,1)}), bf16[32,8,2560]{2,1,0:T(8,128)(2,1)S(1)}, u32[]{:S(2)}, u32[]{:S(2)}) async-start(bf16[32,8,2560]{2,1,0:T(8,128)(2,1)} %fusion.4), calls=%async_computation.4 | async-start | bytes 2621440 | tf_op jit(solution)/shard_map/all_to_all | solution.py:29
  41.8 1.1 copy-start.9
  41.8 17.1 %copy-start.5 = (bf16[512,1280]{1,0:T(8,128)(2,1)}, bf16[512,1280]{1,0:T(8,128)(2,1)S(1)}, u32[]{:S(2)}) copy-start(bf16[512,1280]{1,0:T(8,128)(2,1)S(1)} %get-tuple-element.57) | copy-start | bytes 3932164
  54.3 1.1 copy-start.11
  55.4 64.8 %all-to-all-start = ((bf16[32,16,2560]{2,1,0:T(8,128)(2,1)}), bf16[32,16,2560]{2,1,0:T(8,128)(2,1)}, u32[]{:S(2)}, u32[]{:S(2)}) async-start(bf16[32,16,2560]{2,1,0:T(8,128)(2,1)} %bitcast.285), calls=%async_computation | async-start | bytes 5242880 | tf_op jit(solution)/shard_map/all_to_all | solution.py:29
  120.2 4.4 copy-start.27
  120.2 5.2 %copy-start.2 = (s32[640]{0:T(1024)S(1)}, s32[640]{0:T(1024)}, u32[]{:S(2)}) copy-start(s32[640]{0:T(1024)} %param.18) | copy-start | bytes 7684
  120.2 7.7 %copy-start.28 = (s32[1,64]{1,0:T(1,128)S(1)}, s32[1,64]{1,0:T(1,128)}, u32[]{:S(2)}) copy-start(s32[1,64]{1,0:T(1,128)} %param.26) | copy-start | bytes 772
  120.2 65.1 %all-to-all-start.2 = ((bf16[32,16,2560]{2,1,0:T(8,128)(2,1)}), bf16[32,16,2560]{2,1,0:T(8,128)(2,1)}, u32[]{:S(2)}, u32[]{:S(2)}) async-start(bf16[32,16,2560]{2,1,0:T(8,128)(2,1)} %bitcast.284), calls=%async_computation.2 | async-start | bytes 5242880 | tf_op jit(solution)/shard_map/all_to_all | solution.py:29
  130.0 2.3 copy-start.21
  130.0 3.9 copy-start.22
  132.2 29.1 %copy-start.3 = (bf16[4,640,640]{2,1,0:T(8,128)(2,1)}, bf16[4,640,640]{2,1,0:T(8,128)(2,1)S(1)}, u32[]{:S(2)}) copy-start(bf16[4,640,640]{2,1,0:T(8,128)(2,1)S(1)} %constant_dynamic-slice_fusion.2) | copy-start | bytes 9830404
  154.8 2.4 copy-start.29
  185.3 13.9 %slice-start = ((s8[6553600]{0:T(1024)(128)(4,1)}), s8[2359296]{0:T(1024)(128)(4,1)S(1)}, s32[]{:S(2)}) async-start(s8[6553600]{0:T(1024)(128)(4,1)} %bitcast.266), calls=%async_computation.8 | async-start | bytes 4718592
  193.6 5.7 %slice-start.1 = ((s8[6553600]{0:T(1024)(128)(4,1)}), s8[4194304]{0:T(1024)(128)(4,1)S(1)}, s32[]{:S(2)}) async-start(s8[6553600]{0:T(1024)(128)(4,1)} %bitcast.266), calls=%async_computation.9 | async-start | bytes 8388608
  193.6 5.7 %copy-start.12 = (bf16[8,8,2,4,32,80]{5,4,3,2,1,0:T(8,128)(2,1)S(1)}, bf16[8,8,2,4,32,80]{5,4,3,2,1,0:T(8,128)(2,1)}, u32[]{:S(2)}) copy-start(bf16[8,8,2,4,32,80]{5,4,3,2,1,0:T(8,128)(2,1)} %copy.94) | copy-start | bytes 7864324
  215.0 4.5 copy-start.13
  215.0 4.5 copy-start.20
  215.0 4.5 copy-start.25
  215.0 4.5 copy-start.26
  215.0 4.5 copy-start.30
  224.1 4.9 %copy-start.19 = (pred[8,640]{1,0:T(8,128)(4,1)S(1)}, pred[8,640]{1,0:T(8,128)(4,1)}, u32[]{:S(2)}) copy-start(pred[8,640]{1,0:T(8,128)(4,1)} %iota_compare_fusion.2) | copy-start | bytes 15364
  232.3 8.4 %copy-start.15 = (s32[8,8]{1,0:T(8,128)S(1)}, s32[8,8]{1,0:T(8,128)}, u32[]{:S(2)}) copy-start(s32[8,8]{1,0:T(8,128)} %convert_reduce_fusion) | copy-start | bytes 772
  232.3 8.4 %copy-start.24 = (s32[8]{0:T(128)S(1)}, s32[8]{0:T(128)}, u32[]{:S(2)}) copy-start(s32[8]{0:T(128)} %fusion.78) | copy-start | bytes 100
  232.3 20.4 %copy-start.8 = (bf16[256,1280]{1,0:T(8,128)(2,1)S(1)}, bf16[256,1280]{1,0:T(8,128)(2,1)}, u32[]{:S(2)}) copy-start(bf16[256,1280]{1,0:T(8,128)(2,1)} %copy-done.7) | copy-start | bytes 1966084
  237.2 17.4 %copy-start.6 = (bf16[512,1280]{1,0:T(8,128)(2,1)S(1)}, bf16[512,1280]{1,0:T(8,128)(2,1)}, u32[]{:S(2)}) copy-start(bf16[512,1280]{1,0:T(8,128)(2,1)} %copy-done.5) | copy-start | bytes 3932164
  238.1 14.6 %all-to-all-start.6 = ((bf16[32,40,80]{2,1,0:T(8,128)(2,1)}), bf16[32,40,80]{2,1,0:T(8,128)(2,1)S(1)}, u32[]{:S(2)}, u32[]{:S(2)}) async-start(bf16[32,40,80]{2,1,0:T(8,128)(2,1)} %bitcast.93), calls=%async_computation.6 | async-start | bytes 655360 | tf_op jit(solution)/shard_map/all_to_all | solution.py:29
  253.0 2.9 copy-start.23
  256.9 31.2 %all-to-all-start.7 = ((f32[8,2,128]{2,1,0:T(2,128)}), f32[8,2,128]{2,1,0:T(2,128)S(1)}, u32[]{:S(2)}, u32[]{:S(2)}) async-start(f32[8,2,128]{2,1,0:T(2,128)} %bitcast.103), calls=%async_computation.7 | async-start | bytes 16384 | tf_op jit(solution)/shard_map/all_to_all | solution.py:247
  288.1 65.6 %all-to-all-start.1 = ((bf16[32,16,2560]{2,1,0:T(8,128)(2,1)}), bf16[32,16,2560]{2,1,0:T(8,128)(2,1)}, u32[]{:S(2)}, u32[]{:S(2)}) async-start(bf16[32,16,2560]{2,1,0:T(8,128)(2,1)} %reshape.391), calls=%async_computation.1 | async-start | bytes 5242880 | tf_op jit(solution)/shard_map/all_to_all | solution.py:29
  319.7 37.5 %copy-start.16 = (s32[48,128]{1,0:T(8,128)S(1)}, s32[48,128]{1,0:T(8,128)}, u32[]{:S(2)}) copy-start(s32[48,128]{1,0:T(8,128)} %param.31) | copy-start | bytes 73732
  319.7 37.5 %copy-start.17 = (f32[48,128]{1,0:T(8,128)S(1)}, f32[48,128]{1,0:T(8,128)}, u32[]{:S(2)}) copy-start(f32[48,128]{1,0:T(8,128)} %param.30) | copy-start | bytes 73732
  319.7 37.5 %copy-start.18 = (f32[48,128]{1,0:T(8,128)S(1)}, f32[48,128]{1,0:T(8,128)}, u32[]{:S(2)}) copy-start(f32[48,128]{1,0:T(8,128)} %param.29) | copy-start | bytes 73732
  319.7 37.5 %copy-start.14 = (f32[8,48,128]{2,1,0:T(8,128)S(1)}, f32[8,48,128]{2,1,0:T(8,128)}, u32[]{:S(2)}) copy-start(f32[8,48,128]{2,1,0:T(8,128)} %param.28) | copy-start | bytes 589828
  319.7 42.4 %copy-start.31 = (s32[1,64]{1,0:T(1,128)S(1)}, s32[1,64]{1,0:T(1,128)}, u32[]{:S(2)}) copy-start(s32[1,64]{1,0:T(1,128)} %param.27) | copy-start | bytes 772
  319.7 43.1 %copy-start.32 = (s32[80]{0:T(128)S(1)}, s32[80]{0:T(128)}, u32[]{:S(2)}) copy-start(s32[80]{0:T(128)} %param.19) | copy-start | bytes 964
  353.7 64.8 %all-to-all-start.3 = ((bf16[32,16,2560]{2,1,0:T(8,128)(2,1)}), bf16[32,16,2560]{2,1,0:T(8,128)(2,1)}, u32[]{:S(2)}, u32[]{:S(2)}) async-start(bf16[32,16,2560]{2,1,0:T(8,128)(2,1)} %reshape.400), calls=%async_computation.3 | async-start | bytes 5242880 | tf_op jit(solution)/shard_map/all_to_all | solution.py:29
  357.3 9.6 %collective-permute-start = (bf16[11,4,128]{2,1,0:T(4,128)(2,1)S(1)}, bf16[11,4,128]{2,1,0:T(4,128)(2,1)S(1)}, u32[]{:S(2)}, u32[]{:S(2)}) collective-permute-start(bf16[11,4,128]{2,1,0:T(4,128)(2,1)S(1)} %get-tuple-element.51), channel_id=1, source_target_pairs={{0,8},{8,16},{16,24},{1,9},{9,17},{17,25},{2,10},{10,18},{18,26},{... | collective-permute-start | bytes 33800 | tf_op jit(solution)/shard_map/ppermute | solution.py:22
  360.8 12.7 %collective-permute-start.1 = (bf16[11,4,128]{2,1,0:T(4,128)(2,1)S(1)}, bf16[11,4,128]{2,1,0:T(4,128)(2,1)S(1)}, u32[]{:S(2)}, u32[]{:S(2)}) collective-permute-start(bf16[11,4,128]{2,1,0:T(4,128)(2,1)S(1)} %get-tuple-element.52), channel_id=1, source_target_pairs={{8,0},{16,8},{24,16},{9,1},{17,9},{25,17},{10,2},{18,10},{26,18},{... | collective-permute-start | bytes 33800 | tf_op jit(solution)/shard_map/ppermute | solution.py:23
  373.7 2.7 collective-permute-start.2
  375.0 3.9 collective-permute-start.3
  379.6 1.9 copy-start.4
  379.6 2.3 copy-start.33
  418.5 53.7 %all-to-all-start.5 = ((bf16[32,8,2560]{2,1,0:T(8,128)(2,1)}), bf16[32,8,2560]{2,1,0:T(8,128)(2,1)}, u32[]{:S(2)}, u32[]{:S(2)}) async-start(bf16[32,8,2560]{2,1,0:T(8,128)(2,1)} %reshape.409), calls=%async_computation.5 | async-start | bytes 2621440 | tf_op jit(solution)/shard_map/all_to_all | solution.py:29
  439.1 2.5 copy-start.10
  472.2 10.8 %copy-start.1 = (bf16[1,8,128,128]{3,2,1,0:T(8,128)(2,1)S(1)}, bf16[1,8,128,128]{3,2,1,0:T(8,128)(2,1)}, u32[]{:S(2)}) copy-start(bf16[1,8,128,128]{3,2,1,0:T(8,128)(2,1)} %param.24) | copy-start | bytes 786436

commit v2 on v1

--- a/solution.py
+++ b/solution.py
@@ -1,15 +1,20 @@
+import functools
 import math
 
 import jax
 import jax.numpy as jnp
 from jax import lax
+from jax.experimental import pallas as pl
+from jax.experimental.pallas import tpu as pltpu
 from jax.sharding import PartitionSpec as P
 
 
 SWEEPS = 4
 CAP = 2
 AXES = ("lev", "wav")
-CHUNKS = (1, 2, 2)
+CHUNKS = (2, 3)
+UNIT = 4
+LANES = 128
 
 
 def with_halo(value, sides, width):
@@ -29,31 +34,241 @@
     return lax.all_to_all(value, AXES, split_axis=0, concat_axis=0, tiled=True)
 
 
-def wave_table(waves, valid, lon_count):
-    shape = waves.shape[:-1] + (2, waves.shape[-1])
-    quarter = jnp.arange(2, dtype=jnp.int32) * (lon_count // 4)
-    quarter = jnp.broadcast_to(quarter[:, None], shape).reshape(-1)
-    waves = jnp.broadcast_to(waves[..., None, :], shape).reshape(-1)
-    scale = jnp.where(valid, math.sqrt(2.0 / lon_count), 0.0)
-    scale = jnp.broadcast_to(scale[..., None, :], shape).reshape(-1)
-    longitude = jnp.arange(lon_count, dtype=jnp.int32)
-    steps = (waves[:, None] * longitude[None, :] + quarter[:, None]).astype(jnp.float32)
-    steps = steps - lon_count * jnp.round(steps * (1.0 / lon_count))
-    return (scale[:, None] * jnp.cos(steps * (2.0 * math.pi / lon_count))).astype(jnp.bfloat16)
-
-
-def return_order(steps):
-    return list(range(1, steps)) + [0]
-
-
-def split_slots(count):
-    total = sum(CHUNKS)
+def table_kernel(unit, lon_count, waves_ref, table_ref):
+    rows = waves_ref.shape[0]
+    lane = lax.broadcasted_iota(jnp.int32, (rows, LANES), 1)
+    half = (lax.broadcasted_iota(jnp.int32, (rows, LANES), 0) // unit) % 2
+    waves = jnp.broadcast_to(waves_ref[...], (rows, LANES))
+    scale = jnp.where(waves < 0, 0.0, math.sqrt(2.0 / lon_count))
+
+    def angle(steps):
+        steps = steps.astype(jnp.float32)
+        steps = steps - lon_count * jnp.round(steps * (1.0 / lon_count))
+        return steps * (2.0 * math.pi / lon_count)
+
+    low = angle(waves * lane + half * (lon_count // 4))
+    high = angle(waves * (lane * LANES))
+    cos_low, sin_low = scale * jnp.cos(low), scale * jnp.sin(low)
+    cos_high, sin_high = jnp.cos(high), jnp.sin(high)
+    for tile in range(lon_count // LANES):
+        part = cos_low * cos_high[:, tile : tile + 1] - sin_low * sin_high[:, tile : tile + 1]
+        table_ref[:, tile * LANES : (tile + 1) * LANES] = part.astype(jnp.bfloat16)
+
+
+def wave_table(waves, valid, unit, lon_count):
+    devices, count = waves.shape
+    waves = jnp.where(valid, waves, -1).reshape(devices, count // unit, 1, unit)
+    waves = jnp.broadcast_to(waves, (devices, count // unit, 2, unit)).reshape(-1, 1)
+    rows = waves.shape[0]
+    block = math.gcd(rows, 128)
+    if block % (2 * unit):
+        block = rows
+    return pl.pallas_call(
+        functools.partial(table_kernel, unit, lon_count),
+        grid=(rows // block,),
+        in_specs=[pl.BlockSpec((block, 1), lambda i: (i, 0))],
+        out_specs=pl.BlockSpec((block, lon_count), lambda i: (i, 0)),
+        out_shape=jax.ShapeDtypeStruct((rows, lon_count), jnp.bfloat16),
+    )(waves)
+
+
+def segments(length, source, target):
+    cuts = {0}
+    cuts.update(i for i in range(1, length) if (source + i) % LANES == 0)
+    cuts.update(i for i in range(1, length) if (target + i) % LANES == 0)
+    return [
+        ((source + i) // LANES, (target + i) // LANES, (target + i) % LANES) for i in sorted(cuts)
+    ]
+
+
+def move_runs(load, store, lane, runs):
+    tile, value = 0, None
+    for index, source, target, length in runs:
+        for src, dst, low in segments(length, source, target):
+            piece = pltpu.roll(load(index, src), (target - source) % LANES, 1) if (
+                target - source
+            ) % LANES else load(index, src)
+            if dst != tile:
+                store(tile, value)
+                tile, value = dst, None
+            value = piece if low == 0 else jnp.where(lane >= low, piece, value)
+    store(tile, value)
+
+
+def spectral_kernel(
+    groups,
+    owners,
+    lev_dev,
+    lat_dev,
+    base_ref,
+    waves_ref,
+    arrived_ref,
+    leg_ref,
+    analysis_ref,
+    synthesis_ref,
+    damping_ref,
+    weights_ref,
+    sent_ref,
+    flux_ref,
+    stage_ref,
+):
+    rows = 2 * UNIT
+    levels = groups * lev_dev
+    wave_count = leg_ref.shape[2]
+    width = owners * lat_dev
+    unit = pl.program_id(0)
+    lane = lax.broadcasted_iota(jnp.int32, (rows, LANES), 1)
+
+    def take(group, carry):
+        for x in range(lev_dev):
+            first = pl.multiple_of((group * lev_dev + x) * rows, rows)
+
+            def load(owner, tile):
+                part = arrived_ref[group * owners + owner, :, tile * LANES : (tile + 1) * LANES]
+                return part.astype(jnp.float32)
+
+            def store(tile, value):
+                stage_ref[tile, pl.ds(first, rows), :] = value
+
+            move_runs(
+                load,
+                store,
+                lane,
+                [(w, x * lat_dev, w * lat_dev, lat_dev) for w in range(owners)],
+            )
+        return carry
+
+    lax.fori_loop(0, groups, take, 0)
+    degree = lax.broadcasted_iota(jnp.int32, (2 * levels, wave_count), 1)
+    flux_row = lax.broadcasted_iota(jnp.int32, (16, wave_count), 0)
+
+    def solve(slot, carry):
+        halves = [
+            [
+                stage_ref[tile, pl.ds(k * UNIT + slot, levels, stride=rows), :]
+                for tile in range(width // LANES)
+            ]
+            for k in range(2)
+        ]
+        fields = jnp.concatenate([jnp.concatenate(half, axis=1) for half in halves], axis=0)
+        leg = leg_ref[slot]
+        spectra = jnp.dot(fields.astype(jnp.bfloat16), leg, preferred_element_type=jnp.float32)
+        wave = waves_ref[unit * UNIT + slot]
+        spectra = jnp.where(degree >= wave, spectra, 0.0).astype(jnp.bfloat16)
+        solved, flux = [], 0.0
+        for k in range(2):
+            modal = jnp.dot(
+                analysis_ref[...],
+                spectra[k * levels : (k + 1) * levels],
+                preferred_element_type=jnp.float32,
+            )
+            modal = (modal * damping_ref[...]).astype(jnp.bfloat16)
+            part = jnp.dot(
+                synthesis_ref[...], modal, preferred_element_type=jnp.float32
+            ).astype(jnp.bfloat16)
+            coef = jnp.sum(weights_ref[...] * part.astype(jnp.float32), axis=0, keepdims=True)
+            flux = jnp.where(flux_row == k, coef, flux)
+            solved.append(part)
+        solved.append(flux.astype(jnp.bfloat16))
+        grid = lax.dot_general(
+            jnp.concatenate(solved, axis=0),
+            leg,
+            (((1,), (1,)), ((), ())),
+            preferred_element_type=jnp.float32,
+        )
+        for k in range(2):
+            for tile in range(width // LANES):
+                stage_ref[tile, pl.ds(k * UNIT + slot, levels, stride=rows), :] = grid[
+                    k * levels : (k + 1) * levels, tile * LANES : (tile + 1) * LANES
+                ]
+            flux_ref[0, pl.ds(k * UNIT + slot, 1), :] = grid[2 * levels + k : 2 * levels + k + 1]
+        return carry
+
+    lax.fori_loop(0, UNIT, solve, 0)
+
+    def send(group, carry):
+        for w in range(owners):
+
+            def load(x, tile):
+                first = pl.multiple_of((group * lev_dev + x) * rows, rows)
+                return stage_ref[tile, pl.ds(first, rows), :]
+
+            def store(tile, value):
+                sent_ref[group * owners + w, :, tile * LANES : (tile + 1) * LANES] = value.astype(
+                    jnp.bfloat16
+                )
+
+            move_runs(
+                load,
+                store,
+                lane,
+                [(x, w * lat_dev, x * lat_dev, lat_dev) for x in range(lev_dev)],
+            )
+        return carry
+
+    lax.fori_loop(0, groups, send, 0)
+
+
+def spectral_call(
+    arrived,
+    legendre,
+    base,
+    waves,
+    analysis,
+    synthesis,
+    damping,
+    weights,
+    groups,
+    owners,
+    lev_dev,
+    lat_dev,
+):
+    devices, columns, cells = arrived.shape
+    units = columns // (2 * UNIT)
+    levels = groups * lev_dev
+    rows_all, wave_count = legendre.shape[1:]
+    body = functools.partial(spectral_kernel, groups, owners, lev_dev, lat_dev)
+    whole = lambda shape: pl.BlockSpec(shape, lambda i, base, waves: (0,) * len(shape))
+    return pl.pallas_call(
+        body,
+        grid_spec=pltpu.PrefetchScalarGridSpec(
+            num_scalar_prefetch=2,
+            grid=(units,),
+            in_specs=[
+                pl.BlockSpec((devices, 2 * UNIT, cells), lambda i, base, waves: (0, i, 0)),
+                pl.BlockSpec(
+                    (UNIT, rows_all, wave_count), lambda i, base, waves: (base[0] + i, 0, 0)
+                ),
+                whole(analysis.shape),
+                whole(synthesis.shape),
+                whole(damping.shape),
+                whole((levels, 1)),
+            ],
+            out_specs=[
+                pl.BlockSpec((devices, 2 * UNIT, cells), lambda i, base, waves: (0, i, 0)),
+                pl.BlockSpec((1, 2 * UNIT, rows_all), lambda i, base, waves: (i, 0, 0)),
+            ],
+            scratch_shapes=[
+                pltpu.VMEM((rows_all // LANES, levels * 2 * UNIT, LANES), jnp.float32)
+            ],
+        ),
+        out_shape=[
+            jax.ShapeDtypeStruct(arrived.shape, jnp.bfloat16),
+            jax.ShapeDtypeStruct((units, 2 * UNIT, rows_all), jnp.float32),
+        ],
+        compiler_params=pltpu.CompilerParams(vmem_limit_bytes=48 * 1024 * 1024),
+    )(base, waves, arrived, legendre, analysis, synthesis, damping, weights.reshape(levels, 1))
+
+
+def split_slots(count, unit):
+    total = sum(CHUNKS) * unit
     if count % total:
         return [(0, count)]
-    unit, start, out = count // total, 0, []
+    start, out = 0, []
     for part in CHUNKS:
-        out.append((start, part * unit))
-        start += part * unit
+        part = count // sum(CHUNKS) * part
+        out.append((start, part))
+        start += part
     return out
 
 
@@ -124,28 +339,59 @@
         slot = owner * slots_owner + jnp.minimum(local, slots_owner - 1)
         return local, wave_of_slot[slot], local < slots_owner
 
-    chunks = split_slots(slots_dev)
+    exact = slots_owner == slots_dev * groups
+    fused = (
+        exact
+        and slots_dev % UNIT == 0
+        and lon_count % LANES == 0
+        and cells % LANES == 0
+        and owners * lat_dev % LANES == 0
+        and groups * lev_dev % 8 == 0
+    )
+    unit = UNIT if fused else slots_dev
+    chunks = split_slots(slots_dev, unit)
     spare = groups * slots_dev - slots_owner
     all_waves = jnp.pad(wave_of_slot.reshape(owners, slots_owner), ((0, 0), (0, spare)))
     all_waves = all_waves.reshape(owners, groups, slots_dev).transpose(1, 0, 2)
     all_valid = jnp.arange(groups * slots_dev, dtype=jnp.int32) < slots_owner
-    all_valid = all_valid.reshape(groups, 1, slots_dev)
+    all_valid = jnp.broadcast_to(all_valid.reshape(groups, 1, slots_dev), all_waves.shape)
+    all_waves = all_waves.reshape(devices, slots_dev)
+    all_valid = all_valid.reshape(devices, slots_dev)
 
     def forward(start, count):
-        waves = all_waves[:, :, start : start + count]
-        valid = jnp.broadcast_to(all_valid[:, :, start : start + count], waves.shape)
-        table = lax.optimization_barrier(wave_table(waves, valid, lon_count))
+        chosen = slice(start, start + count)
+        table = wave_table(all_waves[:, chosen], all_valid[:, chosen], unit, lon_count)
         fourier = lax.dot_general(
             table, rows_flat, (((1,), (1,)), ((), ())), preferred_element_type=jnp.float32
         ).astype(jnp.bfloat16)
         return table, fourier.reshape(devices, 2 * count, cells)
 
+    def spectral_fused(arrived, start, count):
+        base = my_group * (slots_dev // UNIT) + start // UNIT
+        first = my_owner * slots_owner + my_group * slots_dev + start
+        my_waves = lax.dynamic_slice_in_dim(wave_of_slot, first, count)
+        grid_coef, flux_lat = spectral_call(
+            arrived,
+            legendre,
+            base.astype(jnp.int32).reshape(1),
+            my_waves,
+            analysis,
+            synthesis,
+            damping,
+            flux_weights,
+            groups,
+            owners,
+            lev_dev,
+            lat_dev,
+        )
+        return grid_coef, flux_lat.astype(jnp.bfloat16).reshape(2 * count, owners, lat_dev)
+
     def spectral(arrived, start, count):
         arrived, my_analysis, my_synthesis, my_damping, my_weights = lax.optimization_barrier(
             (arrived, analysis, synthesis, damping, flux_weights)
         )
         local, my_waves, _ = slots_of(my_group, my_owner, start, count)
-        if slots_owner == slots_dev * groups:
+        if exact:
             leg = lax.dynamic_slice_in_dim(legendre, my_group * slots_dev + start, count, axis=0)
         else:
             leg = jnp.take(legendre, jnp.minimum(local, slots_owner - 1), axis=0)
@@ -189,7 +435,8 @@
         tables.append(table)
         arrivals.append(exchange(fourier))
     for index, chunk in enumerate(chunks):
-        grid_coef, flux_lat = spectral(arrivals[index], *chunk)
+        step = spectral_fused if fused else spectral
+        grid_coef, flux_lat = step(arrivals[index], *chunk)
         sent.append(grid_coef)
         flux_parts.append(flux_lat)
     for value in sent:
@@ -211,13 +458,15 @@
     )
     latitude = jnp.broadcast_to(latitude[None], (lev_dev, lat_dev)).reshape(cells, 1)
     regridded = 0.0
-    for index in return_order(len(chunks)):
+    for index in range(len(chunks)):
         regridded += lax.dot_general(
             returned[index].reshape(-1, cells),
             tables[index],
             (((0,), (0,)), ((), ())),
             preferred_element_type=jnp.float32,
         )
+        if index + 1 < len(chunks):
+            regridded = lax.optimization_barrier(regridded)
     atm_out = regridded * (1.0 + rows_flat.astype(jnp.float32) * latitude)
     atm_out = atm_out.astype(jnp.bfloat16).reshape(lev_dev, lat_dev, lon_count)
 

time: 492 us -> 414 us (0.84)
  the two profiles are of different devices: /device:TPU:0 before, /device:TPU:9 now
where the time goes in v2:
time: 414 us
  waiting for transfers between devices  185 us (45%)
  blocking collectives  71.2 us (17%)
  Pallas kernels  55.7 us (13%)
  matrix products  43.6 us (11%)
  starting transfers between devices  40.2 us (10%)
  local copies, waits for them, and re-layouts  11.3 us (3%)
  other arithmetic  5.47 us (1%)
    all_to_all x4, waiting for transfers between devices, exchange(): return lax.all_to_all(value, AXES, split_axis=0, concat_axis=0, tiled=True)  110 us
    ppermute x2, waiting for transfers between devices, with_halo(): before = lax.ppermute(last, axis, up)  65.2 us
    all_to_all x1, blocking collectives, exchange(): return lax.all_to_all(value, AXES, split_axis=0, concat_axis=0, tiled=True)  62.7 us
    pallas_call x2, Pallas kernels, spectral_call(): pl.pallas_call(body, grid_spec=pltpu.PrefetchScalarGridSpec(num_scalar_pr...  43 us
    all_to_all x4, starting transfers between devices, exchange(): return lax.all_to_all(value, AXES, split_axis=0, concat_axis=0, tiled=True)  27.7 us
    dot_general x2, matrix products, per_device(): lax.dot_general(returned[index].reshape(-1, cells), tables[index], (((0,)...  20.4 us
    dot_general x2, matrix products, forward(): lax.dot_general(table, rows_flat, (((1,), (1,)), ((), ())), preferred_ele...  18.3 us
    pallas_call x2, Pallas kernels, wave_table(): pl.pallas_call(functools.partial(table_kernel, unit, lon_count), grid=(ro...  12.7 us
  transfers between devices with their start and end apart: 8, of which 7 were waited for; matrix products, arithmetic and copies ran while one was open for 7% of the time, Pallas kernels for 6%

profile of v2, /device:TPU:9, one launch (start us, length us, event | category | flops | bytes accessed | tf_op | source)
XLA Modules:
  0.0 413.5 jit_solution(6181494355931529997)
XLA Ops:
  0.7 0.8 reshape.177
  1.6 0.1 copy.55
  1.7 0.9 reshape.207.waves_ref
  2.6 5.4 %shard_map.175 = bf16[512,1280]{1,0:T(8,128)(2,1)} custom-call(s32[512,1]{1,0:T(8,128)} %reshape.207.waves_ref), custom_call_target="tpu_custom_call" | custom-call | tf_op jit(solution)/shard_map/pallas_call | solution.py:66
  8.0 8.4 %convolution_convert_fusion.1 = bf16[512,2560]{1,0:T(8,128)(2,1)} fusion(bf16[512,1280]{1,0:T(8,128)(2,1)} %shard_map.175, bf16[2560,1280]{1,0:T(8,128)(2,1)} %bitcast.95), kind=kOutput, calls=%fused_computation.5 | convolution fusion | flops 3356753920 | bytes 10485760 | tf_op jit(solution)/shard_map/dot_general | solution.py:364
  16.4 6.3 %all-to-all-start = ((bf16[32,16,2560]{2,1,0:T(8,128)(2,1)}), bf16[32,16,2560]{2,1,0:T(8,128)(2,1)S(1)}, u32[]{:S(2)}, u32[]{:S(2)}) async-start(bf16[32,16,2560]{2,1,0:T(8,128)(2,1)} %bitcast.85), calls=%async_computation | async-start | bytes 5242880 | tf_op jit(solution)/shard_map/all_to_all | solution.py:34
  22.8 0.1 reshape.208
  22.9 1.0 reshape.209.waves_ref
  23.9 7.3 %shard_map.177 = bf16[768,1280]{1,0:T(8,128)(2,1)} custom-call(s32[768,1]{1,0:T(8,128)} %reshape.209.waves_ref), custom_call_target="tpu_custom_call" | custom-call | tf_op jit(solution)/shard_map/pallas_call | solution.py:66
  31.2 9.9 %convolution_convert_fusion = bf16[768,2560]{1,0:T(8,128)(2,1)} fusion(bf16[768,1280]{1,0:T(8,128)(2,1)} %shard_map.177, bf16[2560,1280]{1,0:T(8,128)(2,1)} %bitcast.96), kind=kOutput, calls=%fused_computation.4 | convolution fusion | flops 5035130880 | bytes 12451840 | tf_op jit(solution)/shard_map/dot_general | solution.py:364
  41.1 38.3 %all-to-all-done.arrived_ref = bf16[32,16,2560]{2,1,0:T(8,128)(2,1)S(1)} async-done(((bf16[32,16,2560]{2,1,0:T(8,128)(2,1)}), bf16[32,16,2560]{2,1,0:T(8,128)(2,1)S(1)}, u32[]{:S(2)}, u32[]{:S(2)}) %all-to-all-start) | async-done | bytes 2621472 | tf_op jit(solution)/shard_map/all_to_all | solution.py:34
  79.4 8.1 %all-to-all-start.2 = ((bf16[32,24,2560]{2,1,0:T(8,128)(2,1)}), bf16[32,24,2560]{2,1,0:T(8,128)(2,1)}, u32[]{:S(2)}, u32[]{:S(2)}) async-start(bf16[32,24,2560]{2,1,0:T(8,128)(2,1)} %bitcast.83), calls=%async_computation.2 | async-start | bytes 7864320 | tf_op jit(solution)/shard_map/all_to_all | solution.py:34
  87.6 0.8 dynamic_slice.17.waves_ref
  88.3 0.8 dynamic_slice.18.waves_ref
  89.1 0.6 broadcast.123
  89.7 0.7 reduce.6
  90.4 0.1 reshape_squeeze.3
  90.5 0.1 copy.57.weights_ref
  90.6 0.1 fusion.32
  90.8 0.3 convert_reduce_fusion
  91.0 0.1 add_divide_fusion.damping_ref
  91.2 17.6 %shard_map.176 = (bf16[32,16,2560]{2,1,0:T(8,128)(2,1)S(1)}, f32[2,8,640]{2,1,0:T(8,128)S(1)}) custom-call(s32[1]{0:T(128)} %bitcast.base_ref, s32[8]{0:T(128)S(1)} %dynamic_slice.17.waves_ref, bf16[32,16,2560]{2,1,0:T(8,128)(2,1)S(1)} %all-to-all-done.arrived_ref, bf16[80,640,640]{2,1,0:T(8,128)(2,1)} %leg_ref.3, bf16[128,128]{1,0:T(8,128)(2,1)S(1)} %copy-done.4, ...), custom_call_target="tpu_custom_call" | custom-call | tf_op jit(solution)/shard_map/pallas_call | solution.py:232
  108.8 1.5 copy-done.2
  110.3 0.1 reshape.189
  110.4 61.8 %all-to-all-done.2.arrived_ref = bf16[32,24,2560]{2,1,0:T(8,128)(2,1)} async-done(((bf16[32,24,2560]{2,1,0:T(8,128)(2,1)}), bf16[32,24,2560]{2,1,0:T(8,128)(2,1)}, u32[]{:S(2)}, u32[]{:S(2)}) %all-to-all-start.2) | async-done | bytes 3932192 | tf_op jit(solution)/shard_map/all_to_all | solution.py:34
  172.3 25.4 %shard_map.178 = (bf16[32,24,2560]{2,1,0:T(8,128)(2,1)S(1)}, f32[3,8,640]{2,1,0:T(8,128)S(1)}) custom-call(s32[1]{0:T(128)} %bitcast.9.base_ref, s32[12]{0:T(128)S(1)} %dynamic_slice.18.waves_ref, bf16[32,24,2560]{2,1,0:T(8,128)(2,1)} %all-to-all-done.2.arrived_ref, bf16[80,640,640]{2,1,0:T(8,128)(2,1)} %leg_ref.3, bf16[128,128]{1,0:T(8,128)(2,1)S(1)} %copy-done.4, ...), custom_call_target="tpu_custom_call" | custom-call | tf_op jit(solution)/shard_map/pallas_call | solution.py:232
  197.7 1.9 copy-done.1
  199.6 0.1 reshape.190
  199.8 0.8 broadcast_in_dim.89
  200.5 7.3 %all-to-all-start.4 = ((bf16[32,40,80]{2,1,0:T(8,128)(2,1)}), bf16[32,40,80]{2,1,0:T(8,128)(2,1)S(1)}, u32[]{:S(2)}, u32[]{:S(2)}) async-start(bf16[32,40,80]{2,1,0:T(8,128)(2,1)} %bitcast.31), calls=%async_computation.4 | async-start | bytes 655360 | tf_op jit(solution)/shard_map/all_to_all | solution.py:34
  207.9 10.0 %all-to-all-done.4 = bf16[32,40,80]{2,1,0:T(8,128)(2,1)S(1)} async-done(((bf16[32,40,80]{2,1,0:T(8,128)(2,1)}), bf16[32,40,80]{2,1,0:T(8,128)(2,1)S(1)}, u32[]{:S(2)}, u32[]{:S(2)}) %all-to-all-start.4) | async-done | bytes 204832 | tf_op jit(solution)/shard_map/all_to_all | solution.py:34
  218.0 1.7 fusion.36
  219.7 2.0 fusion.2
  221.7 0.3 reshape.194
  222.0 0.6 gather_fusion
  222.6 0.2 fusion.18
  222.9 0.1 fusion.26
  223.0 8.5 %all_to_all.30 = f32[8,2,128]{2,1,0:T(2,128)S(1)} all-to-all(f32[8,2,128]{2,1,0:T(2,128)S(1)} %bitcast.91), channel_id=1, replica_groups=mesh['lev'=4,'wav'=8] {'wav'}, dimensions={0} | all-to-all | bytes 16384 | tf_op jit(solution)/shard_map/all_to_all | solution.py:496
  231.5 62.7 %all_to_all.31 = bf16[32,16,2560]{2,1,0:T(8,128)(2,1)} all-to-all(bf16[32,16,2560]{2,1,0:T(8,128)(2,1)S(1)} %copy-done.3), channel_id=1, replica_groups=mesh['lev'=4,'wav'=8] {'lev','wav'}, dimensions={0} | all-to-all | bytes 5242880 | tf_op jit(solution)/shard_map/all_to_all | solution.py:34
  294.2 6.0 %all-to-all-start.3 = ((bf16[32,24,2560]{2,1,0:T(8,128)(2,1)}), bf16[32,24,2560]{2,1,0:T(8,128)(2,1)}, u32[]{:S(2)}, u32[]{:S(2)}) async-start(bf16[32,24,2560]{2,1,0:T(8,128)(2,1)} %copy-done.1), calls=%async_computation.3 | async-start | bytes 7864320 | tf_op jit(solution)/shard_map/all_to_all | solution.py:34
  300.3 3.1 collective-permute-start
  303.4 1.3 collective-permute-start.1
  304.7 0.7 reduce.7
  305.4 0.1 eq.97
  305.6 0.1 and_reduce_fusion
  305.8 8.5 %collective-permute-done = bf16[11,4,128]{2,1,0:T(4,128)(2,1)S(1)} collective-permute-done((bf16[11,4,128]{2,1,0:T(4,128)(2,1)S(1)}, bf16[11,4,128]{2,1,0:T(4,128)(2,1)S(1)}, u32[]{:S(2)}, u32[]{:S(2)}) %collective-permute-start) | collective-permute-done | bytes 11296 | tf_op jit(solution)/shard_map/ppermute | solution.py:27
  314.2 7.3 %collective-permute-done.1 = bf16[11,4,128]{2,1,0:T(4,128)(2,1)S(1)} collective-permute-done((bf16[11,4,128]{2,1,0:T(4,128)(2,1)S(1)}, bf16[11,4,128]{2,1,0:T(4,128)(2,1)S(1)}, u32[]{:S(2)}, u32[]{:S(2)}) %collective-permute-start.1) | collective-permute-done | bytes 11296 | tf_op jit(solution)/shard_map/ppermute | solution.py:28
  321.5 0.1 fusion.33
  321.7 6.1 %collective-permute-start.2 = (bf16[11,56,4]{2,1,0:T(8,128)(2,1)S(1)}, bf16[11,56,4]{2,1,0:T(8,128)(2,1)S(1)}, u32[]{:S(2)}, u32[]{:S(2)}) collective-permute-start(bf16[11,56,4]{2,1,0:T(8,128)(2,1)S(1)} %get-tuple-element.23), channel_id=1, source_target_pairs={{0,1},{1,2},{2,3},{3,4},{4,5},{5,6},{6,7},{8,9},{9,10},{10,11},{11... | collective-permute-start | bytes 14792 | tf_op jit(solution)/shard_map/ppermute | solution.py:27
  327.8 1.9 collective-permute-start.3
  329.8 56.7 %collective-permute-done.2 = bf16[11,56,4]{2,1,0:T(8,128)(2,1)S(1)} collective-permute-done((bf16[11,56,4]{2,1,0:T(8,128)(2,1)S(1)}, bf16[11,56,4]{2,1,0:T(8,128)(2,1)S(1)}, u32[]{:S(2)}, u32[]{:S(2)}) %collective-permute-start.2) | collective-permute-done | bytes 4960 | tf_op jit(solution)/shard_map/ppermute | solution.py:27
  386.5 2.4 collective-permute-done.3
  388.9 0.3 maximum_convert_fusion
  389.1 0.1 slice_bitcast_fusion.11
  389.2 0.1 slice_bitcast_fusion.6
  389.3 0.1 slice_bitcast_fusion.7
  389.5 0.1 slice_bitcast_fusion.8
  389.6 0.6 fusion.17
  390.2 0.6 fusion.12
  390.8 0.6 fusion.7
  391.3 1.0 fusion.24
  392.3 0.8 convolution_bitcast_fusion
  393.1 6.6 %fusion.35 = f32[2560,1280]{1,0:T(8,128)} fusion(bf16[512,2560]{1,0:T(8,128)(2,1)S(1)} %bitcast.84, bf16[512,1280]{1,0:T(8,128)(2,1)S(1)} %copy-done.7), kind=kOutput, calls=%fused_computation.100 | convolution fusion | flops 3355443200 | bytes 17039360 | tf_op jit(solution)/shard_map/dot_general | solution.py:462
  399.8 13.7 %fusion.1 = bf16[2560,1280]{1,0:T(8,128)(2,1)} fusion(bf16[2560,1280]{1,0:T(8,128)(2,1)} %bitcast.97, f32[2560,1280]{1,0:T(8,128)} %fusion.35, bf16[768,2560]{1,0:T(8,128)(2,1)} %bitcast.11, bf16[768,1280]{1,0:T(8,128)(2,1)S(1)} %copy-done.6, f32[2560]{0:T(1024)S(1)} %mul.235), kind=kOutput, calls=%fused_computation.3 | convolution fusion | flops 5052825600 | bytes 32122880 | tf_op jit(solution)/shard_map/dot_general | solution.py:462
  (70 shorter events, 0.9 us)
Async XLA Ops:
  0.6 222.0 %copy-start = (bf16[1,8,128,128]{3,2,1,0:T(8,128)(2,1)S(1)}, bf16[1,8,128,128]{3,2,1,0:T(8,128)(2,1)}, u32[]{:S(2)}) copy-start(bf16[1,8,128,128]{3,2,1,0:T(8,128)(2,1)} %param.24) | copy-start | bytes 786436
  16.4 63.0 %all-to-all-start = ((bf16[32,16,2560]{2,1,0:T(8,128)(2,1)}), bf16[32,16,2560]{2,1,0:T(8,128)(2,1)S(1)}, u32[]{:S(2)}, u32[]{:S(2)}) async-start(bf16[32,16,2560]{2,1,0:T(8,128)(2,1)} %bitcast.85), calls=%async_computation | async-start | bytes 5242880 | tf_op jit(solution)/shard_map/all_to_all | solution.py:34
  79.4 10.3 %copy-start.15 = (s32[1,64,1]{1,2,0:T(1,128)S(1)}, s32[1,64,1]{1,2,0:T(1,128)}, u32[]{:S(2)}) copy-start(s32[1,64,1]{1,2,0:T(1,128)} %param.25) | copy-start | bytes 772
  79.4 11.1 %copy-start.13 = (f32[128]{0:T(128)S(1)}, f32[128]{0:T(128)}, u32[]{:S(2)}) copy-start(f32[128]{0:T(128)} %param.23) | copy-start | bytes 1540
  79.4 11.2 %copy-start.16 = (s32[1,64]{1,0:T(1,128)S(1)}, s32[1,64]{1,0:T(1,128)}, u32[]{:S(2)}) copy-start(s32[1,64]{1,0:T(1,128)} %param.26) | copy-start | bytes 772
  79.4 11.6 %copy-start.14 = (f32[128]{0:T(128)S(1)}, f32[128]{0:T(128)}, u32[]{:S(2)}) copy-start(f32[128]{0:T(128)} %param.22) | copy-start | bytes 1540
  79.4 11.8 %copy-start.4 = (bf16[128,128]{1,0:T(8,128)(2,1)S(1)}, bf16[128,128]{1,0:T(8,128)(2,1)}, u32[]{:S(2)}) copy-start(bf16[128,128]{1,0:T(8,128)(2,1)} %analysis_ref.3) | copy-start | bytes 98308
  79.4 11.8 %copy-start.5 = (bf16[128,128]{1,0:T(8,128)(2,1)S(1)}, bf16[128,128]{1,0:T(8,128)(2,1)}, u32[]{:S(2)}) copy-start(bf16[128,128]{1,0:T(8,128)(2,1)} %synthesis_ref.3) | copy-start | bytes 98308
  79.4 92.8 %all-to-all-start.2 = ((bf16[32,24,2560]{2,1,0:T(8,128)(2,1)}), bf16[32,24,2560]{2,1,0:T(8,128)(2,1)}, u32[]{:S(2)}, u32[]{:S(2)}) async-start(bf16[32,24,2560]{2,1,0:T(8,128)(2,1)} %bitcast.83), calls=%async_computation.2 | async-start | bytes 7864320 | tf_op jit(solution)/shard_map/all_to_all | solution.py:34
  108.8 1.5 copy-start.2
  197.7 1.9 copy-start.1
  199.6 31.9 %copy-start.3 = (bf16[32,16,2560]{2,1,0:T(8,128)(2,1)S(1)}, bf16[32,16,2560]{2,1,0:T(8,128)(2,1)}, u32[]{:S(2)}) copy-start(bf16[32,16,2560]{2,1,0:T(8,128)(2,1)} %copy-done.2) | copy-start | bytes 7864324
  200.5 17.4 %all-to-all-start.4 = ((bf16[32,40,80]{2,1,0:T(8,128)(2,1)}), bf16[32,40,80]{2,1,0:T(8,128)(2,1)S(1)}, u32[]{:S(2)}, u32[]{:S(2)}) async-start(bf16[32,40,80]{2,1,0:T(8,128)(2,1)} %bitcast.31), calls=%async_computation.4 | async-start | bytes 655360 | tf_op jit(solution)/shard_map/all_to_all | solution.py:34
  294.2 6.0 %copy-start.10 = (s32[48,128]{1,0:T(8,128)S(1)}, s32[48,128]{1,0:T(8,128)}, u32[]{:S(2)}) copy-start(s32[48,128]{1,0:T(8,128)} %param.31) | copy-start | bytes 73732
  294.2 6.0 %copy-start.11 = (f32[48,128]{1,0:T(8,128)S(1)}, f32[48,128]{1,0:T(8,128)}, u32[]{:S(2)}) copy-start(f32[48,128]{1,0:T(8,128)} %param.30) | copy-start | bytes 73732
  294.2 6.0 %copy-start.12 = (f32[48,128]{1,0:T(8,128)S(1)}, f32[48,128]{1,0:T(8,128)}, u32[]{:S(2)}) copy-start(f32[48,128]{1,0:T(8,128)} %param.29) | copy-start | bytes 73732
  294.2 6.1 %copy-start.9 = (f32[8,48,128]{2,1,0:T(8,128)S(1)}, f32[8,48,128]{2,1,0:T(8,128)}, u32[]{:S(2)}) copy-start(f32[8,48,128]{2,1,0:T(8,128)} %param.28) | copy-start | bytes 589828
  294.2 10.5 %copy-start.17 = (s32[1,64]{1,0:T(1,128)S(1)}, s32[1,64]{1,0:T(1,128)}, u32[]{:S(2)}) copy-start(s32[1,64]{1,0:T(1,128)} %param.27) | copy-start | bytes 772
  294.2 11.3 %copy-start.18 = (s32[80]{0:T(128)S(1)}, s32[80]{0:T(128)}, u32[]{:S(2)}) copy-start(s32[80]{0:T(128)} %param.19) | copy-start | bytes 964
  294.2 105.6 %all-to-all-start.3 = ((bf16[32,24,2560]{2,1,0:T(8,128)(2,1)}), bf16[32,24,2560]{2,1,0:T(8,128)(2,1)}, u32[]{:S(2)}, u32[]{:S(2)}) async-start(bf16[32,24,2560]{2,1,0:T(8,128)(2,1)} %copy-done.1), calls=%async_computation.3 | async-start | bytes 7864320 | tf_op jit(solution)/shard_map/all_to_all | solution.py:34
  300.3 13.9 %collective-permute-start = (bf16[11,4,128]{2,1,0:T(4,128)(2,1)S(1)}, bf16[11,4,128]{2,1,0:T(4,128)(2,1)S(1)}, u32[]{:S(2)}, u32[]{:S(2)}) collective-permute-start(bf16[11,4,128]{2,1,0:T(4,128)(2,1)S(1)} %get-tuple-element.25), channel_id=1, source_target_pairs={{0,8},{8,16},{16,24},{1,9},{9,17},{17,25},{2,10},{10,18},{18,26},{... | collective-permute-start | bytes 33800 | tf_op jit(solution)/shard_map/ppermute | solution.py:27
  303.4 18.1 %collective-permute-start.1 = (bf16[11,4,128]{2,1,0:T(4,128)(2,1)S(1)}, bf16[11,4,128]{2,1,0:T(4,128)(2,1)S(1)}, u32[]{:S(2)}, u32[]{:S(2)}) collective-permute-start(bf16[11,4,128]{2,1,0:T(4,128)(2,1)S(1)} %get-tuple-element.26), channel_id=1, source_target_pairs={{8,0},{16,8},{24,16},{9,1},{17,9},{25,17},{10,2},{18,10},{26,18},{... | collective-permute-start | bytes 33800 | tf_op jit(solution)/shard_map/ppermute | solution.py:28
  321.7 64.8 %collective-permute-start.2 = (bf16[11,56,4]{2,1,0:T(8,128)(2,1)S(1)}, bf16[11,56,4]{2,1,0:T(8,128)(2,1)S(1)}, u32[]{:S(2)}, u32[]{:S(2)}) collective-permute-start(bf16[11,56,4]{2,1,0:T(8,128)(2,1)S(1)} %get-tuple-element.23), channel_id=1, source_target_pairs={{0,1},{1,2},{2,3},{3,4},{4,5},{5,6},{6,7},{8,9},{9,10},{10,11},{11... | collective-permute-start | bytes 14792 | tf_op jit(solution)/shard_map/ppermute | solution.py:27
  327.8 61.1 %collective-permute-start.3 = (bf16[11,56,4]{2,1,0:T(8,128)(2,1)S(1)}, bf16[11,56,4]{2,1,0:T(8,128)(2,1)S(1)}, u32[]{:S(2)}, u32[]{:S(2)}) collective-permute-start(bf16[11,56,4]{2,1,0:T(8,128)(2,1)S(1)} %get-tuple-element.24), channel_id=1, source_target_pairs={{1,0},{2,1},{3,2},{4,3},{5,4},{6,5},{7,6},{9,8},{10,9},{11,10},{12... | collective-permute-start | bytes 14792 | tf_op jit(solution)/shard_map/ppermute | solution.py:28
  390.2 3.0 copy-start.7
  390.2 3.0 copy-start.8
  393.1 6.7 %copy-start.6 = (bf16[768,1280]{1,0:T(8,128)(2,1)S(1)}, bf16[768,1280]{1,0:T(8,128)(2,1)}, u32[]{:S(2)}) copy-start(bf16[768,1280]{1,0:T(8,128)(2,1)} %shard_map.177) | copy-start | bytes 5898244

commit v3 on v2

--- a/solution.py
+++ b/solution.py
@@ -12,8 +12,9 @@
 SWEEPS = 4
 CAP = 2
 AXES = ("lev", "wav")
-CHUNKS = (2, 3)
+CHUNKS = (3, 2)
 UNIT = 4
+BLOCK = 1280
 LANES = 128
 
 
@@ -53,6 +54,45 @@
     for tile in range(lon_count // LANES):
         part = cos_low * cos_high[:, tile : tile + 1] - sin_low * sin_high[:, tile : tile + 1]
         table_ref[:, tile * LANES : (tile + 1) * LANES] = part.astype(jnp.bfloat16)
+
+
+def swap(value, axis, bit, place):
+    pairs = [(i, i ^ bit) for i in range(lax.axis_size(axis))]
+    mine = (lax.axis_index(axis) // bit) % 2
+    if place is None:
+        kept = sent = value
+        place = 1
+    else:
+        kept = lax.dynamic_index_in_dim(value, mine, place, keepdims=False)
+        sent = lax.dynamic_index_in_dim(value, 1 - mine, place, keepdims=False)
+    came = lax.ppermute(sent, axis, pairs)
+    first = jnp.where(mine == 0, kept, came)
+    second = jnp.where(mine == 0, came, kept)
+    return jnp.stack([first, second], axis=place)
+
+
+def bits_of(axis):
+    return [1 << i for i in range(lax.axis_size(axis).bit_length() - 1)]
+
+
+def power_of_two(axis):
+    return lax.axis_size(axis) & (lax.axis_size(axis) - 1) == 0
+
+
+def share_flux(value):
+    owners, columns, rows = value.shape
+    groups = lax.axis_size("lev")
+    if not (power_of_two("lev") and power_of_two("wav")):
+        copies = jnp.broadcast_to(value[None], (groups,) + value.shape)
+        return exchange(copies.reshape(groups * owners, columns, rows))
+    for bit in bits_of("lev"):
+        value = swap(value, "lev", bit, None)
+    bits = bits_of("wav")
+    value = value.reshape((2,) * len(bits) + (groups, columns, rows))
+    for index, bit in enumerate(bits):
+        value = swap(value, "wav", bit, len(bits) - 1 - index)
+    value = value.reshape(owners, groups, columns, rows).transpose(1, 0, 2, 3)
+    return value.reshape(groups * owners, columns, rows)
 
 
 def wave_table(waves, valid, unit, lon_count):
@@ -70,6 +110,85 @@
         out_specs=pl.BlockSpec((block, lon_count), lambda i: (i, 0)),
         out_shape=jax.ShapeDtypeStruct((rows, lon_count), jnp.bfloat16),
     )(waves)
+
+
+def fourier_kernel(
+    owners, slots_owner, slots_dev, start, units, waves_ref, rows_ref, fourier_ref, table_ref
+):
+    rows, lon_count = table_ref.shape
+    tile_rows = 4 * UNIT
+
+    @pl.when(pl.program_id(0) == 0)
+    def _():
+        lane = lax.broadcasted_iota(jnp.int32, (tile_rows, LANES), 1)
+        row = lax.broadcasted_iota(jnp.int32, (tile_rows, LANES), 0)
+        half = row // UNIT % 2
+        first = lane == 0
+        scale = math.sqrt(2.0 / lon_count)
+
+        def tile(index, carry):
+            waves = jnp.zeros((tile_rows, LANES), jnp.int32)
+            for part in range(2):
+                group = index * 2 + part
+                device = group // units
+                slot = (device % owners) * slots_owner + (device // owners) * slots_dev
+                slot = slot + start + group % units * UNIT
+                for i in range(UNIT):
+                    here = (row // (2 * UNIT) == part) & (row % UNIT == i)
+                    waves = jnp.where(here, waves_ref[slot + i], waves)
+            steps = waves * lane + half * (lon_count // 4)
+            steps = jnp.where(first, waves * LANES, steps).astype(jnp.float32)
+            steps = steps - lon_count * jnp.round(steps * (1.0 / lon_count))
+            angle = steps * (2.0 * math.pi / lon_count)
+            cosine, sine = jnp.cos(angle), jnp.sin(angle)
+            cos_step = jnp.broadcast_to(cosine[:, :1], cosine.shape)
+            sin_step = jnp.broadcast_to(sine[:, :1], sine.shape)
+            turn = half.astype(jnp.float32)
+            cosine = scale * jnp.where(first, 1.0 - turn, cosine)
+            sine = scale * jnp.where(first, turn, sine)
+            place = pl.ds(pl.multiple_of(index * tile_rows, tile_rows), tile_rows)
+            for column in range(lon_count // LANES):
+                table_ref[place, column * LANES : (column + 1) * LANES] = cosine.astype(
+                    jnp.bfloat16
+                )
+                cosine, sine = (
+                    cosine * cos_step - sine * sin_step,
+                    sine * cos_step + cosine * sin_step,
+                )
+            return carry
+
+        tiles = rows // tile_rows
+        lax.fori_loop(0, tiles, tile, 0, unroll=math.gcd(tiles, 8))
+
+    fourier_ref[...] = lax.dot_general(
+        table_ref[...], rows_ref[...], (((1,), (1,)), ((), ())), preferred_element_type=jnp.float32
+    ).astype(jnp.bfloat16)
+
+
+def fourier_call(waves, rows_flat, owners, devices, slots_owner, slots_dev, start, count):
+    cells, lon_count = rows_flat.shape
+    rows = devices * 2 * count
+    block = math.gcd(cells, BLOCK)
+    body = functools.partial(
+        fourier_kernel, owners, slots_owner, slots_dev, start, count // UNIT
+    )
+    return pl.pallas_call(
+        body,
+        grid_spec=pltpu.PrefetchScalarGridSpec(
+            num_scalar_prefetch=1,
+            grid=(cells // block,),
+            in_specs=[pl.BlockSpec((block, lon_count), lambda i, waves: (i, 0))],
+            out_specs=[
+                pl.BlockSpec((rows, block), lambda i, waves: (0, i)),
+                pl.BlockSpec((rows, lon_count), lambda i, waves: (0, 0)),
+            ],
+        ),
+        out_shape=[
+            pltpu.HBM((rows, cells), jnp.bfloat16),
+            pltpu.HBM((rows, lon_count), jnp.bfloat16),
+        ],
+        compiler_params=pltpu.CompilerParams(vmem_limit_bytes=32 * 1024 * 1024),
+    )(waves, pltpu.with_memory_space_constraint(rows_flat, pltpu.HBM))
 
 
 def segments(length, source, target):
@@ -253,7 +372,7 @@
             ],
         ),
         out_shape=[
-            jax.ShapeDtypeStruct(arrived.shape, jnp.bfloat16),
+            pltpu.HBM(arrived.shape, jnp.bfloat16),
             jax.ShapeDtypeStruct((units, 2 * UNIT, rows_all), jnp.float32),
         ],
         compiler_params=pltpu.CompilerParams(vmem_limit_bytes=48 * 1024 * 1024),
@@ -359,6 +478,11 @@
     all_valid = all_valid.reshape(devices, slots_dev)
 
     def forward(start, count):
+        if fused:
+            fourier, table = fourier_call(
+                wave_of_slot, rows_flat, owners, devices, slots_owner, slots_dev, start, count
+            )
+            return table, fourier.reshape(devices, 2 * count, cells)
         chosen = slice(start, start + count)
         table = wave_table(all_waves[:, chosen], all_valid[:, chosen], unit, lon_count)
         fourier = lax.dot_general(
@@ -442,8 +566,7 @@
     for value in sent:
         returned.append(exchange(value))
     flux_lat = jnp.concatenate(flux_parts, axis=0).transpose(1, 0, 2)
-    flux_copies = jnp.broadcast_to(flux_lat[None], (groups,) + flux_lat.shape)
-    flux_back = exchange(flux_copies.reshape(devices, 2 * slots_dev, lat_dev))
+    flux_back = share_flux(flux_lat)
 
     flux_grid = 0.0
     for (start, count), table in zip(chunks, tables):
@@ -466,7 +589,8 @@
             preferred_element_type=jnp.float32,
         )
         if index + 1 < len(chunks):
-            regridded = lax.optimization_barrier(regridded)
+            regridded = lax.optimization_barrier(regridded.astype(jnp.bfloat16))
+            regridded = regridded.astype(jnp.float32)
     atm_out = regridded * (1.0 + rows_flat.astype(jnp.float32) * latitude)
     atm_out = atm_out.astype(jnp.bfloat16).reshape(lev_dev, lat_dev, lon_count)
 

time: 414 us -> 419 us (1.012)
  waiting for transfers between devices: 185 us -> 258 us
  blocking collectives: 71.2 us -> 11.8 us
  matrix products: 43.6 us -> 22.6 us
  Pallas kernels: 55.7 us -> 66.6 us
  starting transfers between devices: 40.2 us -> 47.4 us
  local copies, waits for them, and re-layouts: 11.3 us -> 4.11 us
    all_to_all x4, waiting for transfers between devices: 110 us -> 188 us  [exchange(): return lax.all_to_all(value, AXES, split_axis=0, concat_axis=0, tiled=True)]
    all_to_all x1 -> x0, blocking collectives: 62.7 us -> none  [exchange(): return lax.all_to_all(value, AXES, split_axis=0, concat_axis=0, tiled=True)]
    dot_general x2 -> x0, matrix products: 18.3 us -> none  [forward(): lax.dot_general(table, rows_flat, (((1,), (1,)), ((), ())), preferred_ele...]
    ppermute x0 -> x5, waiting for transfers between devices: none -> 16.4 us  [swap(): came = lax.ppermute(sent, axis, pairs)]
    ppermute x2, waiting for transfers between devices: 65.2 us -> 51.5 us  [with_halo(): before = lax.ppermute(last, axis, up)]
    ppermute x0 -> x5, starting transfers between devices: none -> 10.5 us  [swap(): came = lax.ppermute(sent, axis, pairs)]
    pallas_call x2, Pallas kernels: 12.7 us -> 22 us  [fourier_call(): pl.pallas_call(body, grid_spec=pltpu.PrefetchScalarGridSpec(num_scalar_pr...]
    ppermute x2, waiting for transfers between devices: 9.62 us -> 2.42 us  [with_halo(): after = lax.ppermute(initial, axis, down)]
  transfers between devices with their start and end apart: 8 -> 13, of which waited for: 7 -> 10; matrix products, arithmetic and copies ran while one was open for 7% -> 5% of each run, Pallas kernels for 6% -> 7%
where the time goes in v3:
time: 419 us; the launch traced here: 418 us
  waiting for transfers between devices  258 us (62%)
  Pallas kernels  66.6 us (16%)
  starting transfers between devices  47.4 us (11%)
  matrix products  22.6 us (5%)
  blocking collectives  11.8 us (3%)
  other arithmetic  6.65 us (2%)
    all_to_all x4, waiting for transfers between devices, exchange(): return lax.all_to_all(value, AXES, split_axis=0, concat_axis=0, tiled=True)  188 us
    ppermute x2, waiting for transfers between devices, with_halo(): before = lax.ppermute(last, axis, up)  51.5 us
    pallas_call x2, Pallas kernels, spectral_call(): pl.pallas_call(body, grid_spec=pltpu.PrefetchScalarGridSpec(num_scalar_pr...  44.7 us
    all_to_all x4, starting transfers between devices, exchange(): return lax.all_to_all(value, AXES, split_axis=0, concat_axis=0, tiled=True)  27 us
    pallas_call x2, Pallas kernels, fourier_call(): pl.pallas_call(body, grid_spec=pltpu.PrefetchScalarGridSpec(num_scalar_pr...  22 us
    dot_general x2, matrix products, per_device(): lax.dot_general(returned[index].reshape(-1, cells), tables[index], (((0,)...  20.6 us
    ppermute x5, waiting for transfers between devices, swap(): came = lax.ppermute(sent, axis, pairs)  16.4 us
    all_to_all x1, blocking collectives, per_device(): lax.all_to_all(outgoing, 'wav', split_axis=0, concat_axis=0, tiled=True)  11.8 us
  transfers between devices with their start and end apart: 13, of which 10 were waited for; matrix products, arithmetic and copies ran while one was open for 5% of the time, Pallas kernels for 7%

profile of v3, /device:TPU:9, one launch (start us, length us, event | category | flops | bytes accessed | tf_op | source)
XLA Modules:
  0.0 418.5 jit_solution(1763286782261739144)
XLA Ops:
  0.7 0.7 copy-done.3
  1.4 9.5 %shard_map.177 = (bf16[512,2560]{1,0:T(8,128)(2,1)}, bf16[512,1280]{1,0:T(8,128)(2,1)}) custom-call(s32[640]{0:T(1024)S(1)} %copy-done.3, bf16[2560,1280]{1,0:T(8,128)(2,1)} %bitcast.131), custom_call_target="tpu_custom_call" | custom-call | tf_op jit(solution)/shard_map/pallas_call | solution.py:175
  10.9 6.3 %all-to-all-start.2 = ((bf16[32,16,2560]{2,1,0:T(8,128)(2,1)}), bf16[32,16,2560]{2,1,0:T(8,128)(2,1)S(1)}, u32[]{:S(2)}, u32[]{:S(2)}) async-start(bf16[32,16,2560]{2,1,0:T(8,128)(2,1)} %bitcast.136), calls=%async_computation.2 | async-start | bytes 5242880 | tf_op jit(solution)/shard_map/all_to_all | solution.py:35
  17.2 12.5 %shard_map.175 = (bf16[768,2560]{1,0:T(8,128)(2,1)}, bf16[768,1280]{1,0:T(8,128)(2,1)}) custom-call(s32[640]{0:T(1024)S(1)} %copy-done.4, bf16[2560,1280]{1,0:T(8,128)(2,1)} %bitcast.132), custom_call_target="tpu_custom_call" | custom-call | tf_op jit(solution)/shard_map/pallas_call | solution.py:175
  29.7 44.2 %all-to-all-done.2.arrived_ref = bf16[32,16,2560]{2,1,0:T(8,128)(2,1)S(1)} async-done(((bf16[32,16,2560]{2,1,0:T(8,128)(2,1)}), bf16[32,16,2560]{2,1,0:T(8,128)(2,1)S(1)}, u32[]{:S(2)}, u32[]{:S(2)}) %all-to-all-start.2) | async-done | bytes 2621472 | tf_op jit(solution)/shard_map/all_to_all | solution.py:35
  73.9 8.1 %all-to-all-start = ((bf16[32,24,2560]{2,1,0:T(8,128)(2,1)}), bf16[32,24,2560]{2,1,0:T(8,128)(2,1)}, u32[]{:S(2)}, u32[]{:S(2)}) async-start(bf16[32,24,2560]{2,1,0:T(8,128)(2,1)} %bitcast.134), calls=%async_computation | async-start | bytes 7864320 | tf_op jit(solution)/shard_map/all_to_all | solution.py:35
  82.1 0.1 dynamic_slice.38.waves_ref
  82.2 0.5 broadcast.118
  82.8 0.6 reduce.6
  83.4 0.1 reshape_squeeze.3
  83.5 0.1 copy.48.weights_ref
  83.6 0.3 convert_reduce_fusion
  83.9 0.1 add_divide_fusion.damping_ref
  84.1 18.5 %shard_map.178 = (bf16[32,16,2560]{2,1,0:T(8,128)(2,1)}, f32[2,8,640]{2,1,0:T(8,128)S(1)}) custom-call(s32[1]{0:T(128)} %bitcast.5.base_ref, s32[8]{0:T(128)S(1)} %dynamic_slice.39.waves_ref, bf16[32,16,2560]{2,1,0:T(8,128)(2,1)S(1)} %all-to-all-done.2.arrived_ref, bf16[80,640,640]{2,1,0:T(8,128)(2,1)} %leg_ref.3, bf16[128,128]{1,0:T(8,128)(2,1)S(1)} %copy-done.1, ...), custom_call_target="tpu_custom_call" | custom-call | tf_op jit(solution)/shard_map/pallas_call | solution.py:351
  102.5 0.1 reshape.158
  102.7 64.1 %all-to-all-done.arrived_ref = bf16[32,24,2560]{2,1,0:T(8,128)(2,1)} async-done(((bf16[32,24,2560]{2,1,0:T(8,128)(2,1)}), bf16[32,24,2560]{2,1,0:T(8,128)(2,1)}, u32[]{:S(2)}, u32[]{:S(2)}) %all-to-all-start) | async-done | bytes 3932192 | tf_op jit(solution)/shard_map/all_to_all | solution.py:35
  166.8 26.2 %shard_map.176 = (bf16[32,24,2560]{2,1,0:T(8,128)(2,1)}, f32[3,8,640]{2,1,0:T(8,128)S(1)}) custom-call(s32[1]{0:T(128)} %bitcast.base_ref, s32[12]{0:T(128)S(1)} %dynamic_slice.38.waves_ref, bf16[32,24,2560]{2,1,0:T(8,128)(2,1)} %all-to-all-done.arrived_ref, bf16[80,640,640]{2,1,0:T(8,128)(2,1)} %leg_ref.3, bf16[128,128]{1,0:T(8,128)(2,1)S(1)} %copy-done.1, ...), custom_call_target="tpu_custom_call" | custom-call | tf_op jit(solution)/shard_map/pallas_call | solution.py:351
  193.0 0.1 reshape.157
  193.1 1.4 collective-permute-start.4
  194.5 2.0 collective-permute-done.4
  196.6 1.4 collective-permute-start.5
  198.1 2.7 collective-permute-done.5
  201.0 2.8 collective-permute-start.6
  203.8 1.0 collective-permute-done.6
  204.8 0.1 fusion.30
  205.0 4.8 %collective-permute-start.7 = (bf16[2,2,4,40,80]{4,3,2,1,0:T(8,128)(2,1)S(1)}, bf16[2,2,4,40,80]{4,3,2,1,0:T(8,128)(2,1)S(1)}, u32[]{:S(2)}, u32[]{:S(2)}) collective-permute-start(bf16[2,2,4,40,80]{4,3,2,1,0:T(8,128)(2,1)S(1)} %bitcast.144), channel_id=1, source_target_pairs={{0,2},{1,3},{2,0},{3,1},{4,6},{5,7},{6,4},{7,5},{8,10},{9,11},{10,... | collective-permute-start | bytes 307208 | tf_op jit(solution)/shard_map/ppermute | solution.py:68
  209.7 0.1 compare_and_fusion.1
  209.8 4.1 collective-permute-done.7
  214.1 6.5 %collective-permute-done.8 = bf16[2,2,4,40,80]{4,3,2,1,0:T(8,128)(2,1)S(1)} collective-permute-done((bf16[2,2,4,40,80]{4,3,2,1,0:T(8,128)(2,1)S(1)}, bf16[2,2,4,40,80]{4,3,2,1,0:T(8,128)(2,1)S(1)}, u32[]{:S(2)}, u32[]{:S(2)}) %collective-permute-start.8) | collective-permute-done | bytes 102432 | tf_op jit(solution)/shard_map/ppermute | solution.py:68
  220.9 0.5 fusion.46
  221.4 0.4 fusion.2
  221.7 0.3 reshape.164
  222.0 0.6 gather_fusion
  222.6 0.1 select_bitcast_fusion.6
  222.6 0.2 fusion.18
  222.9 0.1 fusion.36
  223.0 11.8 %all_to_all.25 = f32[8,2,128]{2,1,0:T(2,128)S(1)} all-to-all(f32[8,2,128]{2,1,0:T(2,128)S(1)} %bitcast.145), channel_id=1, replica_groups=mesh['lev'=4,'wav'=8] {'wav'}, dimensions={0} | all-to-all | bytes 16384 | tf_op jit(solution)/shard_map/all_to_all | solution.py:620
  234.8 5.0 %all-to-all-start.1 = ((bf16[32,24,2560]{2,1,0:T(8,128)(2,1)}), bf16[32,24,2560]{2,1,0:T(8,128)(2,1)}, u32[]{:S(2)}, u32[]{:S(2)}) async-start(bf16[32,24,2560]{2,1,0:T(8,128)(2,1)} %get-tuple-element.12), calls=%async_computation.1 | async-start | bytes 7864320 | tf_op jit(solution)/shard_map/all_to_all | solution.py:35
  240.0 3.1 collective-permute-start
  243.1 1.3 collective-permute-start.1
  244.4 0.6 reduce.7
  245.1 0.1 eq.123
  245.1 79.4 %all-to-all-done.1 = bf16[32,24,2560]{2,1,0:T(8,128)(2,1)} async-done(((bf16[32,24,2560]{2,1,0:T(8,128)(2,1)}), bf16[32,24,2560]{2,1,0:T(8,128)(2,1)}, u32[]{:S(2)}, u32[]{:S(2)}) %all-to-all-start.1) | async-done | bytes 3932192 | tf_op jit(solution)/shard_map/all_to_all | solution.py:35
  324.6 7.5 %all-to-all-start.3 = ((bf16[32,16,2560]{2,1,0:T(8,128)(2,1)}), bf16[32,16,2560]{2,1,0:T(8,128)(2,1)S(1)}, u32[]{:S(2)}, u32[]{:S(2)}) async-start(bf16[32,16,2560]{2,1,0:T(8,128)(2,1)} %get-tuple-element.15), calls=%async_computation.3 | async-start | bytes 5242880 | tf_op jit(solution)/shard_map/all_to_all | solution.py:35
  332.1 0.1 iota_compare_fusion
  332.2 0.1 and_reduce_fusion
  332.4 0.1 fusion.44
  332.5 3.4 collective-permute-start.2
  336.0 2.1 collective-permute-start.3
  338.1 0.7 mul.235
  338.8 51.5 %collective-permute-done.2 = bf16[11,56,4]{2,1,0:T(8,128)(2,1)S(1)} collective-permute-done((bf16[11,56,4]{2,1,0:T(8,128)(2,1)S(1)}, bf16[11,56,4]{2,1,0:T(8,128)(2,1)S(1)}, u32[]{:S(2)}, u32[]{:S(2)}) %collective-permute-start.2) | collective-permute-done | bytes 4960 | tf_op jit(solution)/shard_map/ppermute | solution.py:28
  390.3 2.4 collective-permute-done.3
  392.7 1.2 maximum_convert_fusion
  393.9 0.1 slice_bitcast_fusion.11
  394.0 0.1 slice_bitcast_fusion.6
  394.1 0.1 slice_bitcast_fusion.7
  394.2 0.1 slice_bitcast_fusion.8
  394.4 0.6 fusion.17
  394.9 0.6 fusion.12
  395.5 0.6 fusion.7
  396.1 1.0 fusion.24
  397.1 0.8 convolution_bitcast_fusion
  397.9 10.4 %convolution_convert_fusion = bf16[2560,1280]{1,0:T(8,128)(2,1)} fusion(bf16[768,2560]{1,0:T(8,128)(2,1)} %bitcast.4, bf16[768,1280]{1,0:T(8,128)(2,1)S(1)} %copy-done.6), kind=kOutput, calls=%fused_computation.4 | convolution fusion | flops 5036441600 | bytes 12451840 | tf_op jit(solution)/shard_map/dot_general | solution.py:585
  408.3 10.2 %fusion.1 = bf16[2560,1280]{1,0:T(8,128)(2,1)} fusion(bf16[2560,1280]{1,0:T(8,128)(2,1)} %bitcast.133, bf16[512,2560]{1,0:T(8,128)(2,1)S(1)} %bitcast.135, bf16[512,1280]{1,0:T(8,128)(2,1)} %get-tuple-element.16, bf16[2560,1280]{1,0:T(8,128)(2,1)} %convolution_convert_fusion, f32[2560]{0:T(1024)S(1)} %copy-done.12), kind=kOutput, calls=%fused_computation.3 | convolution fusion | flops 3378380800 | bytes 23603200 | tf_op jit(solution)/shard_map/dot_general | solution.py:585
  (77 shorter events, 1.1 us)
Async XLA Ops:
  0.6 222.0 %copy-start = (bf16[1,8,128,128]{3,2,1,0:T(8,128)(2,1)S(1)}, bf16[1,8,128,128]{3,2,1,0:T(8,128)(2,1)}, u32[]{:S(2)}) copy-start(bf16[1,8,128,128]{3,2,1,0:T(8,128)(2,1)} %param.24) | copy-start | bytes 786436
  0.6 0.7 copy-start.3
  10.9 6.3 %copy-start.4 = (s32[640]{0:T(1024)S(1)}, s32[640]{0:T(1024)}, u32[]{:S(2)}) copy-start(s32[640]{0:T(1024)} %waves_ref.3) | copy-start | bytes 7684
  10.9 63.0 %all-to-all-start.2 = ((bf16[32,16,2560]{2,1,0:T(8,128)(2,1)}), bf16[32,16,2560]{2,1,0:T(8,128)(2,1)S(1)}, u32[]{:S(2)}, u32[]{:S(2)}) async-start(bf16[32,16,2560]{2,1,0:T(8,128)(2,1)} %bitcast.136), calls=%async_computation.2 | async-start | bytes 5242880 | tf_op jit(solution)/shard_map/all_to_all | solution.py:35
  73.9 8.9 %copy-start.15 = (s32[1,64,1]{1,2,0:T(1,128)S(1)}, s32[1,64,1]{1,2,0:T(1,128)}, u32[]{:S(2)}) copy-start(s32[1,64,1]{1,2,0:T(1,128)} %param.25) | copy-start | bytes 772
  73.9 9.6 %copy-start.13 = (f32[128]{0:T(128)S(1)}, f32[128]{0:T(128)}, u32[]{:S(2)}) copy-start(f32[128]{0:T(128)} %param.23) | copy-start | bytes 1540
  73.9 10.0 %copy-start.14 = (f32[128]{0:T(128)S(1)}, f32[128]{0:T(128)}, u32[]{:S(2)}) copy-start(f32[128]{0:T(128)} %param.22) | copy-start | bytes 1540
  73.9 10.1 %copy-start.1 = (bf16[128,128]{1,0:T(8,128)(2,1)S(1)}, bf16[128,128]{1,0:T(8,128)(2,1)}, u32[]{:S(2)}) copy-start(bf16[128,128]{1,0:T(8,128)(2,1)} %analysis_ref.3) | copy-start | bytes 98308
  73.9 10.1 %copy-start.2 = (bf16[128,128]{1,0:T(8,128)(2,1)S(1)}, bf16[128,128]{1,0:T(8,128)(2,1)}, u32[]{:S(2)}) copy-start(bf16[128,128]{1,0:T(8,128)(2,1)} %synthesis_ref.3) | copy-start | bytes 98308
  73.9 92.8 %all-to-all-start = ((bf16[32,24,2560]{2,1,0:T(8,128)(2,1)}), bf16[32,24,2560]{2,1,0:T(8,128)(2,1)}, u32[]{:S(2)}, u32[]{:S(2)}) async-start(bf16[32,24,2560]{2,1,0:T(8,128)(2,1)} %bitcast.134), calls=%async_computation | async-start | bytes 7864320 | tf_op jit(solution)/shard_map/all_to_all | solution.py:35
  166.8 31.2 %copy-start.16 = (s32[1,64]{1,0:T(1,128)S(1)}, s32[1,64]{1,0:T(1,128)}, u32[]{:S(2)}) copy-start(s32[1,64]{1,0:T(1,128)} %param.26) | copy-start | bytes 772
  193.1 3.4 collective-permute-start.4
  194.5 26.3 %copy-start.5 = (bf16[768,1280]{1,0:T(8,128)(2,1)S(1)}, bf16[768,1280]{1,0:T(8,128)(2,1)}, u32[]{:S(2)}) copy-start(bf16[768,1280]{1,0:T(8,128)(2,1)} %get-tuple-element.13) | copy-start | bytes 5898244
  196.6 4.2 %collective-permute-start.5 = (bf16[8,2,40,80]{3,2,1,0:T(8,128)(2,1)S(1)}, bf16[8,2,40,80]{3,2,1,0:T(8,128)(2,1)S(1)}, u32[]{:S(2)}, u32[]{:S(2)}) collective-permute-start(bf16[8,2,40,80]{3,2,1,0:T(8,128)(2,1)S(1)} %pad_maximum_fusion.2), channel_id=1, source_target_pairs={{0,16},{8,24},{16,0},{24,8},{1,17},{9,25},{17,1},{25,9},{2,18},{10... | collective-permute-start | bytes 307208 | tf_op jit(solution)/shard_map/ppermute | solution.py:68
  201.0 3.8 collective-permute-start.6
  203.8 17.6 %copy-start.7 = (bf16[512,1280]{1,0:T(8,128)(2,1)S(1)}, bf16[512,1280]{1,0:T(8,128)(2,1)}, u32[]{:S(2)}) copy-start(bf16[512,1280]{1,0:T(8,128)(2,1)} %get-tuple-element.16) | copy-start | bytes 3932164
  205.0 9.0 %collective-permute-start.7 = (bf16[2,2,4,40,80]{4,3,2,1,0:T(8,128)(2,1)S(1)}, bf16[2,2,4,40,80]{4,3,2,1,0:T(8,128)(2,1)S(1)}, u32[]{:S(2)}, u32[]{:S(2)}) collective-permute-start(bf16[2,2,4,40,80]{4,3,2,1,0:T(8,128)(2,1)S(1)} %bitcast.144), channel_id=1, source_target_pairs={{0,2},{1,3},{2,0},{3,1},{4,6},{5,7},{6,4},{7,5},{8,10},{9,11},{10,... | collective-permute-start | bytes 307208 | tf_op jit(solution)/shard_map/ppermute | solution.py:68
  214.0 6.6 %collective-permute-start.8 = (bf16[2,2,4,40,80]{4,3,2,1,0:T(8,128)(2,1)S(1)}, bf16[2,2,4,40,80]{4,3,2,1,0:T(8,128)(2,1)S(1)}, u32[]{:S(2)}, u32[]{:S(2)}) collective-permute-start(bf16[2,2,4,40,80]{4,3,2,1,0:T(8,128)(2,1)S(1)} %fusion.26), channel_id=1, source_target_pairs={{0,4},{1,5},{2,6},{3,7},{4,0},{5,1},{6,2},{7,3},{8,12},{9,13},{10,... | collective-permute-start | bytes 307208 | tf_op jit(solution)/shard_map/ppermute | solution.py:68
  234.8 5.1 %copy-start.9 = (s32[48,128]{1,0:T(8,128)S(1)}, s32[48,128]{1,0:T(8,128)}, u32[]{:S(2)}) copy-start(s32[48,128]{1,0:T(8,128)} %param.31) | copy-start | bytes 73732
  234.8 5.1 %copy-start.10 = (f32[48,128]{1,0:T(8,128)S(1)}, f32[48,128]{1,0:T(8,128)}, u32[]{:S(2)}) copy-start(f32[48,128]{1,0:T(8,128)} %param.30) | copy-start | bytes 73732
  234.8 5.1 %copy-start.11 = (f32[48,128]{1,0:T(8,128)S(1)}, f32[48,128]{1,0:T(8,128)}, u32[]{:S(2)}) copy-start(f32[48,128]{1,0:T(8,128)} %param.29) | copy-start | bytes 73732
  234.8 5.1 %copy-start.8 = (f32[8,48,128]{2,1,0:T(8,128)S(1)}, f32[8,48,128]{2,1,0:T(8,128)}, u32[]{:S(2)}) copy-start(f32[8,48,128]{2,1,0:T(8,128)} %param.28) | copy-start | bytes 589828
  234.8 9.6 %copy-start.17 = (s32[1,64]{1,0:T(1,128)S(1)}, s32[1,64]{1,0:T(1,128)}, u32[]{:S(2)}) copy-start(s32[1,64]{1,0:T(1,128)} %param.27) | copy-start | bytes 772
  234.8 89.8 %all-to-all-start.1 = ((bf16[32,24,2560]{2,1,0:T(8,128)(2,1)}), bf16[32,24,2560]{2,1,0:T(8,128)(2,1)}, u32[]{:S(2)}, u32[]{:S(2)}) async-start(bf16[32,24,2560]{2,1,0:T(8,128)(2,1)} %get-tuple-element.12), calls=%async_computation.1 | async-start | bytes 7864320 | tf_op jit(solution)/shard_map/all_to_all | solution.py:35
  239.9 92.2 %copy-start.18 = (s32[80]{0:T(128)S(1)}, s32[80]{0:T(128)}, u32[]{:S(2)}) copy-start(s32[80]{0:T(128)} %param.19) | copy-start | bytes 964
  240.0 92.3 %collective-permute-start = (bf16[11,4,128]{2,1,0:T(4,128)(2,1)S(1)}, bf16[11,4,128]{2,1,0:T(4,128)(2,1)S(1)}, u32[]{:S(2)}, u32[]{:S(2)}) collective-permute-start(bf16[11,4,128]{2,1,0:T(4,128)(2,1)S(1)} %get-tuple-element.45), channel_id=1, source_target_pairs={{0,8},{8,16},{16,24},{1,9},{9,17},{17,25},{2,10},{10,18},{18,26},{... | collective-permute-start | bytes 33800 | tf_op jit(solution)/shard_map/ppermute | solution.py:28
  243.1 89.2 %collective-permute-start.1 = (bf16[11,4,128]{2,1,0:T(4,128)(2,1)S(1)}, bf16[11,4,128]{2,1,0:T(4,128)(2,1)S(1)}, u32[]{:S(2)}, u32[]{:S(2)}) collective-permute-start(bf16[11,4,128]{2,1,0:T(4,128)(2,1)S(1)} %get-tuple-element.46), channel_id=1, source_target_pairs={{8,0},{16,8},{24,16},{9,1},{17,9},{25,17},{10,2},{18,10},{26,18},{... | collective-permute-start | bytes 33800 | tf_op jit(solution)/shard_map/ppermute | solution.py:29
  324.6 83.7 %all-to-all-start.3 = ((bf16[32,16,2560]{2,1,0:T(8,128)(2,1)}), bf16[32,16,2560]{2,1,0:T(8,128)(2,1)S(1)}, u32[]{:S(2)}, u32[]{:S(2)}) async-start(bf16[32,16,2560]{2,1,0:T(8,128)(2,1)} %get-tuple-element.15), calls=%async_computation.3 | async-start | bytes 5242880 | tf_op jit(solution)/shard_map/all_to_all | solution.py:35
  332.5 57.8 %collective-permute-start.2 = (bf16[11,56,4]{2,1,0:T(8,128)(2,1)S(1)}, bf16[11,56,4]{2,1,0:T(8,128)(2,1)S(1)}, u32[]{:S(2)}, u32[]{:S(2)}) collective-permute-start(bf16[11,56,4]{2,1,0:T(8,128)(2,1)S(1)} %get-tuple-element.43), channel_id=1, source_target_pairs={{0,1},{1,2},{2,3},{3,4},{4,5},{5,6},{6,7},{8,9},{9,10},{10,11},{11... | collective-permute-start | bytes 14792 | tf_op jit(solution)/shard_map/ppermute | solution.py:28
  336.0 56.7 %collective-permute-start.3 = (bf16[11,56,4]{2,1,0:T(8,128)(2,1)S(1)}, bf16[11,56,4]{2,1,0:T(8,128)(2,1)}, u32[]{:S(2)}, u32[]{:S(2)}) collective-permute-start(bf16[11,56,4]{2,1,0:T(8,128)(2,1)S(1)} %get-tuple-element.44), channel_id=1, source_target_pairs={{1,0},{2,1},{3,2},{4,3},{5,4},{6,5},{7,6},{9,8},{10,9},{11,10},{12... | collective-permute-start | bytes 14792 | tf_op jit(solution)/shard_map/ppermute | solution.py:29
  394.9 3.0 copy-start.6
  397.9 10.4 %copy-start.12 = (f32[2560]{0:T(1024)S(1)}, f32[2560]{0:T(1024)}, u32[]{:S(2)}) copy-start(f32[2560]{0:T(1024)} %mul.235) | copy-start | bytes 30724

commit v4 on v3

--- a/solution.py
+++ b/solution.py
@@ -93,6 +93,17 @@
         value = swap(value, "wav", bit, len(bits) - 1 - index)
     value = value.reshape(owners, groups, columns, rows).transpose(1, 0, 2, 3)
     return value.reshape(groups * owners, columns, rows)
+
+
+def share_pairs(value):
+    if not power_of_two("wav"):
+        return lax.all_to_all(value, "wav", split_axis=0, concat_axis=0, tiled=True)
+    bits = bits_of("wav")
+    shape = value.shape
+    value = value.reshape((2,) * len(bits) + shape[1:])
+    for index, bit in enumerate(bits):
+        value = swap(value, "wav", bit, len(bits) - 1 - index)
+    return value.reshape(shape)
 
 
 def wave_table(waves, valid, unit, lon_count):
@@ -189,6 +200,47 @@
         ],
         compiler_params=pltpu.CompilerParams(vmem_limit_bytes=32 * 1024 * 1024),
     )(waves, pltpu.with_memory_space_constraint(rows_flat, pltpu.HBM))
+
+
+def final_kernel(lat_dev, returned_ref, table_ref, partial_ref, rows_ref, latitude_ref, out_ref):
+    total = partial_ref[...].astype(jnp.float32) + lax.dot_general(
+        returned_ref[...],
+        table_ref[...],
+        (((0,), (0,)), ((), ())),
+        preferred_element_type=jnp.float32,
+    )
+    shape = (out_ref.shape[0] // lat_dev, lat_dev, out_ref.shape[1])
+    field = rows_ref[...].astype(jnp.float32).reshape(shape)
+    total = total.reshape(shape) * (1.0 + field * latitude_ref[...][None])
+    out_ref[...] = total.reshape(out_ref.shape).astype(jnp.bfloat16)
+
+
+def final_call(returned, table, partial, rows_flat, latitude):
+    cells, lon_count = rows_flat.shape
+    lat_dev = latitude.shape[0]
+    columns = returned.shape[0]
+    block = lat_dev * 16
+    rows = pl.BlockSpec((block, lon_count), lambda i: (i, 0))
+    return pl.pallas_call(
+        functools.partial(final_kernel, lat_dev),
+        grid=(cells // block,),
+        in_specs=[
+            pl.BlockSpec((columns, block), lambda i: (0, i)),
+            pl.BlockSpec((columns, lon_count), lambda i: (0, 0)),
+            rows,
+            rows,
+            pl.BlockSpec((lat_dev, 1), lambda i: (0, 0)),
+        ],
+        out_specs=rows,
+        out_shape=pltpu.HBM((cells, lon_count), jnp.bfloat16),
+        compiler_params=pltpu.CompilerParams(vmem_limit_bytes=32 * 1024 * 1024),
+    )(
+        pltpu.with_memory_space_constraint(returned, pltpu.HBM),
+        table,
+        pltpu.with_memory_space_constraint(partial, pltpu.HBM),
+        pltpu.with_memory_space_constraint(rows_flat, pltpu.HBM),
+        latitude[:, None],
+    )
 
 
 def segments(length, source, target):
@@ -466,6 +518,8 @@
         and cells % LANES == 0
         and owners * lat_dev % LANES == 0
         and groups * lev_dev % 8 == 0
+        and lev_dev % 16 == 0
+        and lat_dev % 16 == 0
     )
     unit = UNIT if fused else slots_dev
     chunks = split_slots(slots_dev, unit)
@@ -579,19 +633,23 @@
     latitude = jnp.sin(
         math.pi * (lat_of_row.astype(jnp.float32) + 0.5) / (lat_dev * owners) - math.pi / 2
     )
-    latitude = jnp.broadcast_to(latitude[None], (lev_dev, lat_dev)).reshape(cells, 1)
     regridded = 0.0
-    for index in range(len(chunks)):
+    for index in range(len(chunks) - fused):
         regridded += lax.dot_general(
             returned[index].reshape(-1, cells),
             tables[index],
             (((0,), (0,)), ((), ())),
             preferred_element_type=jnp.float32,
         )
-        if index + 1 < len(chunks):
-            regridded = lax.optimization_barrier(regridded.astype(jnp.bfloat16))
-            regridded = regridded.astype(jnp.float32)
-    atm_out = regridded * (1.0 + rows_flat.astype(jnp.float32) * latitude)
+    if fused:
+        regridded = jnp.broadcast_to(regridded, rows_flat.shape).astype(jnp.bfloat16)
+        regridded = lax.optimization_barrier(regridded)
+        atm_out = final_call(
+            returned[-1].reshape(-1, cells), tables[-1], regridded, rows_flat, latitude
+        )
+    else:
+        latitude = jnp.broadcast_to(latitude[None], (lev_dev, lat_dev)).reshape(cells, 1)
+        atm_out = regridded * (1.0 + rows_flat.astype(jnp.float32) * latitude)
     atm_out = atm_out.astype(jnp.bfloat16).reshape(lev_dev, lat_dev, lon_count)
 
     ocean_now = ocean(ocean_temp, diffusivity, surface_heat, land_mask)
@@ -617,7 +675,7 @@
         preferred_element_type=jnp.float32,
     )
     outgoing = outgoing.reshape(owners, CAP, ocean_cols)
-    incoming = lax.all_to_all(outgoing, "wav", split_axis=0, concat_axis=0, tiled=True)
+    incoming = share_pairs(outgoing)
     mine = (all_dest == my_owner)[:, None, :] & (
         rank[:, None, :] == jnp.arange(CAP, dtype=jnp.int32)[None, :, None]
     )

time: 419 us -> 402 us (0.959)
  the two profiles are of different devices: /device:TPU:9 before, /device:TPU:0 now
where the time goes in v4:
time: 402 us; the launch traced here: 401 us
  waiting for transfers between devices  191 us (48%)
  starting transfers between devices  95.1 us (24%)
  Pallas kernels  76.2 us (19%)
  other arithmetic  15.5 us (4%)
  matrix products  14.2 us (4%)
  local copies, waits for them, and re-layouts  7.63 us (2%)
    all_to_all x4, waiting for transfers between devices, exchange(): return lax.all_to_all(value, AXES, split_axis=0, concat_axis=0, tiled=True)  115 us
    ppermute x8, waiting for transfers between devices, swap(): came = lax.ppermute(sent, axis, pairs)  67.7 us
    ppermute x8, starting transfers between devices, swap(): came = lax.ppermute(sent, axis, pairs)  67.4 us
    pallas_call x2, Pallas kernels, spectral_call(): pl.pallas_call(body, grid_spec=pltpu.PrefetchScalarGridSpec(num_scalar_pr...  44.6 us
    pallas_call x2, Pallas kernels, fourier_call(): pl.pallas_call(body, grid_spec=pltpu.PrefetchScalarGridSpec(num_scalar_pr...  22 us
    all_to_all x4, starting transfers between devices, exchange(): return lax.all_to_all(value, AXES, split_axis=0, concat_axis=0, tiled=True)  19.1 us
    dot_general x1, matrix products, per_device(): lax.dot_general(returned[index].reshape(-1, cells), tables[index], (((0,)...  10.5 us
    pallas_call x1, Pallas kernels, final_call(): pl.pallas_call(functools.partial(final_kernel, lat_dev), grid=(cells // b...  9.59 us
  transfers between devices with their start and end apart: 16, of which 13 were waited for; matrix products, arithmetic and copies ran while one was open for 9% of the time, Pallas kernels for 13%

profile of v4, /device:TPU:0, one launch (start us, length us, event | category | flops | bytes accessed | tf_op | source)
XLA Modules:
  0.0 401.3 jit_solution(2706767274500670653)
XLA Ops:
  0.7 0.7 copy-done.4
  1.4 12.5 %shard_map.177 = (bf16[768,2560]{1,0:T(8,128)(2,1)}, bf16[768,1280]{1,0:T(8,128)(2,1)}) custom-call(s32[640]{0:T(1024)S(1)} %copy-done.4, bf16[2560,1280]{1,0:T(8,128)(2,1)} %bitcast.170), custom_call_target="tpu_custom_call" | custom-call | tf_op jit(solution)/shard_map/pallas_call | solution.py:186
  13.9 7.4 %all-to-all-start.2 = ((bf16[32,24,2560]{2,1,0:T(8,128)(2,1)}), bf16[32,24,2560]{2,1,0:T(8,128)(2,1)}, u32[]{:S(2)}, u32[]{:S(2)}) async-start(bf16[32,24,2560]{2,1,0:T(8,128)(2,1)} %bitcast.174), calls=%async_computation.2 | async-start | bytes 7864320 | tf_op jit(solution)/shard_map/all_to_all | solution.py:35
  21.3 9.5 %shard_map.175 = (bf16[512,2560]{1,0:T(8,128)(2,1)}, bf16[512,1280]{1,0:T(8,128)(2,1)}) custom-call(s32[640]{0:T(1024)S(1)} %copy-done.5, bf16[2560,1280]{1,0:T(8,128)(2,1)} %bitcast.171), custom_call_target="tpu_custom_call" | custom-call | tf_op jit(solution)/shard_map/pallas_call | solution.py:186
  30.8 79.8 %all-to-all-done.2.arrived_ref = bf16[32,24,2560]{2,1,0:T(8,128)(2,1)} async-done(((bf16[32,24,2560]{2,1,0:T(8,128)(2,1)}), bf16[32,24,2560]{2,1,0:T(8,128)(2,1)}, u32[]{:S(2)}, u32[]{:S(2)}) %all-to-all-start.2) | async-done | bytes 3932192 | tf_op jit(solution)/shard_map/all_to_all | solution.py:35
  110.7 2.9 all-to-all-start
  113.9 26.2 %shard_map.178 = (bf16[32,24,2560]{2,1,0:T(8,128)(2,1)}, f32[3,8,640]{2,1,0:T(8,128)S(1)}) custom-call(s32[1]{0:T(128)} %bitcast.5.base_ref, s32[12]{0:T(128)S(1)} %dynamic_slice.60.waves_ref, bf16[32,24,2560]{2,1,0:T(8,128)(2,1)} %all-to-all-done.2.arrived_ref, bf16[80,640,640]{2,1,0:T(8,128)(2,1)} %leg_ref.3, bf16[128,128]{1,0:T(8,128)(2,1)S(1)} %copy-done.2, ...), custom_call_target="tpu_custom_call" | custom-call | tf_op jit(solution)/shard_map/pallas_call | solution.py:403
  140.1 34.8 %all-to-all-done.arrived_ref = bf16[32,16,2560]{2,1,0:T(8,128)(2,1)S(1)} async-done(((bf16[32,16,2560]{2,1,0:T(8,128)(2,1)}), bf16[32,16,2560]{2,1,0:T(8,128)(2,1)S(1)}, u32[]{:S(2)}, u32[]{:S(2)}) %all-to-all-start) | async-done | bytes 2621472 | tf_op jit(solution)/shard_map/all_to_all | solution.py:35
  174.9 3.7 all-to-all-start.3
  178.7 1.0 multiply_convert_fusion
  179.6 0.6 pad_maximum_fusion.7
  180.2 4.1 %collective-permute-start = (bf16[11,4,128]{2,1,0:T(4,128)(2,1)}, bf16[11,4,128]{2,1,0:T(4,128)(2,1)}, u32[]{:S(2)}, u32[]{:S(2)}) collective-permute-start(bf16[11,4,128]{2,1,0:T(4,128)(2,1)} %get-tuple-element.45), channel_id=1, source_target_pairs={{0,8},{8,16},{16,24},{1,9},{9,17},{17,25},{2,10},{10,18},{18,26},{... | collective-permute-start | bytes 33800 | tf_op jit(solution)/shard_map/ppermute | solution.py:28
  184.3 1.3 collective-permute-start.1
  185.6 0.5 broadcast.117
  186.1 1.3 reduce.7
  187.4 1.3 reduce.6
  188.8 0.5 compare_convert_fusion
  189.4 0.7 fusion.48
  190.1 1.3 compare_and_fusion.1
  191.4 0.6 pad_clamp_fusion
  192.0 0.3 convert_reduce_fusion
  192.5 1.3 sine_bitcast_fusion
  193.8 0.5 fusion.49
  194.3 5.1 %collective-permute-done = bf16[11,4,128]{2,1,0:T(4,128)(2,1)} collective-permute-done((bf16[11,4,128]{2,1,0:T(4,128)(2,1)}, bf16[11,4,128]{2,1,0:T(4,128)(2,1)}, u32[]{:S(2)}, u32[]{:S(2)}) %collective-permute-start) | collective-permute-done | bytes 11296 | tf_op jit(solution)/shard_map/ppermute | solution.py:28
  199.5 3.3 collective-permute-done.1
  202.7 0.8 pad_maximum_fusion.3
  203.5 0.8 fusion.50
  204.3 2.0 collective-permute-start.2
  206.3 1.3 collective-permute-start.3
  207.8 0.6 reshape.152
  208.4 0.8 copy.40.latitude_ref
  209.2 0.7 collective-permute-done.3
  209.9 2.2 maximum_convert_fusion
  212.1 18.5 %shard_map.176 = (bf16[32,16,2560]{2,1,0:T(8,128)(2,1)}, f32[2,8,640]{2,1,0:T(8,128)S(1)}) custom-call(s32[1]{0:T(128)} %bitcast.base_ref, s32[8]{0:T(128)S(1)} %dynamic_slice.59.waves_ref, bf16[32,16,2560]{2,1,0:T(8,128)(2,1)S(1)} %all-to-all-done.arrived_ref, bf16[80,640,640]{2,1,0:T(8,128)(2,1)} %leg_ref.3, bf16[128,128]{1,0:T(8,128)(2,1)S(1)} %copy-done.2, ...), custom_call_target="tpu_custom_call" | custom-call | tf_op jit(solution)/shard_map/pallas_call | solution.py:403
  230.8 1.1 collective-permute-start.4
  232.0 1.0 slice_bitcast_fusion.6
  233.0 5.0 %collective-permute-done.4 = bf16[8,40,80]{2,1,0:T(8,128)(2,1)S(1)} collective-permute-done((bf16[8,40,80]{2,1,0:T(8,128)(2,1)S(1)}, bf16[8,40,80]{2,1,0:T(8,128)(2,1)S(1)}, u32[]{:S(2)}, u32[]{:S(2)}) %collective-permute-start.4) | collective-permute-done | bytes 51232 | tf_op jit(solution)/shard_map/ppermute | solution.py:68
  238.1 1.5 collective-permute-start.5
  239.6 0.6 fusion.15
  240.2 3.3 collective-permute-done.5
  243.6 29.8 %collective-permute-start.6 = (bf16[2,2,4,40,80]{4,3,2,1,0:T(8,128)(2,1)S(1)}, bf16[2,2,4,40,80]{4,3,2,1,0:T(8,128)(2,1)S(1)}, u32[]{:S(2)}, u32[]{:S(2)}) collective-permute-start(bf16[2,2,4,40,80]{4,3,2,1,0:T(8,128)(2,1)S(1)} %dynamic-slice_bitcast_fusion), channel_id=1, source_target_pairs={{0,1},{1,0},{2,3},{3,2},{4,5},{5,4},{6,7},{7,6},{8,9},{9,8},{10,11... | collective-permute-start | bytes 307208 | tf_op jit(solution)/shard_map/ppermute | solution.py:68
  273.5 0.9 collective-permute-done.6
  274.6 24.6 %collective-permute-start.7 = (bf16[2,2,4,40,80]{4,3,2,1,0:T(8,128)(2,1)S(1)}, bf16[2,2,4,40,80]{4,3,2,1,0:T(8,128)(2,1)S(1)}, u32[]{:S(2)}, u32[]{:S(2)}) collective-permute-start(bf16[2,2,4,40,80]{4,3,2,1,0:T(8,128)(2,1)S(1)} %bitcast.183), channel_id=1, source_target_pairs={{0,2},{1,3},{2,0},{3,1},{4,6},{5,7},{6,4},{7,5},{8,10},{9,11},{10,... | collective-permute-start | bytes 307208 | tf_op jit(solution)/shard_map/ppermute | solution.py:68
  299.2 0.6 fusion.10
  299.8 4.2 %collective-permute-done.7 = bf16[2,2,4,40,80]{4,3,2,1,0:T(8,128)(2,1)S(1)} collective-permute-done((bf16[2,2,4,40,80]{4,3,2,1,0:T(8,128)(2,1)S(1)}, bf16[2,2,4,40,80]{4,3,2,1,0:T(8,128)(2,1)S(1)}, u32[]{:S(2)}, u32[]{:S(2)}) %collective-permute-start.7) | collective-permute-done | bytes 102432 | tf_op jit(solution)/shard_map/ppermute | solution.py:68
  304.0 3.7 collective-permute-start.8
  307.7 0.7 slice_bitcast_fusion.8
  308.5 6.4 %collective-permute-done.8 = bf16[2,2,4,40,80]{4,3,2,1,0:T(8,128)(2,1)S(1)} collective-permute-done((bf16[2,2,4,40,80]{4,3,2,1,0:T(8,128)(2,1)S(1)}, bf16[2,2,4,40,80]{4,3,2,1,0:T(8,128)(2,1)S(1)}, u32[]{:S(2)}, u32[]{:S(2)}) %collective-permute-start.8) | collective-permute-done | bytes 102432 | tf_op jit(solution)/shard_map/ppermute | solution.py:68
  314.9 5.1 %all-to-all-start.1 = ((bf16[32,16,2560]{2,1,0:T(8,128)(2,1)}), bf16[32,16,2560]{2,1,0:T(8,128)(2,1)}, u32[]{:S(2)}, u32[]{:S(2)}) async-start(bf16[32,16,2560]{2,1,0:T(8,128)(2,1)} %get-tuple-element.12), calls=%async_computation.1 | async-start | bytes 5242880 | tf_op jit(solution)/shard_map/all_to_all | solution.py:35
  320.2 2.1 fusion.52
  322.4 0.4 fusion
  322.8 0.3 reshape.160
  323.1 0.7 gather_fusion
  323.8 0.2 fusion.16
  324.4 0.6 fusion.5
  325.0 0.4 collective-permute-done.9
  325.4 1.8 collective-permute-start.10
  327.3 35.9 %collective-permute-done.10 = f32[2,2,2,128]{3,2,0,1:T(2,128)S(1)} collective-permute-done((f32[2,2,2,128]{3,2,0,1:T(2,128)S(1)}, f32[2,2,2,128]{3,2,0,1:T(2,128)S(1)}, u32[]{:S(2)}, u32[]{:S(2)}) %collective-permute-start.10) | collective-permute-done | bytes 4128 | tf_op jit(solution)/shard_map/ppermute | solution.py:68
  363.2 4.6 %collective-permute-start.11 = (f32[2,2,2,128]{3,2,1,0:T(2,128)S(1)}, f32[2,2,2,128]{3,2,1,0:T(2,128)S(1)}, u32[]{:S(2)}, u32[]{:S(2)}) collective-permute-start(f32[2,2,2,128]{3,2,1,0:T(2,128)S(1)} %fusion.39), channel_id=1, source_target_pairs={{0,4},{1,5},{2,6},{3,7},{4,0},{5,1},{6,2},{7,3},{8,12},{9,13},{10,... | collective-permute-start | bytes 12296 | tf_op jit(solution)/shard_map/ppermute | solution.py:68
  367.8 1.0 fusion.22
  368.8 11.6 %collective-permute-done.11 = f32[2,2,2,128]{3,2,1,0:T(2,128)S(1)} collective-permute-done((f32[2,2,2,128]{3,2,1,0:T(2,128)S(1)}, f32[2,2,2,128]{3,2,1,0:T(2,128)S(1)}, u32[]{:S(2)}, u32[]{:S(2)}) %collective-permute-start.11) | collective-permute-done | bytes 4128 | tf_op jit(solution)/shard_map/ppermute | solution.py:68
  380.4 0.8 fusion.53
  381.2 10.5 %convolution_convert_fusion.partial_ref = bf16[2560,1280]{1,0:T(8,128)(2,1)} fusion(bf16[768,2560]{1,0:T(8,128)(2,1)} %bitcast.7, bf16[768,1280]{1,0:T(8,128)(2,1)S(1)} %copy-done.7), kind=kOutput, calls=%fused_computation.1 | convolution fusion | flops 5036441600 | bytes 12451840 | tf_op jit(solution)/shard_map/dot_general | solution.py:638
  391.7 9.6 %shard_map.179 = bf16[2560,1280]{1,0:T(8,128)(2,1)} custom-call(bf16[512,2560]{1,0:T(8,128)(2,1)} %bitcast.4.returned_ref, bf16[512,1280]{1,0:T(8,128)(2,1)S(1)} %copy-done.1, bf16[2560,1280]{1,0:T(8,128)(2,1)} %convolution_convert_fusion.partial_ref, bf16[2560,1280]{1,0:T(8,128)(2,1)} %bitcast.172, f32[80,1]{1,0:T(8,128)S(1)} %copy.40.latitude_ref), custom_call_target="tpu_custom_call" | custom-call | tf_op jit(solution)/shard_map/pallas_call | solution.py:224
  (95 shorter events, 2.4 us)
Async XLA Ops:
  0.6 323.2 %copy-start = (bf16[1,8,128,128]{3,2,1,0:T(8,128)(2,1)S(1)}, bf16[1,8,128,128]{3,2,1,0:T(8,128)(2,1)}, u32[]{:S(2)}) copy-start(bf16[1,8,128,128]{3,2,1,0:T(8,128)(2,1)} %param.24) | copy-start | bytes 786436
  0.6 0.7 copy-start.4
  13.8 7.5 %copy-start.5 = (s32[640]{0:T(1024)S(1)}, s32[640]{0:T(1024)}, u32[]{:S(2)}) copy-start(s32[640]{0:T(1024)} %waves_ref.3) | copy-start | bytes 7684
  13.9 96.8 %all-to-all-start.2 = ((bf16[32,24,2560]{2,1,0:T(8,128)(2,1)}), bf16[32,24,2560]{2,1,0:T(8,128)(2,1)}, u32[]{:S(2)}, u32[]{:S(2)}) async-start(bf16[32,24,2560]{2,1,0:T(8,128)(2,1)} %bitcast.174), calls=%async_computation.2 | async-start | bytes 7864320 | tf_op jit(solution)/shard_map/all_to_all | solution.py:35
  110.6 3.0 copy-start.18
  110.6 3.1 copy-start.19
  110.6 3.3 copy-start.2
  110.6 3.3 copy-start.3
  110.7 64.2 %all-to-all-start = ((bf16[32,16,2560]{2,1,0:T(8,128)(2,1)}), bf16[32,16,2560]{2,1,0:T(8,128)(2,1)S(1)}, u32[]{:S(2)}, u32[]{:S(2)}) async-start(bf16[32,16,2560]{2,1,0:T(8,128)(2,1)} %bitcast.175), calls=%async_computation | async-start | bytes 5242880 | tf_op jit(solution)/shard_map/all_to_all | solution.py:35
  174.9 3.7 copy-start.13
  174.9 3.7 copy-start.14
  174.9 3.7 copy-start.15
  174.9 140.0 %all-to-all-start.3 = ((bf16[32,24,2560]{2,1,0:T(8,128)(2,1)}), bf16[32,24,2560]{2,1,0:T(8,128)(2,1)}, u32[]{:S(2)}, u32[]{:S(2)}) async-start(bf16[32,24,2560]{2,1,0:T(8,128)(2,1)} %get-tuple-element.15), calls=%async_computation.3 | async-start | bytes 7864320 | tf_op jit(solution)/shard_map/all_to_all | solution.py:35
  178.6 29.1 %copy-start.12 = (bf16[1,48,128]{2,1,0:T(8,128)(2,1)}, bf16[1,48,128]{2,1,0:T(8,128)(2,1)S(1)}, u32[]{:S(2)}) copy-start(bf16[1,48,128]{2,1,0:T(8,128)(2,1)S(1)} %get-tuple-element.48) | copy-start | bytes 36868
  178.6 29.1 %copy-start.10 = (bf16[1,48,128]{2,1,0:T(8,128)(2,1)}, bf16[1,48,128]{2,1,0:T(8,128)(2,1)S(1)}, u32[]{:S(2)}) copy-start(bf16[1,48,128]{2,1,0:T(8,128)(2,1)S(1)} %get-tuple-element.55) | copy-start | bytes 36868
  178.7 29.1 %copy-start.11 = (bf16[1,48,128]{2,1,0:T(8,128)(2,1)}, bf16[1,48,128]{2,1,0:T(8,128)(2,1)S(1)}, u32[]{:S(2)}) copy-start(bf16[1,48,128]{2,1,0:T(8,128)(2,1)S(1)} %get-tuple-element.56) | copy-start | bytes 36868
  180.2 19.2 %collective-permute-start = (bf16[11,4,128]{2,1,0:T(4,128)(2,1)}, bf16[11,4,128]{2,1,0:T(4,128)(2,1)}, u32[]{:S(2)}, u32[]{:S(2)}) collective-permute-start(bf16[11,4,128]{2,1,0:T(4,128)(2,1)} %get-tuple-element.45), channel_id=1, source_target_pairs={{0,8},{8,16},{16,24},{1,9},{9,17},{17,25},{2,10},{10,18},{18,26},{... | collective-permute-start | bytes 33800 | tf_op jit(solution)/shard_map/ppermute | solution.py:28
  184.3 18.4 %collective-permute-start.1 = (bf16[11,4,128]{2,1,0:T(4,128)(2,1)}, bf16[11,4,128]{2,1,0:T(4,128)(2,1)}, u32[]{:S(2)}, u32[]{:S(2)}) collective-permute-start(bf16[11,4,128]{2,1,0:T(4,128)(2,1)} %get-tuple-element.46), channel_id=1, source_target_pairs={{8,0},{16,8},{24,16},{9,1},{17,9},{25,17},{10,2},{18,10},{26,18},{... | collective-permute-start | bytes 33800 | tf_op jit(solution)/shard_map/ppermute | solution.py:29
  204.3 4.8 %collective-permute-start.2 = (bf16[11,56,4]{2,1,0:T(8,128)(2,1)}, bf16[11,56,4]{2,1,0:T(8,128)(2,1)}, u32[]{:S(2)}, u32[]{:S(2)}) collective-permute-start(bf16[11,56,4]{2,1,0:T(8,128)(2,1)} %get-tuple-element.43), channel_id=1, source_target_pairs={{0,1},{1,2},{2,3},{3,4},{4,5},{5,6},{6,7},{8,9},{9,10},{10,11},{11... | collective-permute-start | bytes 14792 | tf_op jit(solution)/shard_map/ppermute | solution.py:28
  206.3 3.6 collective-permute-start.3
  212.1 27.5 %copy-start.16 = (f32[8]{0:T(128)S(1)}, f32[8]{0:T(128)}, u32[]{:S(2)}) copy-start(f32[8]{0:T(128)} %compare_convert_fusion) | copy-start | bytes 100
  230.5 9.1 %copy-start.6 = (f32[11,56,136]{2,1,0:T(8,128)S(1)}, f32[11,56,136]{2,1,0:T(8,128)}, u32[]{:S(2)}) copy-start(f32[11,56,136]{2,1,0:T(8,128)} %maximum_convert_fusion) | copy-start | bytes 1005316
  230.8 7.1 %collective-permute-start.4 = (bf16[8,40,80]{2,1,0:T(8,128)(2,1)S(1)}, bf16[8,40,80]{2,1,0:T(8,128)(2,1)S(1)}, u32[]{:S(2)}, u32[]{:S(2)}) collective-permute-start(bf16[8,40,80]{2,1,0:T(8,128)(2,1)S(1)} %maximum_bitcast_fusion), channel_id=1, source_target_pairs={{0,8},{8,0},{16,24},{24,16},{1,9},{9,1},{17,25},{25,17},{2,10},{10... | collective-permute-start | bytes 153608 | tf_op jit(solution)/shard_map/ppermute | solution.py:68
  238.1 5.4 %collective-permute-start.5 = (bf16[8,2,40,80]{3,2,1,0:T(8,128)(2,1)S(1)}, bf16[8,2,40,80]{3,2,1,0:T(8,128)(2,1)S(1)}, u32[]{:S(2)}, u32[]{:S(2)}) collective-permute-start(bf16[8,2,40,80]{3,2,1,0:T(8,128)(2,1)S(1)} %pad_maximum_fusion.2), channel_id=1, source_target_pairs={{0,16},{8,24},{16,0},{24,8},{1,17},{9,25},{17,1},{25,9},{2,18},{10... | collective-permute-start | bytes 307208 | tf_op jit(solution)/shard_map/ppermute | solution.py:68
  243.6 30.9 %collective-permute-start.6 = (bf16[2,2,4,40,80]{4,3,2,1,0:T(8,128)(2,1)S(1)}, bf16[2,2,4,40,80]{4,3,2,1,0:T(8,128)(2,1)S(1)}, u32[]{:S(2)}, u32[]{:S(2)}) collective-permute-start(bf16[2,2,4,40,80]{4,3,2,1,0:T(8,128)(2,1)S(1)} %dynamic-slice_bitcast_fusion), channel_id=1, source_target_pairs={{0,1},{1,0},{2,3},{3,2},{4,5},{5,4},{6,7},{7,6},{8,9},{9,8},{10,11... | collective-permute-start | bytes 307208 | tf_op jit(solution)/shard_map/ppermute | solution.py:68
  274.6 29.3 %collective-permute-start.7 = (bf16[2,2,4,40,80]{4,3,2,1,0:T(8,128)(2,1)S(1)}, bf16[2,2,4,40,80]{4,3,2,1,0:T(8,128)(2,1)S(1)}, u32[]{:S(2)}, u32[]{:S(2)}) collective-permute-start(bf16[2,2,4,40,80]{4,3,2,1,0:T(8,128)(2,1)S(1)} %bitcast.183), channel_id=1, source_target_pairs={{0,2},{1,3},{2,0},{3,1},{4,6},{5,7},{6,4},{7,5},{8,10},{9,11},{10,... | collective-permute-start | bytes 307208 | tf_op jit(solution)/shard_map/ppermute | solution.py:68
  304.0 10.9 %collective-permute-start.8 = (bf16[2,2,4,40,80]{4,3,2,1,0:T(8,128)(2,1)S(1)}, bf16[2,2,4,40,80]{4,3,2,1,0:T(8,128)(2,1)S(1)}, u32[]{:S(2)}, u32[]{:S(2)}) collective-permute-start(bf16[2,2,4,40,80]{4,3,2,1,0:T(8,128)(2,1)S(1)} %fusion.24), channel_id=1, source_target_pairs={{0,4},{1,5},{2,6},{3,7},{4,0},{5,1},{6,2},{7,3},{8,12},{9,13},{10,... | collective-permute-start | bytes 307208 | tf_op jit(solution)/shard_map/ppermute | solution.py:68
  314.9 76.8 %all-to-all-start.1 = ((bf16[32,16,2560]{2,1,0:T(8,128)(2,1)}), bf16[32,16,2560]{2,1,0:T(8,128)(2,1)}, u32[]{:S(2)}, u32[]{:S(2)}) async-start(bf16[32,16,2560]{2,1,0:T(8,128)(2,1)} %get-tuple-element.12), calls=%async_computation.1 | async-start | bytes 5242880 | tf_op jit(solution)/shard_map/all_to_all | solution.py:35
  320.0 2.4 copy-start.1
  320.2 3.5 copy-start.20
  320.2 3.9 copy-start.21
  320.2 4.2 %copy-start.8 = (f32[50,130]{1,0:T(8,128)S(1)}, f32[50,130]{1,0:T(8,128)}, u32[]{:S(2)}) copy-start(f32[50,130]{1,0:T(8,128)} %get-tuple-element.23) | copy-start | bytes 78004
  320.2 4.2 %copy-start.9 = (f32[50,130]{1,0:T(8,128)S(1)}, f32[50,130]{1,0:T(8,128)}, u32[]{:S(2)}) copy-start(f32[50,130]{1,0:T(8,128)} %get-tuple-element.24) | copy-start | bytes 78004
  322.8 57.6 %copy-start.17 = (pred[48,16]{0,1:T(8,128)(4,1)S(1)}, pred[48,16]{0,1:T(8,128)(4,1)}, u32[]{:S(2)}) copy-start(pred[48,16]{0,1:T(8,128)(4,1)} %reshape.152) | copy-start | bytes 2308
  323.7 57.5 %copy-start.7 = (bf16[768,1280]{1,0:T(8,128)(2,1)S(1)}, bf16[768,1280]{1,0:T(8,128)(2,1)}, u32[]{:S(2)}) copy-start(bf16[768,1280]{1,0:T(8,128)(2,1)} %get-tuple-element.16) | copy-start | bytes 5898244
  324.2 1.2 collective-permute-start.9
  325.4 37.8 %collective-permute-start.10 = (f32[2,2,2,128]{3,2,0,1:T(2,128)S(1)}, f32[2,2,2,128]{3,2,0,1:T(2,128)S(1)}, u32[]{:S(2)}, u32[]{:S(2)}) collective-permute-start(f32[2,2,2,128]{3,2,0,1:T(2,128)S(1)} %fusion.43), channel_id=1, source_target_pairs={{0,2},{1,3},{2,0},{3,1},{4,6},{5,7},{6,4},{7,5},{8,10},{9,11},{10,... | collective-permute-start | bytes 12296 | tf_op jit(solution)/shard_map/ppermute | solution.py:68
  363.2 17.2 %collective-permute-start.11 = (f32[2,2,2,128]{3,2,1,0:T(2,128)S(1)}, f32[2,2,2,128]{3,2,1,0:T(2,128)S(1)}, u32[]{:S(2)}, u32[]{:S(2)}) collective-permute-start(f32[2,2,2,128]{3,2,1,0:T(2,128)S(1)} %fusion.39), channel_id=1, source_target_pairs={{0,4},{1,5},{2,6},{3,7},{4,0},{5,1},{6,2},{7,3},{8,12},{9,13},{10,... | collective-permute-start | bytes 12296 | tf_op jit(solution)/shard_map/ppermute | solution.py:68

commit v5 on v4

--- a/solution.py
+++ b/solution.py
@@ -12,7 +12,7 @@
 SWEEPS = 4
 CAP = 2
 AXES = ("lev", "wav")
-CHUNKS = (3, 2)
+CHUNKS = (2, 3)
 UNIT = 4
 BLOCK = 1280
 LANES = 128
@@ -127,13 +127,13 @@
     owners, slots_owner, slots_dev, start, units, waves_ref, rows_ref, fourier_ref, table_ref
 ):
     rows, lon_count = table_ref.shape
-    tile_rows = 4 * UNIT
+    tile_rows = 2 * UNIT
 
     @pl.when(pl.program_id(0) == 0)
     def _():
         lane = lax.broadcasted_iota(jnp.int32, (tile_rows, LANES), 1)
         row = lax.broadcasted_iota(jnp.int32, (tile_rows, LANES), 0)
-        half = row // UNIT % 2
+        upper = row < UNIT
         first = lane == 0
         scale = math.sqrt(2.0 / lon_count)
 
@@ -145,31 +145,32 @@
                 slot = (device % owners) * slots_owner + (device // owners) * slots_dev
                 slot = slot + start + group % units * UNIT
                 for i in range(UNIT):
-                    here = (row // (2 * UNIT) == part) & (row % UNIT == i)
-                    waves = jnp.where(here, waves_ref[slot + i], waves)
-            steps = waves * lane + half * (lon_count // 4)
-            steps = jnp.where(first, waves * LANES, steps).astype(jnp.float32)
+                    waves = jnp.where(row == part * UNIT + i, waves_ref[slot + i], waves)
+            steps = jnp.where(first, waves * LANES, waves * lane).astype(jnp.float32)
             steps = steps - lon_count * jnp.round(steps * (1.0 / lon_count))
             angle = steps * (2.0 * math.pi / lon_count)
             cosine, sine = jnp.cos(angle), jnp.sin(angle)
             cos_step = jnp.broadcast_to(cosine[:, :1], cosine.shape)
             sin_step = jnp.broadcast_to(sine[:, :1], sine.shape)
-            turn = half.astype(jnp.float32)
-            cosine = scale * jnp.where(first, 1.0 - turn, cosine)
-            sine = scale * jnp.where(first, turn, sine)
-            place = pl.ds(pl.multiple_of(index * tile_rows, tile_rows), tile_rows)
+            cosine = scale * jnp.where(first, 1.0, cosine)
+            sine = -scale * jnp.where(first, 0.0, sine)
+            place = pl.ds(pl.multiple_of(index * 2 * tile_rows, 2 * tile_rows), 2 * tile_rows)
             for column in range(lon_count // LANES):
-                table_ref[place, column * LANES : (column + 1) * LANES] = cosine.astype(
-                    jnp.bfloat16
-                )
+                pair = [
+                    jnp.where(upper, cosine, pltpu.roll(sine, UNIT, 0)),
+                    jnp.where(upper, pltpu.roll(cosine, UNIT, 0), sine),
+                ]
+                table_ref[place, column * LANES : (column + 1) * LANES] = jnp.concatenate(
+                    pair, axis=0
+                ).astype(jnp.bfloat16)
                 cosine, sine = (
-                    cosine * cos_step - sine * sin_step,
-                    sine * cos_step + cosine * sin_step,
+                    cosine * cos_step + sine * sin_step,
+                    sine * cos_step - cosine * sin_step,
                 )
             return carry
 
-        tiles = rows // tile_rows
-        lax.fori_loop(0, tiles, tile, 0, unroll=math.gcd(tiles, 8))
+        tiles = rows // (2 * tile_rows)
+        lax.fori_loop(0, tiles, tile, 0, unroll=math.gcd(tiles, 16))
 
     fourier_ref[...] = lax.dot_general(
         table_ref[...], rows_ref[...], (((1,), (1,)), ((), ())), preferred_element_type=jnp.float32
@@ -199,7 +200,10 @@
             pltpu.HBM((rows, lon_count), jnp.bfloat16),
         ],
         compiler_params=pltpu.CompilerParams(vmem_limit_bytes=32 * 1024 * 1024),
-    )(waves, pltpu.with_memory_space_constraint(rows_flat, pltpu.HBM))
+    )(
+        pltpu.with_memory_space_constraint(waves, pltpu.HBM),
+        pltpu.with_memory_space_constraint(rows_flat, pltpu.HBM),
+    )
 
 
 def final_kernel(lat_dev, returned_ref, table_ref, partial_ref, rows_ref, latitude_ref, out_ref):

time: 402 us -> 392 us (0.975)
  waiting for transfers between devices: 191 us -> 180 us
  matrix products: 14.2 us -> 8.35 us
    ppermute x8, waiting for transfers between devices: 67.7 us -> 39.8 us  [swap(): came = lax.ppermute(sent, axis, pairs)]
    all_to_all x4, waiting for transfers between devices: 115 us -> 140 us  [exchange(): return lax.all_to_all(value, AXES, split_axis=0, concat_axis=0, tiled=True)]
    ppermute x8, starting transfers between devices: 67.4 us -> 72.7 us  [swap(): came = lax.ppermute(sent, axis, pairs)]
    ppermute x2, waiting for transfers between devices: 5.12 us -> 0.01 us  [with_halo(): before = lax.ppermute(last, axis, up)]
    dot_general x1, matrix products: 10.5 us -> 5.61 us  [per_device(): lax.dot_general(returned[index].reshape(-1, cells), tables[index], (((0,)...]
  transfers between devices with their start and end apart: 16 -> 16, of which waited for: 13 -> 11; matrix products, arithmetic and copies ran while one was open for 9% -> 8% of each run, Pallas kernels for 13% -> 14%
where the time goes in v5:
time: 392 us; the launch traced here: 391 us
  waiting for transfers between devices  180 us (46%)
  starting transfers between devices  99.1 us (25%)
  Pallas kernels  77.5 us (20%)
  other arithmetic  13.3 us (3%)
  local copies, waits for them, and re-layouts  11.5 us (3%)
  matrix products  8.35 us (2%)
    all_to_all x4, waiting for transfers between devices, exchange(): return lax.all_to_all(value, AXES, split_axis=0, concat_axis=0, tiled=True)  140 us
    ppermute x8, starting transfers between devices, swap(): came = lax.ppermute(sent, axis, pairs)  72.7 us
    pallas_call x2, Pallas kernels, spectral_call(): pl.pallas_call(body, grid_spec=pltpu.PrefetchScalarGridSpec(num_scalar_pr...  44.7 us
    ppermute x8, waiting for transfers between devices, swap(): came = lax.ppermute(sent, axis, pairs)  39.8 us
    pallas_call x2, Pallas kernels, fourier_call(): pl.pallas_call(body, grid_spec=pltpu.PrefetchScalarGridSpec(num_scalar_pr...  21.1 us
    all_to_all x4, starting transfers between devices, exchange(): return lax.all_to_all(value, AXES, split_axis=0, concat_axis=0, tiled=True)  17.5 us
    pallas_call x1, Pallas kernels, final_call(): pl.pallas_call(functools.partial(final_kernel, lat_dev), grid=(cells // b...  11.7 us
  transfers between devices with their start and end apart: 16, of which 11 were waited for; matrix products, arithmetic and copies ran while one was open for 8% of the time, Pallas kernels for 14%

profile of v5, /device:TPU:0, one launch (start us, length us, event | category | flops | bytes accessed | tf_op | source)
XLA Modules:
  0.0 391.4 jit_solution(14405450557268031285)
XLA Ops:
  0.6 9.2 %shard_map.177 = (bf16[512,2560]{1,0:T(8,128)(2,1)}, bf16[512,1280]{1,0:T(8,128)(2,1)}) custom-call(s32[640]{0:T(1024)} %waves_ref.3, bf16[2560,1280]{1,0:T(8,128)(2,1)} %bitcast.170), custom_call_target="tpu_custom_call" | custom-call | tf_op jit(solution)/shard_map/pallas_call | solution.py:187
  9.8 7.3 %all-to-all-start.2 = ((bf16[32,16,2560]{2,1,0:T(8,128)(2,1)}), bf16[32,16,2560]{2,1,0:T(8,128)(2,1)S(1)}, u32[]{:S(2)}, u32[]{:S(2)}) async-start(bf16[32,16,2560]{2,1,0:T(8,128)(2,1)} %bitcast.176), calls=%async_computation.2 | async-start | bytes 5242880 | tf_op jit(solution)/shard_map/all_to_all | solution.py:35
  17.2 11.9 %shard_map.175 = (bf16[768,2560]{1,0:T(8,128)(2,1)}, bf16[768,1280]{1,0:T(8,128)(2,1)}) custom-call(s32[640]{0:T(1024)} %waves_ref.3, bf16[2560,1280]{1,0:T(8,128)(2,1)} %bitcast.171), custom_call_target="tpu_custom_call" | custom-call | tf_op jit(solution)/shard_map/pallas_call | solution.py:187
  29.0 49.4 %all-to-all-done.2.arrived_ref = bf16[32,16,2560]{2,1,0:T(8,128)(2,1)S(1)} async-done(((bf16[32,16,2560]{2,1,0:T(8,128)(2,1)}), bf16[32,16,2560]{2,1,0:T(8,128)(2,1)S(1)}, u32[]{:S(2)}, u32[]{:S(2)}) %all-to-all-start.2) | async-done | bytes 2621472 | tf_op jit(solution)/shard_map/all_to_all | solution.py:35
  78.4 3.7 all-to-all-start
  82.2 0.1 copy.38.weights_ref
  82.3 0.8 dynamic_slice.60.waves_ref
  83.0 0.1 add_divide_fusion.damping_ref
  83.2 18.5 %shard_map.178 = (bf16[32,16,2560]{2,1,0:T(8,128)(2,1)}, f32[2,8,640]{2,1,0:T(8,128)S(1)}) custom-call(s32[1]{0:T(128)} %bitcast.5.base_ref, s32[8]{0:T(128)S(1)} %dynamic_slice.60.waves_ref, bf16[32,16,2560]{2,1,0:T(8,128)(2,1)S(1)} %all-to-all-done.2.arrived_ref, bf16[80,640,640]{2,1,0:T(8,128)(2,1)} %leg_ref.3, bf16[128,128]{1,0:T(8,128)(2,1)S(1)} %copy-done.2, ...), custom_call_target="tpu_custom_call" | custom-call | tf_op jit(solution)/shard_map/pallas_call | solution.py:407
  101.7 69.8 %all-to-all-done.arrived_ref = bf16[32,24,2560]{2,1,0:T(8,128)(2,1)} async-done(((bf16[32,24,2560]{2,1,0:T(8,128)(2,1)}), bf16[32,24,2560]{2,1,0:T(8,128)(2,1)}, u32[]{:S(2)}, u32[]{:S(2)}) %all-to-all-start) | async-done | bytes 3932192 | tf_op jit(solution)/shard_map/all_to_all | solution.py:35
  171.5 2.9 all-to-all-start.3
  174.5 0.9 multiply_convert_fusion
  175.5 0.6 pad_maximum_fusion.7
  176.1 4.1 %collective-permute-start = (bf16[11,4,128]{2,1,0:T(4,128)(2,1)}, bf16[11,4,128]{2,1,0:T(4,128)(2,1)}, u32[]{:S(2)}, u32[]{:S(2)}) collective-permute-start(bf16[11,4,128]{2,1,0:T(4,128)(2,1)} %get-tuple-element.45), channel_id=1, source_target_pairs={{0,8},{8,16},{16,24},{1,9},{9,17},{17,25},{2,10},{10,18},{18,26},{... | collective-permute-start | bytes 33800 | tf_op jit(solution)/shard_map/ppermute | solution.py:28
  180.3 1.3 collective-permute-start.1
  181.5 0.5 broadcast.117
  182.1 0.7 reduce.7
  182.8 0.7 reduce.6
  183.6 0.6 compare_and_fusion.1
  184.2 0.5 compare_convert_fusion
  184.8 0.6 pad_clamp_fusion
  185.4 0.3 convert_reduce_fusion
  185.7 0.7 and_reduce_fusion
  186.4 1.2 sine_bitcast_fusion
  187.7 0.6 fusion.49
  188.3 0.8 dynamic_slice.59.waves_ref
  189.0 26.2 %shard_map.176 = (bf16[32,24,2560]{2,1,0:T(8,128)(2,1)}, f32[3,8,640]{2,1,0:T(8,128)S(1)}) custom-call(s32[1]{0:T(128)} %bitcast.base_ref, s32[12]{0:T(128)S(1)} %dynamic_slice.59.waves_ref, bf16[32,24,2560]{2,1,0:T(8,128)(2,1)} %all-to-all-done.arrived_ref, bf16[80,640,640]{2,1,0:T(8,128)(2,1)} %leg_ref.3, bf16[128,128]{1,0:T(8,128)(2,1)S(1)} %copy-done.2, ...), custom_call_target="tpu_custom_call" | custom-call | tf_op jit(solution)/shard_map/pallas_call | solution.py:407
  215.2 20.5 %all-to-all-done.3 = bf16[32,16,2560]{2,1,0:T(8,128)(2,1)S(1)} async-done(((bf16[32,16,2560]{2,1,0:T(8,128)(2,1)}), bf16[32,16,2560]{2,1,0:T(8,128)(2,1)S(1)}, u32[]{:S(2)}, u32[]{:S(2)}) %all-to-all-start.3) | async-done | bytes 2621472 | tf_op jit(solution)/shard_map/all_to_all | solution.py:35
  235.8 1.6 copy-done.4
  237.3 3.6 all-to-all-start.1
  240.9 0.8 pad_maximum_fusion.3
  241.8 2.0 collective-permute-start.2
  243.8 1.5 collective-permute-start.3
  245.4 1.2 reshape.152
  246.6 0.7 copy.40.latitude_ref
  247.4 0.9 collective-permute-done.3
  248.3 1.0 maximum_convert_fusion
  249.6 1.5 collective-permute-start.4
  251.3 14.2 %collective-permute-done.4 = bf16[8,40,80]{2,1,0:T(8,128)(2,1)S(1)} collective-permute-done((bf16[8,40,80]{2,1,0:T(8,128)(2,1)S(1)}, bf16[8,40,80]{2,1,0:T(8,128)(2,1)S(1)}, u32[]{:S(2)}, u32[]{:S(2)}) %collective-permute-start.4) | collective-permute-done | bytes 51232 | tf_op jit(solution)/shard_map/ppermute | solution.py:68
  265.6 1.5 collective-permute-start.5
  267.1 0.6 fusion.15
  267.7 8.2 %collective-permute-done.5 = bf16[8,2,40,80]{3,2,1,0:T(8,128)(2,1)S(1)} collective-permute-done((bf16[8,2,40,80]{3,2,1,0:T(8,128)(2,1)S(1)}, bf16[8,2,40,80]{3,2,1,0:T(8,128)(2,1)S(1)}, u32[]{:S(2)}, u32[]{:S(2)}) %collective-permute-start.5) | collective-permute-done | bytes 102432 | tf_op jit(solution)/shard_map/ppermute | solution.py:68
  276.0 41.0 %collective-permute-start.6 = (bf16[2,2,4,40,80]{4,3,2,1,0:T(8,128)(2,1)S(1)}, bf16[2,2,4,40,80]{4,3,2,1,0:T(8,128)(2,1)S(1)}, u32[]{:S(2)}, u32[]{:S(2)}) collective-permute-start(bf16[2,2,4,40,80]{4,3,2,1,0:T(8,128)(2,1)S(1)} %dynamic-slice_bitcast_fusion), channel_id=1, source_target_pairs={{0,1},{1,0},{2,3},{3,2},{4,5},{5,4},{6,7},{7,6},{8,9},{9,8},{10,11... | collective-permute-start | bytes 307208 | tf_op jit(solution)/shard_map/ppermute | solution.py:68
  317.2 0.9 collective-permute-done.6
  318.2 23.5 %collective-permute-start.7 = (bf16[2,2,4,40,80]{4,3,2,1,0:T(8,128)(2,1)S(1)}, bf16[2,2,4,40,80]{4,3,2,1,0:T(8,128)(2,1)S(1)}, u32[]{:S(2)}, u32[]{:S(2)}) collective-permute-start(bf16[2,2,4,40,80]{4,3,2,1,0:T(8,128)(2,1)S(1)} %bitcast.184), channel_id=1, source_target_pairs={{0,2},{1,3},{2,0},{3,1},{4,6},{5,7},{6,4},{7,5},{8,10},{9,11},{10,... | collective-permute-start | bytes 307208 | tf_op jit(solution)/shard_map/ppermute | solution.py:68
  341.8 0.6 fusion.10
  342.4 4.1 %collective-permute-done.7 = bf16[2,2,4,40,80]{4,3,2,1,0:T(8,128)(2,1)S(1)} collective-permute-done((bf16[2,2,4,40,80]{4,3,2,1,0:T(8,128)(2,1)S(1)}, bf16[2,2,4,40,80]{4,3,2,1,0:T(8,128)(2,1)S(1)}, u32[]{:S(2)}, u32[]{:S(2)}) %collective-permute-start.7) | collective-permute-done | bytes 102432 | tf_op jit(solution)/shard_map/ppermute | solution.py:68
  346.6 3.7 collective-permute-start.8
  350.3 0.7 slice_bitcast_fusion.8
  351.0 6.4 %collective-permute-done.8 = bf16[2,2,4,40,80]{4,3,2,1,0:T(8,128)(2,1)S(1)} collective-permute-done((bf16[2,2,4,40,80]{4,3,2,1,0:T(8,128)(2,1)S(1)}, bf16[2,2,4,40,80]{4,3,2,1,0:T(8,128)(2,1)S(1)}, u32[]{:S(2)}, u32[]{:S(2)}) %collective-permute-start.8) | collective-permute-done | bytes 102432 | tf_op jit(solution)/shard_map/ppermute | solution.py:68
  357.7 0.4 fusion.52
  358.1 1.2 fusion
  359.3 1.9 reshape.160
  361.1 1.6 gather_fusion
  362.9 0.2 fusion.16
  363.1 0.1 fusion.33
  363.3 1.6 fusion.5
  365.1 3.5 collective-permute-done.10
  368.6 1.2 collective-permute-start.11
  369.9 1.0 fusion.22
  370.9 2.4 collective-permute-done.11
  373.2 0.8 fusion.53
  374.1 5.6 %convolution_convert_fusion.partial_ref = bf16[2560,1280]{1,0:T(8,128)(2,1)} fusion(bf16[512,2560]{1,0:T(8,128)(2,1)S(1)} %bitcast.175, bf16[512,1280]{1,0:T(8,128)(2,1)S(1)} %copy-done.7), kind=kOutput, calls=%fused_computation.1 | convolution fusion | flops 3358720000 | bytes 10485760 | tf_op jit(solution)/shard_map/dot_general | solution.py:642
  379.7 11.7 %shard_map.179 = bf16[2560,1280]{1,0:T(8,128)(2,1)} custom-call(bf16[768,2560]{1,0:T(8,128)(2,1)} %bitcast.4.returned_ref, bf16[768,1280]{1,0:T(8,128)(2,1)S(1)} %copy-done.1, bf16[2560,1280]{1,0:T(8,128)(2,1)} %convolution_convert_fusion.partial_ref, bf16[2560,1280]{1,0:T(8,128)(2,1)} %bitcast.172, f32[80,1]{1,0:T(8,128)S(1)} %copy.40.latitude_ref), custom_call_target="tpu_custom_call" | custom-call | tf_op jit(solution)/shard_map/pallas_call | solution.py:228
  (101 shorter events, 1.9 us)
Async XLA Ops:
  0.6 362.3 %copy-start = (bf16[1,8,128,128]{3,2,1,0:T(8,128)(2,1)S(1)}, bf16[1,8,128,128]{3,2,1,0:T(8,128)(2,1)}, u32[]{:S(2)}) copy-start(bf16[1,8,128,128]{3,2,1,0:T(8,128)(2,1)} %param.24) | copy-start | bytes 786436
  9.8 68.6 %all-to-all-start.2 = ((bf16[32,16,2560]{2,1,0:T(8,128)(2,1)}), bf16[32,16,2560]{2,1,0:T(8,128)(2,1)S(1)}, u32[]{:S(2)}, u32[]{:S(2)}) async-start(bf16[32,16,2560]{2,1,0:T(8,128)(2,1)} %bitcast.176), calls=%async_computation.2 | async-start | bytes 5242880 | tf_op jit(solution)/shard_map/all_to_all | solution.py:35
  78.4 3.7 copy-start.18
  78.4 4.6 %copy-start.19 = (f32[128]{0:T(128)S(1)}, f32[128]{0:T(128)}, u32[]{:S(2)}) copy-start(f32[128]{0:T(128)} %param.22) | copy-start | bytes 1540
  78.4 4.7 %copy-start.2 = (bf16[128,128]{1,0:T(8,128)(2,1)S(1)}, bf16[128,128]{1,0:T(8,128)(2,1)}, u32[]{:S(2)}) copy-start(bf16[128,128]{1,0:T(8,128)(2,1)} %analysis_ref.3) | copy-start | bytes 98308
  78.4 4.8 %copy-start.3 = (bf16[128,128]{1,0:T(8,128)(2,1)S(1)}, bf16[128,128]{1,0:T(8,128)(2,1)}, u32[]{:S(2)}) copy-start(bf16[128,128]{1,0:T(8,128)(2,1)} %synthesis_ref.3) | copy-start | bytes 98308
  78.4 93.1 %all-to-all-start = ((bf16[32,24,2560]{2,1,0:T(8,128)(2,1)}), bf16[32,24,2560]{2,1,0:T(8,128)(2,1)}, u32[]{:S(2)}, u32[]{:S(2)}) async-start(bf16[32,24,2560]{2,1,0:T(8,128)(2,1)} %bitcast.174), calls=%async_computation | async-start | bytes 7864320 | tf_op jit(solution)/shard_map/all_to_all | solution.py:35
  171.5 3.0 copy-start.12
  171.5 3.0 copy-start.13
  171.5 3.0 copy-start.14
  171.5 10.6 %copy-start.22 = (s32[1,64,1]{1,2,0:T(1,128)S(1)}, s32[1,64,1]{1,2,0:T(1,128)}, u32[]{:S(2)}) copy-start(s32[1,64,1]{1,2,0:T(1,128)} %param.25) | copy-start | bytes 772
  171.5 11.3 %copy-start.23 = (s32[1,64]{1,0:T(1,128)S(1)}, s32[1,64]{1,0:T(1,128)}, u32[]{:S(2)}) copy-start(s32[1,64]{1,0:T(1,128)} %param.27) | copy-start | bytes 772
  171.5 12.0 %copy-start.24 = (s32[1,64]{1,0:T(1,128)S(1)}, s32[1,64]{1,0:T(1,128)}, u32[]{:S(2)}) copy-start(s32[1,64]{1,0:T(1,128)} %param.26) | copy-start | bytes 772
  171.5 64.2 %all-to-all-start.3 = ((bf16[32,16,2560]{2,1,0:T(8,128)(2,1)}), bf16[32,16,2560]{2,1,0:T(8,128)(2,1)S(1)}, u32[]{:S(2)}, u32[]{:S(2)}) async-start(bf16[32,16,2560]{2,1,0:T(8,128)(2,1)} %get-tuple-element.15), calls=%async_computation.3 | async-start | bytes 5242880 | tf_op jit(solution)/shard_map/all_to_all | solution.py:35
  174.5 1.6 copy-start.10
  174.5 1.0 copy-start.8
  176.1 64.8 %collective-permute-start = (bf16[11,4,128]{2,1,0:T(4,128)(2,1)}, bf16[11,4,128]{2,1,0:T(4,128)(2,1)}, u32[]{:S(2)}, u32[]{:S(2)}) collective-permute-start(bf16[11,4,128]{2,1,0:T(4,128)(2,1)} %get-tuple-element.45), channel_id=1, source_target_pairs={{0,8},{8,16},{16,24},{1,9},{9,17},{17,25},{2,10},{10,18},{18,26},{... | collective-permute-start | bytes 33800 | tf_op jit(solution)/shard_map/ppermute | solution.py:28
  180.3 60.6 %collective-permute-start.1 = (bf16[11,4,128]{2,1,0:T(4,128)(2,1)}, bf16[11,4,128]{2,1,0:T(4,128)(2,1)}, u32[]{:S(2)}, u32[]{:S(2)}) collective-permute-start(bf16[11,4,128]{2,1,0:T(4,128)(2,1)} %get-tuple-element.46), channel_id=1, source_target_pairs={{8,0},{16,8},{24,16},{9,1},{17,9},{25,17},{10,2},{18,10},{26,18},{... | collective-permute-start | bytes 33800 | tf_op jit(solution)/shard_map/ppermute | solution.py:29
  235.7 1.6 copy-start.4
  235.7 5.2 %copy-start.9 = (bf16[1,48,128]{2,1,0:T(8,128)(2,1)S(1)}, bf16[1,48,128]{2,1,0:T(8,128)(2,1)}, u32[]{:S(2)}) copy-start(bf16[1,48,128]{2,1,0:T(8,128)(2,1)} %copy-done.8) | copy-start | bytes 36868
  235.8 5.2 %copy-start.11 = (bf16[1,48,128]{2,1,0:T(8,128)(2,1)S(1)}, bf16[1,48,128]{2,1,0:T(8,128)(2,1)}, u32[]{:S(2)}) copy-start(bf16[1,48,128]{2,1,0:T(8,128)(2,1)} %copy-done.10) | copy-start | bytes 36868
  237.3 142.4 %all-to-all-start.1 = ((bf16[32,24,2560]{2,1,0:T(8,128)(2,1)}), bf16[32,24,2560]{2,1,0:T(8,128)(2,1)}, u32[]{:S(2)}, u32[]{:S(2)}) async-start(bf16[32,24,2560]{2,1,0:T(8,128)(2,1)} %get-tuple-element.12), calls=%async_computation.1 | async-start | bytes 7864320 | tf_op jit(solution)/shard_map/all_to_all | solution.py:35
  240.9 26.2 %copy-start.15 = (f32[8]{0:T(128)S(1)}, f32[8]{0:T(128)}, u32[]{:S(2)}) copy-start(f32[8]{0:T(128)} %compare_convert_fusion) | copy-start | bytes 100
  241.8 5.6 %collective-permute-start.2 = (bf16[11,56,4]{2,1,0:T(8,128)(2,1)S(1)}, bf16[11,56,4]{2,1,0:T(8,128)(2,1)S(1)}, u32[]{:S(2)}, u32[]{:S(2)}) collective-permute-start(bf16[11,56,4]{2,1,0:T(8,128)(2,1)S(1)} %get-tuple-element.43), channel_id=1, source_target_pairs={{0,1},{1,2},{2,3},{3,4},{4,5},{5,6},{6,7},{8,9},{9,10},{10,11},{11... | collective-permute-start | bytes 14792 | tf_op jit(solution)/shard_map/ppermute | solution.py:28
  243.8 4.5 %collective-permute-start.3 = (bf16[11,56,4]{2,1,0:T(8,128)(2,1)S(1)}, bf16[11,56,4]{2,1,0:T(8,128)(2,1)S(1)}, u32[]{:S(2)}, u32[]{:S(2)}) collective-permute-start(bf16[11,56,4]{2,1,0:T(8,128)(2,1)S(1)} %get-tuple-element.44), channel_id=1, source_target_pairs={{1,0},{2,1},{3,2},{4,3},{5,4},{6,5},{7,6},{9,8},{10,9},{11,10},{12... | collective-permute-start | bytes 14792 | tf_op jit(solution)/shard_map/ppermute | solution.py:29
  249.6 15.9 %collective-permute-start.4 = (bf16[8,40,80]{2,1,0:T(8,128)(2,1)S(1)}, bf16[8,40,80]{2,1,0:T(8,128)(2,1)S(1)}, u32[]{:S(2)}, u32[]{:S(2)}) collective-permute-start(bf16[8,40,80]{2,1,0:T(8,128)(2,1)S(1)} %maximum_bitcast_fusion), channel_id=1, source_target_pairs={{0,8},{8,0},{16,24},{24,16},{1,9},{9,1},{17,25},{25,17},{2,10},{10... | collective-permute-start | bytes 153608 | tf_op jit(solution)/shard_map/ppermute | solution.py:68
  265.6 10.3 %collective-permute-start.5 = (bf16[8,2,40,80]{3,2,1,0:T(8,128)(2,1)S(1)}, bf16[8,2,40,80]{3,2,1,0:T(8,128)(2,1)S(1)}, u32[]{:S(2)}, u32[]{:S(2)}) collective-permute-start(bf16[8,2,40,80]{3,2,1,0:T(8,128)(2,1)S(1)} %pad_maximum_fusion.2), channel_id=1, source_target_pairs={{0,16},{8,24},{16,0},{24,8},{1,17},{9,25},{17,1},{25,9},{2,18},{10... | collective-permute-start | bytes 307208 | tf_op jit(solution)/shard_map/ppermute | solution.py:68
  276.0 42.1 %collective-permute-start.6 = (bf16[2,2,4,40,80]{4,3,2,1,0:T(8,128)(2,1)S(1)}, bf16[2,2,4,40,80]{4,3,2,1,0:T(8,128)(2,1)S(1)}, u32[]{:S(2)}, u32[]{:S(2)}) collective-permute-start(bf16[2,2,4,40,80]{4,3,2,1,0:T(8,128)(2,1)S(1)} %dynamic-slice_bitcast_fusion), channel_id=1, source_target_pairs={{0,1},{1,0},{2,3},{3,2},{4,5},{5,4},{6,7},{7,6},{8,9},{9,8},{10,11... | collective-permute-start | bytes 307208 | tf_op jit(solution)/shard_map/ppermute | solution.py:68
  318.2 28.3 %collective-permute-start.7 = (bf16[2,2,4,40,80]{4,3,2,1,0:T(8,128)(2,1)S(1)}, bf16[2,2,4,40,80]{4,3,2,1,0:T(8,128)(2,1)S(1)}, u32[]{:S(2)}, u32[]{:S(2)}) collective-permute-start(bf16[2,2,4,40,80]{4,3,2,1,0:T(8,128)(2,1)S(1)} %bitcast.184), channel_id=1, source_target_pairs={{0,2},{1,3},{2,0},{3,1},{4,6},{5,7},{6,4},{7,5},{8,10},{9,11},{10,... | collective-permute-start | bytes 307208 | tf_op jit(solution)/shard_map/ppermute | solution.py:68
  342.4 15.3 %copy-start.6 = (bf16[512,1280]{1,0:T(8,128)(2,1)S(1)}, bf16[512,1280]{1,0:T(8,128)(2,1)}, u32[]{:S(2)}) copy-start(bf16[512,1280]{1,0:T(8,128)(2,1)} %get-tuple-element.16) | copy-start | bytes 3932164
  346.6 11.5 %copy-start.1 = (bf16[768,1280]{1,0:T(8,128)(2,1)S(1)}, bf16[768,1280]{1,0:T(8,128)(2,1)}, u32[]{:S(2)}) copy-start(bf16[768,1280]{1,0:T(8,128)(2,1)} %get-tuple-element.13.table_ref) | copy-start | bytes 5898244
  346.6 10.9 %collective-permute-start.8 = (bf16[2,2,4,40,80]{4,3,2,1,0:T(8,128)(2,1)S(1)}, bf16[2,2,4,40,80]{4,3,2,1,0:T(8,128)(2,1)S(1)}, u32[]{:S(2)}, u32[]{:S(2)}) collective-permute-start(bf16[2,2,4,40,80]{4,3,2,1,0:T(8,128)(2,1)S(1)} %fusion.24), channel_id=1, source_target_pairs={{0,4},{1,5},{2,6},{3,7},{4,0},{5,1},{6,2},{7,3},{8,12},{9,13},{10,... | collective-permute-start | bytes 307208 | tf_op jit(solution)/shard_map/ppermute | solution.py:68
  357.7 5.1 %copy-start.20 = (pred[8]{0:T(512)(128)(4,1)S(1)}, pred[8]{0:T(512)(128)(4,1)}, u32[]{:S(2)}) copy-start(pred[8]{0:T(512)(128)(4,1)} %compare_and_fusion.1) | copy-start | bytes 28
  357.7 5.4 %copy-start.21 = (s32[8]{0:T(128)S(1)}, s32[8]{0:T(128)}, u32[]{:S(2)}) copy-start(s32[8]{0:T(128)} %fusion.49) | copy-start | bytes 100
  357.7 5.6 %copy-start.16 = (f32[8]{0:T(128)S(1)}, f32[8]{0:T(128)}, u32[]{:S(2)}) copy-start(f32[8]{0:T(128)} %compare_convert_fusion) | copy-start | bytes 100
  359.3 14.0 %copy-start.17 = (pred[48,16]{0,1:T(8,128)(4,1)S(1)}, pred[48,16]{0,1:T(8,128)(4,1)}, u32[]{:S(2)}) copy-start(pred[48,16]{0,1:T(8,128)(4,1)} %reshape.152) | copy-start | bytes 2308
  362.8 11.3 %copy-start.5 = (bf16[32,16,2560]{2,1,0:T(8,128)(2,1)S(1)}, bf16[32,16,2560]{2,1,0:T(8,128)(2,1)}, u32[]{:S(2)}) copy-start(bf16[32,16,2560]{2,1,0:T(8,128)(2,1)} %copy-done.4) | copy-start | bytes 7864324
  362.8 11.3 %copy-start.7 = (bf16[512,1280]{1,0:T(8,128)(2,1)S(1)}, bf16[512,1280]{1,0:T(8,128)(2,1)}, u32[]{:S(2)}) copy-start(bf16[512,1280]{1,0:T(8,128)(2,1)} %get-tuple-element.16) | copy-start | bytes 3932164
  363.3 1.7 collective-permute-start.9
  365.0 3.7 collective-permute-start.10
  368.6 4.6 %collective-permute-start.11 = (f32[2,2,2,128]{3,2,1,0:T(2,128)S(1)}, f32[2,2,2,128]{3,2,1,0:T(2,128)S(1)}, u32[]{:S(2)}, u32[]{:S(2)}) collective-permute-start(f32[2,2,2,128]{3,2,1,0:T(2,128)S(1)} %fusion.39), channel_id=1, source_target_pairs={{0,4},{1,5},{2,6},{3,7},{4,0},{5,1},{6,2},{7,3},{8,12},{9,13},{10,... | collective-permute-start | bytes 12296 | tf_op jit(solution)/shard_map/ppermute | solution.py:68
